TPU v7x, 32 devices: a whole 2x2x4 slice. The times are simulated.
32 devices in a mesh: rep: 2 (over x), shard: 16 (over z, y, core).
Axes of the slice: x: 2, y: 2, z: 4, core: 2. Of those that a mesh axis runs over, the one named last changes fastest.
Arguments:
- tokens: bfloat16 [8192, 2048], P(('rep', 'shard')), may hold values from -6 to 6
- seg_ids: int32 [8192], P(('rep', 'shard')), may hold values from 0 to 7, never falling along the last dimension, each value on 1 to 2000 neighbouring positions
- mix_gain: bfloat16 [2048], P('shard'), may hold values from 0.099609375 to 1.8984375
- mix_in: bfloat16 [2048, 5120], P('shard'), may hold values from -0.125 to 0.125
- conv_par: bfloat16 [5, 2560], P(None, 'shard'), may hold values from -3 to 3
- gate_w: bfloat16 [2560, 320], P('shard'), may hold values from -0.5 to 0.5
- gate_bias: bfloat16 [2, 2560], P(None, 'shard'), may hold values from -3 to 3
- decay: bfloat16 [2560], P('shard'), may hold values from 2.1875 to 6.875
- out_proj: bfloat16 [2560, 2048], P('shard'), may hold values from -0.5 to 0.5
- mlp_gain: bfloat16 [2048], P('shard'), may hold values from 0.099609375 to 1.8984375
- mlp_in: bfloat16 [2048, 12288], P('shard'), may hold values from -0.125 to 0.125
- mlp_out: bfloat16 [6144, 2048], P('shard'), may hold values from -0.15625 to 0.15625
- cotangent: bfloat16 [8192, 2048], P(('rep', 'shard')), may hold values from -6 to 6
Outputs:
- output: bfloat16 [8192, 2048], P(('rep', 'shard'))
- grad_tokens: float32 [8192, 2048], P(('rep', 'shard'))
- grad_mix_gain: float32 [2048], P('shard')
- grad_mix_in: float32 [2048, 5120], P('shard')
- grad_conv_par: float32 [5, 2560], P(None, 'shard')
- grad_gate_w: float32 [2560, 320], P('shard')
- grad_gate_bias: float32 [2, 2560], P(None, 'shard')
- grad_decay: float32 [2560], P('shard')
- grad_out_proj: float32 [2560, 2048], P('shard')
- grad_mlp_gain: float32 [2048], P('shard')
- grad_mlp_in: float32 [2048, 12288], P('shard')
- grad_mlp_out: float32 [6144, 2048], P('shard')
Inputs may be any that keep to these rules, and one draw needn't show every extreme that they name: `seg_ids`: along the token order the ids never fall; each document has 1 to 2000 tokens and one has exactly 2000.
All inputs are finite; a program needn't handle non-finite values.
Results may differ from a plain program's by a relative error of at most 0.013.
Values may be sent and summed in bfloat16 or wider, within the bound.
A program may use at most 512 MiB of HBM per device.

v0:
```python
import jax
import jax.numpy as jnp
from jax import lax
from jax.sharding import PartitionSpec as P

NBLK = 16
SEQ_LEN = 4096


EPSILON = 1e-06
DECAY_RATE = 8.0


def from_behind(block, axis, distance):
    devices = range(lax.axis_size(axis))
    route = [(i - distance, i) for i in devices if i - distance in devices]
    return lax.ppermute(block, axis, route)


def prefix(value, axis, join, neutral, backward):
    count, mine = (lax.axis_size(axis), lax.axis_index(axis))
    pieces = jax.tree.map(lambda part: lax.all_gather(part, axis), value)
    if backward:
        pieces = jax.tree.map(lambda part: part[::-1], pieces)
        mine = count - 1 - mine
    running = jax.tree.map(
        lambda part, zero: jnp.full_like(part, 0) + jnp.asarray(zero, part.dtype), value, neutral
    )

    def turn(position, running):
        longer = join(running, jax.tree.map(lambda part: part[position], pieces))
        return jax.tree.map(lambda new, old: jnp.where(position < mine, new, old), longer, running)

    return lax.fori_loop(0, count - 1, turn, running)


def norm_rows(values, factor):
    return values * lax.rsqrt(jnp.mean(values * values, axis=-1, keepdims=True) + EPSILON) * factor


def combine_pairs(earlier, later):
    return (earlier[0] * later[0], later[0] * earlier[1] + later[1])


def contract_rows(left_in, right_in):
    return lax.dot_general(
        left_in, right_in, (((0,), (0,)), ((), ())), preferred_element_type=jnp.float32
    )


def times_transposed(left_in, matrix):
    return lax.dot_general(
        left_in, matrix, (((1,), (1,)), ((), ())), preferred_element_type=jnp.float32
    )


def gate_terms(pre_sum, decay_in, conv_out, fresh_mask, block_size):
    length = pre_sum.shape[0]
    channels = decay_in.shape[0]
    recur_gate = jax.nn.sigmoid(pre_sum[:, :, :block_size].reshape(length, channels))
    input_gate = jax.nn.sigmoid(pre_sum[:, :, block_size:].reshape(length, channels))
    log_decay = -DECAY_RATE * jax.nn.softplus(-decay_in) * recur_gate
    kept_rows = (1.0 - fresh_mask.astype(jnp.float32))[:, None]
    coefficient = jnp.exp(log_decay) * kept_rows
    scaling = jnp.where(fresh_mask[:, None], 1.0, jnp.sqrt(-jnp.expm1(2.0 * log_decay)))
    return (coefficient, scaling * input_gate * conv_out)


def gated_product(first_in, second_in):
    return jax.nn.gelu(first_in) * second_in


def on_device(
    tokens,
    seg_ids,
    mix_gain,
    mix_in,
    conv_par,
    gate_w,
    gate_bias,
    decay,
    out_proj,
    mlp_gain,
    mlp_in,
    mlp_out,
    cotangent,
):
    gain_one, in_matrix, taps_full, gate_full, bias_full, decay_full, out_matrix = (
        lax.all_gather(mix_gain, "shard", axis=0, tiled=True),
        lax.all_gather(mix_in, "shard", axis=0, tiled=True),
        lax.all_gather(conv_par, "shard", axis=1, tiled=True),
        lax.all_gather(gate_w, "shard", axis=0, tiled=True),
        lax.all_gather(gate_bias, "shard", axis=1, tiled=True),
        lax.all_gather(decay, "shard", axis=0, tiled=True),
        lax.all_gather(out_proj, "shard", axis=0, tiled=True),
    )
    length = tokens.shape[0]
    channels = decay_full.shape[0]
    block_size = channels // NBLK
    inputs = tokens.astype(jnp.float32)
    gain_one_float = gain_one.astype(jnp.float32)
    normed_one = norm_rows(inputs, gain_one_float).astype(jnp.bfloat16)
    projected = jnp.dot(normed_one, in_matrix, preferred_element_type=jnp.float32)
    branch = projected[:, :channels]
    conv_in = projected[:, channels:].astype(jnp.bfloat16)
    prev_ids = from_behind(seg_ids[-3:], "shard", 1)
    prev_rows = from_behind(conv_in[-3:], "shard", 1)
    extended = jnp.concatenate([prev_ids, seg_ids])
    places = lax.broadcasted_iota(jnp.int32, (length,), 0)
    seq_start = lax.axis_index("shard") * length % SEQ_LEN == 0
    fresh_mask = (extended[3:] != extended[2:-1]) | (places == 0) & seq_start
    keep_ext = jnp.concatenate(
        [(extended[1:3] == extended[0:2]).astype(jnp.float32), 1.0 - fresh_mask.astype(jnp.float32)]
    )
    taps_float = taps_full.astype(jnp.float32)
    padded_in = jnp.concatenate([prev_rows, conv_in]).astype(jnp.float32)
    factors = [jnp.ones((length,), jnp.float32)]
    conv_sum = taps_float[4] + taps_float[0] * padded_in[3:]
    for offset in range(1, 4):
        factors.append(factors[-1] * keep_ext[3 - offset : 3 - offset + length])
        conv_sum = (
            conv_sum
            + taps_float[offset]
            * padded_in[3 - offset : 3 - offset + length]
            * factors[offset][:, None]
        )
    conv_out = conv_sum.astype(jnp.bfloat16)
    conv_float = conv_out.astype(jnp.float32)
    gate_blocks = gate_full.reshape(NBLK, block_size, 2 * block_size)
    bias_float = bias_full.astype(jnp.float32)
    bias_blocks = jnp.concatenate(
        [bias_float[0].reshape(NBLK, block_size), bias_float[1].reshape(NBLK, block_size)], axis=-1
    )
    conv_blocks = conv_out.reshape(length, NBLK, block_size)
    pre_sum = (
        jnp.einsum("tbj,bjk->tbk", conv_blocks, gate_blocks, preferred_element_type=jnp.float32)
        + bias_blocks
    )
    decay_float = decay_full.astype(jnp.float32)
    (coefficient, drive), gate_pull = jax.vjp(
        lambda pre_in, decay_in, conv_value: gate_terms(
            pre_in, decay_in, conv_value, fresh_mask, block_size
        ),
        pre_sum,
        decay_float,
        conv_float,
    )
    prefix_coef, local_state = lax.associative_scan(combine_pairs, (coefficient, drive))
    identity_pair = (jnp.ones((channels,), jnp.float32), jnp.zeros((channels,), jnp.float32))
    carried = prefix(
        (prefix_coef[-1], local_state[-1]), "shard", combine_pairs, identity_pair, False
    )
    state_in = carried[1]
    state = local_state + prefix_coef * state_in
    mixed = (state * jax.nn.gelu(branch)).astype(jnp.bfloat16)
    residual = inputs + jnp.dot(mixed, out_matrix, preferred_element_type=jnp.float32)
    gain_two, up_matrix, down_matrix = (
        lax.all_gather(mlp_gain, "shard", axis=0, tiled=True),
        lax.all_gather(mlp_in, "shard", axis=0, tiled=True),
        lax.all_gather(mlp_out, "shard", axis=0, tiled=True),
    )
    gain_two_float = gain_two.astype(jnp.float32)
    normed_two = norm_rows(residual, gain_two_float).astype(jnp.bfloat16)
    hidden = jnp.dot(normed_two, up_matrix, preferred_element_type=jnp.float32)
    ff_width = hidden.shape[1] // 2
    activated = gated_product(hidden[:, :ff_width], hidden[:, ff_width:]).astype(jnp.bfloat16)
    output = (
        residual + jnp.dot(activated, down_matrix, preferred_element_type=jnp.float32)
    ).astype(jnp.bfloat16)
    up_matrix, down_matrix = (
        lax.all_gather(mlp_in, "shard", axis=0, tiled=True),
        lax.all_gather(mlp_out, "shard", axis=0, tiled=True),
    )
    act_grad = times_transposed(cotangent, down_matrix)
    mlp_out_grad = lax.psum_scatter(
        contract_rows(activated, cotangent), "shard", scatter_dimension=0, tiled=True
    )
    _, act_pull = jax.vjp(gated_product, hidden[:, :ff_width], hidden[:, ff_width:])
    gate_part_grad, up_part_grad = act_pull(act_grad)
    hidden_grad = jnp.concatenate([gate_part_grad, up_part_grad], axis=1).astype(jnp.bfloat16)
    normed_two_grad = times_transposed(hidden_grad, up_matrix)
    mlp_in_grad = lax.psum_scatter(
        contract_rows(normed_two, hidden_grad), "shard", scatter_dimension=0, tiled=True
    )
    _, norm_two_pull = jax.vjp(norm_rows, residual, gain_two_float)
    residual_norm_grad, gain_two_grad = norm_two_pull(normed_two_grad)
    residual_grad = cotangent.astype(jnp.float32) + residual_norm_grad
    residual_low = residual_grad.astype(jnp.bfloat16)
    in_matrix, gate_full, out_matrix = (
        lax.all_gather(mix_in, "shard", axis=0, tiled=True),
        lax.all_gather(gate_w, "shard", axis=0, tiled=True),
        lax.all_gather(out_proj, "shard", axis=0, tiled=True),
    )
    gate_blocks = gate_full.reshape(NBLK, block_size, 2 * block_size)
    mixed_grad = times_transposed(residual_low, out_matrix)
    out_proj_grad = contract_rows(mixed, residual_low)
    _, mix_pull = jax.vjp(
        lambda state_value, branch_value: state_value * jax.nn.gelu(branch_value), state, branch
    )
    state_grad, branch_grad = mix_pull(mixed_grad)
    next_coef = jnp.concatenate([coefficient[1:], jnp.ones((1, channels), jnp.float32)])
    suffix_coef, local_grad = lax.associative_scan(
        combine_pairs, (next_coef, state_grad), reverse=True
    )
    from_right = prefix(
        (coefficient[0] * suffix_coef[0], coefficient[0] * local_grad[0]),
        "shard",
        combine_pairs,
        identity_pair,
        True,
    )
    total_state_grad = local_grad + suffix_coef * from_right[1]
    prev_state = jnp.concatenate([state_in[None], state[:-1]])
    pre_grad, decay_grad, conv_rec_grad = gate_pull(
        (total_state_grad * prev_state, total_state_grad)
    )
    pre_low = pre_grad.astype(jnp.bfloat16)
    bias_sums = jnp.sum(pre_low.astype(jnp.float32), axis=0)
    bias_grad = jnp.stack(
        [bias_sums[:, :block_size].reshape(channels), bias_sums[:, block_size:].reshape(channels)]
    )
    gate_grad = jnp.einsum(
        "tbj,tbk->bjk", conv_blocks, pre_low, preferred_element_type=jnp.float32
    ).reshape(channels, 2 * block_size)
    conv_grad = conv_rec_grad + jnp.einsum(
        "tbk,bjk->tbj", pre_low, gate_blocks, preferred_element_type=jnp.float32
    ).reshape(length, channels)
    edge_sum = jnp.zeros((length + 3, channels), jnp.float32)
    tap_list = []
    for offset in range(4):
        masked_grad = conv_grad * factors[offset][:, None]
        edge_sum = edge_sum + jnp.pad(
            taps_float[offset] * masked_grad, ((3 - offset, offset), (0, 0))
        )
        tap_list.append(jnp.sum(masked_grad * padded_in[3 - offset : 3 - offset + length], axis=0))
    tap_list.append(jnp.sum(conv_grad, axis=0))
    tap_grads = jnp.stack(tap_list)
    back_edge = from_behind(edge_sum[:3], "shard", -1)
    conv_in_grad = edge_sum[3:] + jnp.pad(back_edge, ((length - 3, 0), (0, 0)))
    proj_grad = jnp.concatenate([branch_grad, conv_in_grad], axis=1).astype(jnp.bfloat16)
    normed_one_grad = times_transposed(proj_grad, in_matrix)
    mix_in_grad = contract_rows(normed_one, proj_grad)
    _, norm_one_pull = jax.vjp(norm_rows, inputs, gain_one_float)
    input_norm_grad, gain_one_grad = norm_one_pull(normed_one_grad)
    input_grad = residual_grad + input_norm_grad
    owned = (
        lax.psum_scatter(gain_one_grad, "shard", scatter_dimension=0, tiled=True),
        lax.psum_scatter(mix_in_grad, "shard", scatter_dimension=0, tiled=True),
        lax.psum_scatter(tap_grads, "shard", scatter_dimension=1, tiled=True),
        lax.psum_scatter(gate_grad, "shard", scatter_dimension=0, tiled=True),
        lax.psum_scatter(bias_grad, "shard", scatter_dimension=1, tiled=True),
        lax.psum_scatter(decay_grad, "shard", scatter_dimension=0, tiled=True),
        lax.psum_scatter(out_proj_grad, "shard", scatter_dimension=0, tiled=True),
        lax.psum_scatter(gain_two_grad, "shard", scatter_dimension=0, tiled=True),
    )
    summed = lax.psum(
        (
            owned[0],
            owned[1],
            owned[2],
            owned[3],
            owned[4],
            owned[5],
            owned[6],
            owned[7],
            mlp_in_grad,
            mlp_out_grad,
        ),
        "rep",
    )
    return (
        output,
        input_grad,
        summed[0],
        summed[1],
        summed[2],
        summed[3],
        summed[4],
        summed[5],
        summed[6],
        summed[7],
        summed[8],
        summed[9],
    )


def solution(mesh):
    placed = (
        P(("rep", "shard"), None),
        P(("rep", "shard")),
        P("shard"),
        P("shard", None),
        P(None, "shard"),
        P("shard", None),
        P(None, "shard"),
        P("shard"),
        P("shard", None),
        P("shard"),
        P("shard", None),
        P("shard", None),
        P(("rep", "shard"), None),
    )
    return jax.shard_map(
        on_device,
        mesh=mesh,
        in_specs=placed,
        out_specs=(
            P(("rep", "shard"), None),
            P(("rep", "shard"), None),
            P("shard"),
            P("shard", None),
            P(None, "shard"),
            P("shard", None),
            P(None, "shard"),
            P("shard"),
            P("shard", None),
            P("shard"),
            P("shard", None),
            P("shard", None),
        ),
        check_vma=False,
    )
```

profile of v0, /device:TPU:11, one launch (start us, length us, event | category | flops | bytes accessed | tf_op | source)
XLA Modules:
  0.0 3530.9 jit_solution(1848681823508837055)
XLA Ops:
  14.5 17.4 all-gather.1
  32.0 17.5 all-gather.2
  49.8 19.3 all-gather
  69.2 17.4 all-gather.5
  88.2 25.3 all-reduce.73
  121.0 12.6 fusion.98
  143.2 21.2 all-gather.16.cloned.1.call-done
  178.3 7.0 convert_multiply_fusion.5
  309.8 9.1 pad.255
  342.8 19.9 all-gather.3
  362.7 9.2 pad.239
  374.4 9.3 pad.238
  384.7 18.6 all-gather.4
  405.4 10.9 slice.699
  416.3 6.6 slice.708
  422.9 6.5 slice.701
  429.5 8.7 multiply_convert_fusion.2
  444.6 58.0 %all-gather.20.cloned.1.call-done = bf16[2048,12288]{1,0:T(8,128)(2,1)} async-done(((bf16[128,12288]{1,0:T(8,128)(2,1)}), bf16[2048,12288]{1,0:T(8,128)(2,1)}) %all-gather.20.cloned.1.call-update) | async-done | bytes 50331664 | tf_op jit(solution)/shard_map/all_gather | solution.py:159
  502.6 26.0 fusion.82
  528.6 105.8 %all-gather.22.cloned.1.call-done = bf16[6144,2048]{1,0:T(8,128)(2,1)} async-done(((bf16[384,2048]{1,0:T(8,128)(2,1)}), bf16[6144,2048]{1,0:T(8,128)(2,1)}) %all-gather.22.cloned.1.call-update) | async-done | bytes 25165840 | tf_op jit(solution)/shard_map/all_gather | solution.py:160
  634.4 20.7 fusion.6
  655.1 23.9 multiply_reduce_fusion.5
  681.4 11.0 fusion.15
  698.8 10.7 slice.705
  709.5 10.8 slice.703
  816.7 10.8 slice.761
  851.3 9.1 pad.271
  862.8 9.1 pad.286
  872.0 9.1 pad.287
  887.6 20.7 rev.14
  908.4 21.0 rev.15
  929.4 18.2 all-gather.6
  947.9 17.9 all-gather.7
  968.4 10.0 multiply_reduce_fusion
  996.9 12.8 fusion.46
  1019.0 6.4 multiply_reduce_fusion.1
  1034.4 16.7 fusion.39
  1053.0 20.8 fusion.99
  1075.4 47.7 %fusion.7 = f32[2048,12288]{1,0:T(8,128)} fusion(bf16[256,6144]{1,0:T(8,128)(2,1)} %get-tuple-element.302, bf16[256,6144]{1,0:T(8,128)(2,1)} %get-tuple-element.301, f32[256,2048]{1,0:T(8,128)S(1)} %copy-done.22, f32[2048]{0:T(1024)S(1)} %bitcast.93, f32[256]{0:T(256)S(1)} %copy-done.59), kind=kOutput, calls=%fused_computation.27 | convolution fusion | flops 12899057664 | bytes 109061120 | tf_op jit(solution)/shard_map/dot_general | solution.py:46
  1131.1 149.7 %reduce-scatter.18.cloned.1.call-done = f32[160,2048]{1,0:T(8,128)} async-done(((f32[2560,2048]{1,0:T(8,128)}), f32[160,2048]{1,0:T(8,128)}) %reduce-scatter.18.cloned.1.call-update) | async-done | bytes 1310736 | tf_op jit(solution)/shard_map/reduce_scatter | solution.py:253
  1280.8 404.4 %reduce-scatter.14.cloned.1.call-done = f32[128,5120]{1,0:T(8,128)} async-done(((f32[2048,5120]{1,0:T(8,128)}), f32[128,5120]{1,0:T(8,128)}) %reduce-scatter.14.cloned.1.call-update) | async-done | bytes 2621456 | tf_op jit(solution)/shard_map/reduce_scatter | solution.py:248
  1685.2 471.7 %reduce-scatter.20.cloned.1.call-done = f32[384,2048]{1,0:T(8,128)} async-done(((f32[6144,2048]{1,0:T(8,128)}), f32[384,2048]{1,0:T(8,128)}) %reduce-scatter.20.cloned.1.call-update) | async-done | bytes 3145744 | tf_op jit(solution)/shard_map/reduce_scatter | solution.py:175
  2156.9 913.2 %reduce-scatter.26.cloned.1.call-done = f32[128,12288]{1,0:T(8,128)} async-done(((f32[2048,12288]{1,0:T(8,128)}), f32[128,12288]{1,0:T(8,128)}) %reduce-scatter.26.cloned.1.call-update) | async-done | bytes 6291472
  3071.8 13.3 fusion.29
  3085.1 46.6 %reduce-scatter.24.cloned.1.call-done = f32[160,2]{1,0:T(8,128)} async-done(((f32[2560,2]{1,0:T(8,128)}), f32[160,2]{1,0:T(8,128)}) %reduce-scatter.24.cloned.1.call-update) | async-done | bytes 1296
  3132.7 12.0 fusion.33
  3144.7 48.3 %all-reduce.78 = (f32[2048]{0:T(1024)S(1)}, f32[2560]{0:T(1024)S(1)}, f32[2048]{0:T(1024)S(1)}) all-reduce(f32[2048]{0:T(1024)S(1)} %get-tuple-element.244, f32[2560]{0:T(1024)S(1)} %fusion.64, f32[2048]{0:T(1024)S(1)} %copy-done.107), channel_id=2, replica_groups=mesh['rep'=2,'shard'=16] {'shard'}, use_global_device_ids=true, to_apply=%region_9.10.clone | all-reduce | flops 6656 | bytes 53248
  3203.4 307.1 %all-reduce.83.cloned.1.call-done = (f32[128,5120]{1,0:T(8,128)}, f32[160,320]{1,0:T(8,128)}, f32[160,2048]{1,0:T(8,128)}, f32[128,12288]{1,0:T(8,128)}, f32[384,2048]{1,0:T(8,128)}) async-done(((f32[128,5120]{1,0:T(8,128)}, f32[160,320]{1,0:T(8,128)}, f32[160,2048]{1,0:T(8,128)}, f32[128,12288]{1,0:T(8,128)}, f32[384,2048]{1,0:T(8,128)}), (f32[128,5120]{1,0:T(8,128)}, f32[160,320]{1,0:T(8,128)}, ...) | async-done | bytes 13574160 | tf_op jit(solution)/shard_map/psum | solution.py:256
  (654 shorter events, 414.7 us)
Async XLA Ops:
  7.2 113.9 %all-gather.14.cloned.1.call-start = ((), (), s32[]{:S(2)}) async-start(), calls=%async_computation.7 | async-start | bytes 22282240 | tf_op jit(solution)/shard_map/all_gather | solution.py:90
  7.9 156.5 %all-gather.16.cloned.1.call-start = ((), (), s32[]{:S(2)}) async-start(), calls=%async_computation.8 | async-start | bytes 2088960 | tf_op jit(solution)/shard_map/all_gather | solution.py:92
  8.7 429.5 %all-gather.18.cloned.1.call-start = ((), (), s32[]{:S(2)}) async-start(), calls=%async_computation.9 | async-start | bytes 11141120 | tf_op jit(solution)/shard_map/all_gather | solution.py:95
  9.4 59.8 %copy-start.113 = (bf16[128]{0:T(256)(128)(2,1)S(1)}, bf16[128]{0:T(256)(128)(2,1)}, u32[]{:S(2)}) copy-start(bf16[128]{0:T(256)(128)(2,1)} %param.26) | copy-start | bytes 772
  9.4 77.2 %copy-start.110 = (u32[32]{0:T(128)S(1)}, u32[32]{0:T(128)}, u32[]{:S(2)}) copy-start(u32[32]{0:T(128)} %constant.261) | copy-start | bytes 388
  9.5 78.5 %copy-start.114 = (bf16[160]{0:T(256)(128)(2,1)S(1)}, bf16[160]{0:T(256)(128)(2,1)}, u32[]{:S(2)}) copy-start(bf16[160]{0:T(256)(128)(2,1)} %param.24) | copy-start | bytes 964
  9.5 104.3 %copy-start.13 = (bf16[256,2048]{1,0:T(8,128)(2,1)S(1)}, bf16[256,2048]{1,0:T(8,128)(2,1)}, u32[]{:S(2)}) copy-start(bf16[256,2048]{1,0:T(8,128)(2,1)} %param.17) | copy-start | bytes 3145732
  9.5 493.1 %all-gather.20.cloned.1.call-start = ((), (), s32[]{:S(2)}) async-start(), calls=%async_computation.10 | async-start | bytes 53477376 | tf_op jit(solution)/shard_map/all_gather | solution.py:159
  10.1 624.3 %all-gather.22.cloned.1.call-start = ((), (), s32[]{:S(2)}) async-start(), calls=%async_computation.11 | async-start | bytes 26738688 | tf_op jit(solution)/shard_map/all_gather | solution.py:160
  10.6 1120.5 %reduce-scatter.16.cloned.1.call-start = ((), (), s32[]{:S(2)}) async-start(), calls=%async_computation.13 | async-start | bytes 4177920 | tf_op jit(solution)/shard_map/reduce_scatter | solution.py:250
  10.8 104.0 %collective-permute-start = (s32[3]{0:T(128)S(1)}, s32[3]{0:T(128)S(1)}, u32[]{:S(2)}, u32[]{:S(2)}) collective-permute-start(s32[3]{0:T(128)S(1)} %slice.596), channel_id=1, source_target_pairs={{0,1},{1,2},{2,3},{3,4},{4,5},{5,6},{6,7},{7,8},{8,9},{9,10},{10,1... | collective-permute-start | bytes 44 | tf_op jit(solution)/shard_map/ppermute | solution.py:17
  32.0 101.7 %copy-start.67 = (f32[16,1,128]{2,1,0:T(1,128)}, f32[16,1,128]{2,1,0:T(1,128)S(1)}, u32[]{:S(2)}) copy-start(f32[16,1,128]{2,1,0:T(1,128)S(1)} %convert_element_type.95) | copy-start | bytes 24580
  86.7 592.3 %copy-start.43 = (f32[16,1,128]{2,1,0:T(1,128)}, f32[16,1,128]{2,1,0:T(1,128)S(1)}, u32[]{:S(2)}) copy-start(f32[16,1,128]{2,1,0:T(1,128)S(1)} %convert_element_type.97) | copy-start | bytes 24580
  113.8 64.5 %copy-start.50 = (f32[2560]{0:T(1024)}, f32[2560]{0:T(1024)S(1)}, u32[]{:S(2)}) copy-start(f32[2560]{0:T(1024)S(1)} %get-tuple-element.248) | copy-start | bytes 30724
  113.8 64.5 %copy-start.52 = (f32[2560]{0:T(1024)}, f32[2560]{0:T(1024)S(1)}, u32[]{:S(2)}) copy-start(f32[2560]{0:T(1024)S(1)} %get-tuple-element.249) | copy-start | bytes 30724
  113.8 64.5 %copy-start.54 = (f32[2560]{0:T(1024)}, f32[2560]{0:T(1024)S(1)}, u32[]{:S(2)}) copy-start(f32[2560]{0:T(1024)S(1)} %get-tuple-element.250) | copy-start | bytes 30724
  113.8 64.5 %copy-start.56 = (f32[2560]{0:T(1024)}, f32[2560]{0:T(1024)S(1)}, u32[]{:S(2)}) copy-start(f32[2560]{0:T(1024)S(1)} %get-tuple-element.251) | copy-start | bytes 30724
  113.8 64.5 %copy-start.65 = (f32[2560]{0:T(1024)}, f32[2560]{0:T(1024)S(1)}, u32[]{:S(2)}) copy-start(f32[2560]{0:T(1024)S(1)} %get-tuple-element.247) | copy-start | bytes 30724
  114.7 63.6 %copy-start.63 = (f32[2560]{0:T(1024)}, f32[2560]{0:T(1024)S(1)}, u32[]{:S(2)}) copy-start(f32[2560]{0:T(1024)S(1)} %fusion.65) | copy-start | bytes 30724
  115.0 63.3 %copy-start.79 = (f32[256]{0:T(256)}, f32[256]{0:T(256)S(1)}, u32[]{:S(2)}) copy-start(f32[256]{0:T(256)S(1)} %get-tuple-element.295) | copy-start | bytes 3076
  115.0 63.3 %copy-start.103 = (pred[256]{0:T(512)(128)(4,1)}, pred[256]{0:T(512)(128)(4,1)S(1)}, u32[]{:S(2)}) copy-start(pred[256]{0:T(512)(128)(4,1)S(1)} %get-tuple-element.296) | copy-start | bytes 772
  133.7 4.0 collective-permute-start.1
  444.6 234.4 %copy-start.21 = (f32[256,2048]{1,0:T(8,128)}, f32[256,2048]{1,0:T(8,128)S(1)}, u32[]{:S(2)}) copy-start(f32[256,2048]{1,0:T(8,128)S(1)} %get-tuple-element.393) | copy-start | bytes 6291460
  444.6 234.4 %copy-start.58 = (f32[256]{0:T(256)}, f32[256]{0:T(256)S(1)}, u32[]{:S(2)}) copy-start(f32[256]{0:T(256)S(1)} %fusion.77) | copy-start | bytes 3076
  502.6 131.8 %copy-start.33 = (bf16[256,2048]{1,0:T(8,128)(2,1)S(1)}, bf16[256,2048]{1,0:T(8,128)(2,1)}, u32[]{:S(2)}) copy-start(bf16[256,2048]{1,0:T(8,128)(2,1)} %param.29) | copy-start | bytes 3145732
  908.3 58.3 %copy-start.49 = (f32[2560]{0:T(1024)S(1)}, f32[2560]{0:T(1024)}, u32[]{:S(2)}) copy-start(f32[2560]{0:T(1024)} %custom-call.1) | copy-start | bytes 30724
  908.3 60.0 %copy-start.1 = (f32[259,2560]{1,0:T(8,128)S(1)}, f32[259,2560]{1,0:T(8,128)}, u32[]{:S(2)}) copy-start(f32[259,2560]{1,0:T(8,128)} %copy-done) | copy-start | bytes 7956484
  908.3 60.0 %copy-start.51 = (f32[2560]{0:T(1024)S(1)}, f32[2560]{0:T(1024)}, u32[]{:S(2)}) copy-start(f32[2560]{0:T(1024)} %copy-done.50) | copy-start | bytes 30724
  908.3 60.0 %copy-start.53 = (f32[2560]{0:T(1024)S(1)}, f32[2560]{0:T(1024)}, u32[]{:S(2)}) copy-start(f32[2560]{0:T(1024)} %copy-done.52) | copy-start | bytes 30724
  908.3 60.0 %copy-start.55 = (f32[2560]{0:T(1024)S(1)}, f32[2560]{0:T(1024)}, u32[]{:S(2)}) copy-start(f32[2560]{0:T(1024)} %copy-done.54) | copy-start | bytes 30724
  908.3 60.0 %copy-start.57 = (f32[2560]{0:T(1024)S(1)}, f32[2560]{0:T(1024)}, u32[]{:S(2)}) copy-start(f32[2560]{0:T(1024)} %copy-done.56) | copy-start | bytes 30724
  908.3 60.0 %copy-start.64 = (f32[2560]{0:T(1024)S(1)}, f32[2560]{0:T(1024)}, u32[]{:S(2)}) copy-start(f32[2560]{0:T(1024)} %copy-done.63) | copy-start | bytes 30724
  908.3 60.0 %copy-start.66 = (f32[2560]{0:T(1024)S(1)}, f32[2560]{0:T(1024)}, u32[]{:S(2)}) copy-start(f32[2560]{0:T(1024)} %copy-done.65) | copy-start | bytes 30724
  908.3 60.0 %copy-start.80 = (f32[256]{0:T(256)S(1)}, f32[256]{0:T(256)}, u32[]{:S(2)}) copy-start(f32[256]{0:T(256)} %copy-done.79) | copy-start | bytes 3076
  908.3 60.0 %copy-start.84 = (f32[256]{0:T(256)S(1)}, f32[256]{0:T(256)}, u32[]{:S(2)}) copy-start(f32[256]{0:T(256)} %copy-done.83) | copy-start | bytes 3076
  908.4 60.0 %copy-start.86 = (f32[256]{0:T(256)S(1)}, f32[256]{0:T(256)}, u32[]{:S(2)}) copy-start(f32[256]{0:T(256)} %copy-done.85) | copy-start | bytes 3076
  908.4 60.0 %copy-start.104 = (pred[256]{0:T(512)(128)(4,1)S(1)}, pred[256]{0:T(512)(128)(4,1)}, u32[]{:S(2)}) copy-start(pred[256]{0:T(512)(128)(4,1)} %copy-done.103) | copy-start | bytes 772
  996.8 284.0 %reduce-scatter.18.cloned.1.call-start = ((), (), s32[]{:S(2)}) async-start(), calls=%async_computation.14 | async-start | bytes 22282240 | tf_op jit(solution)/shard_map/reduce_scatter | solution.py:253
  1009.7 675.5 %reduce-scatter.14.cloned.1.call-start = ((), (), s32[]{:S(2)}) async-start(), calls=%async_computation.12 | async-start | bytes 44564480 | tf_op jit(solution)/shard_map/reduce_scatter | solution.py:248
  1026.5 6.6 collective-permute-start.2
  1051.1 1105.8 %reduce-scatter.20.cloned.1.call-start = ((), (), s32[]{:S(2)}) async-start(), calls=%async_computation.15 | async-start | bytes 53477376 | tf_op jit(solution)/shard_map/reduce_scatter | solution.py:175
  1073.8 1996.3 %reduce-scatter.26.cloned.1.call-start = ((), (), s32[]{:S(2)}) async-start(), calls=%async_computation.18 | async-start | bytes 106954752
  1123.1 2008.6 %reduce-scatter.24.cloned.1.call-start = ((), (), s32[]{:S(2)}) async-start(), calls=%async_computation.17 | async-start | bytes 1392640
  1129.3 2067.4 %reduce-scatter.22.cloned.1.call-start = ((), (), s32[]{:S(2)}) async-start(), calls=%async_computation.16 | async-start | bytes 1392640
  1131.1 2379.5 %all-reduce.83.cloned.1.call-start = ((), (), s32[]{:S(2)}) async-start(), calls=%async_computation.19 | async-start | bytes 27230208 | tf_op jit(solution)/shard_map/psum | solution.py:256
  3071.8 60.9 %copy-start.16 = (bf16[256,2048]{1,0:T(8,128)(2,1)S(1)}, bf16[256,2048]{1,0:T(8,128)(2,1)}, u32[]{:S(2)}) copy-start(bf16[256,2048]{1,0:T(8,128)(2,1)} %param.17) | copy-start | bytes 3145732
  3132.7 60.5 %copy-start.106 = (f32[256]{0:T(256)S(1)}, f32[256]{0:T(256)}, u32[]{:S(2)}) copy-start(f32[256]{0:T(256)} %copy-done.105) | copy-start | bytes 3076
  3132.7 60.5 %copy-start.8 = (f32[256,2048]{1,0:T(8,128)S(1)}, f32[256,2048]{1,0:T(8,128)}, u32[]{:S(2)}) copy-start(f32[256,2048]{1,0:T(8,128)} %copy-done.7) | copy-start | bytes 6291460
  (83 other events, 693.1 us)
Sparse Core Ops, SparseCore 0:
  9.6 111.3 all-gather.13
  123.3 41.0 all-gather.15
  166.7 86.8 all-gather.17
  255.0 247.5 all-gather.19
  504.0 130.3 all-gather.21
  996.9 69.3 reduce-scatter.15
  1071.0 209.8 reduce-scatter.17
  1285.6 399.5 reduce-scatter.13
  1690.1 466.8 reduce-scatter.19
  2161.6 908.4 reduce-scatter.25
  3074.3 57.2 reduce-scatter.23
  3136.2 57.6 reduce-scatter.21
  3196.7 313.8 all-reduce.82
where the time goes:
time: 3550 us; the launch traced here: 3530 us
  waiting for transfers between devices  2490 us (70%)
  local copies, waits for them, and re-layouts  416 us (12%)
  matrix products  239 us (7%)
  blocking collectives  226 us (6%)
  other arithmetic  130 us (4%)
    unnamed x16, waiting for transfers between devices  963 us
    reduce_scatter x1, waiting for transfers between devices, on_device(): lax.psum_scatter(contract_rows(activated, cotangent), 'shard', scatter_di...  472 us
    reduce_scatter x1, waiting for transfers between devices, on_device(): lax.psum_scatter(mix_in_grad, 'shard', scatter_dimension=0, tiled=True)  404 us
    psum x1, waiting for transfers between devices, on_device(): lax.psum((owned[0], owned[1], owned[2], owned[3], owned[4], owned[5], own...  307 us
    reduce_scatter x1, waiting for transfers between devices, on_device(): lax.psum_scatter(out_proj_grad, 'shard', scatter_dimension=0, tiled=True)  150 us
    slice x57, local copies, waits for them, and re-layouts, on_device(): lax.associative_scan(combine_pairs, (next_coef, state_grad), reverse=True)  135 us
    all_gather x1, waiting for transfers between devices, on_device(): lax.all_gather(mlp_out, 'shard', axis=0, tiled=True)  106 us
    dot_general x4, matrix products, contract_rows(): lax.dot_general(left_in, right_in, (((0,), (0,)), ((), ())), preferred_el...  98.1 us
  transfers between devices with their start and end apart: 16, of which 12 were waited for; matrix products, arithmetic and copies ran while one was open for 12% of the time, Pallas kernels for 0%

commit v1 on v0

v1 whole, which is shorter than its diff:
```python
import functools

import jax
import jax.numpy as jnp
from jax import lax
from jax.experimental import pallas as pl
from jax.experimental.pallas import tpu as pltpu
from jax.sharding import Mesh, PartitionSpec as P

NBLK = 16
SEQ_LEN = 4096

EPSILON = 1e-06
DECAY_RATE = 8.0
PLANE = ("x", "y", "c")
SHARD = ("l", "y", "c")
EVERY = ("x", "l", "y", "c")
BF = jnp.bfloat16
F32 = jnp.float32


def norm_rows(values, factor):
    return values * lax.rsqrt(jnp.mean(values * values, axis=-1, keepdims=True) + EPSILON) * factor


def contract_rows(left_in, right_in):
    return lax.dot_general(
        left_in, right_in, (((0,), (0,)), ((), ())), preferred_element_type=F32
    )


def times_transposed(left_in, matrix):
    return lax.dot_general(
        left_in, matrix, (((1,), (1,)), ((), ())), preferred_element_type=F32
    )


def scan_kernel(rows, backward, a_ref, b_ref, pa_ref, pb_ref, carry):
    @pl.when(pl.program_id(1) == 0)
    def _():
        carry[0] = jnp.ones_like(carry[0])
        carry[1] = jnp.zeros_like(carry[1])

    place = lax.broadcasted_iota(jnp.int32, (8, a_ref.shape[-1]), 0)
    tiles = rows // 8

    def step(i, state):
        before_a, before_b = state
        tile = tiles - 1 - i if backward else i
        at = pl.ds(pl.multiple_of(tile * 8, 8), 8)
        a, b = a_ref[0, at, :], b_ref[0, at, :]
        for gap in (1, 2, 4):
            turn = 8 - gap if backward else gap
            inside = place < 8 - gap if backward else place >= gap
            near_a = jnp.where(inside, pltpu.roll(a, turn, 0), 1.0)
            near_b = jnp.where(inside, pltpu.roll(b, turn, 0), 0.0)
            b = b + a * near_b
            a = a * near_a
        b = b + a * before_b
        a = a * before_a
        pa_ref[0, at, :] = a
        pb_ref[0, at, :] = b
        last = 0 if backward else 7
        return (
            jnp.broadcast_to(a[last : last + 1], a.shape),
            jnp.broadcast_to(b[last : last + 1], b.shape),
        )

    end = lax.fori_loop(0, tiles, step, (carry[0], carry[1]))
    carry[0] = end[0]
    carry[1] = end[1]


def scan_pairs(a, b, backward):
    runs, length, channels = a.shape
    rows = 256
    steps = length // rows
    place = (lambda i, j: (i, steps - 1 - j, 0)) if backward else (lambda i, j: (i, j, 0))
    spec = pl.BlockSpec((1, rows, channels), place)
    return pl.pallas_call(
        functools.partial(scan_kernel, rows, backward),
        out_shape=[jax.ShapeDtypeStruct(a.shape, F32)] * 2,
        grid=(runs, steps),
        in_specs=[spec, spec],
        out_specs=[spec, spec],
        scratch_shapes=[pltpu.VMEM((2, 8, channels), F32)],
        compiler_params=pltpu.CompilerParams(vmem_limit_bytes=16 << 20),
        cost_estimate=pl.CostEstimate(
            flops=20 * a.size, bytes_accessed=16 * a.size, transcendentals=0
        ),
        name="scan_back" if backward else "scan_fwd",
    )(a, b)


def gate_terms(pre_sum, decay_in, conv_out, fresh, keep, width):
    recur_gate = jax.nn.sigmoid(pre_sum[..., :width])
    input_gate = jax.nn.sigmoid(pre_sum[..., width:])
    log_decay = -DECAY_RATE * jax.nn.softplus(-decay_in) * recur_gate
    coefficient = jnp.exp(log_decay) * keep
    scaling = jnp.where(fresh, 1.0, jnp.sqrt(-jnp.expm1(2.0 * log_decay)))
    return (coefficient, scaling * input_gate * conv_out)


def gated_product(first_in, second_in):
    return jax.nn.gelu(first_in) * second_in


def plane_gather(block):
    return lax.all_gather(block, PLANE, axis=0, tiled=True)


def plane_scatter(partial):
    return lax.psum_scatter(partial.astype(BF), PLANE, scatter_dimension=0, tiled=True)


def columns_in(weight, pieces):
    rows = weight.shape[0]
    pieces = pieces.reshape(rows, -1, 4, pieces.shape[-1])
    sent = jnp.moveaxis(pieces, 2, 0)
    got = lax.all_to_all(sent, ("y", "c"), split_axis=0, concat_axis=0, tiled=True)
    return lax.all_gather(got.reshape(4 * rows, -1), "l", axis=0, tiled=True)


def on_device(
    tokens,
    seg_ids,
    mix_gain,
    mix_in,
    conv_par,
    gate_w,
    gate_bias,
    decay,
    out_proj,
    mlp_gain,
    mlp_in,
    mlp_out,
    cotangent,
):
    lines = lax.axis_size("l")
    owners = 4 * lines
    half, line = lax.axis_index("x"), lax.axis_index("l")
    quarter = 2 * lax.axis_index("y") + lax.axis_index("c")
    mine = 4 * half + quarter
    me = 4 * line + quarter
    length, width = tokens.shape
    channels = owners * decay.shape[0]
    block_size = channels // NBLK
    own = channels // 8
    blocks = NBLK // 8
    ff = owners * mlp_out.shape[0]
    run = 4 * length
    plane = 8 * length
    share = mlp_out.shape[0] // 2
    rows = mix_in.shape[0]

    gains = lax.all_gather(jnp.stack([mix_gain, mlp_gain]), SHARD, axis=1, tiled=True)
    packed = jnp.concatenate([conv_par.T, gate_bias.T, decay[:, None], gate_w], axis=1)
    packed = lax.all_gather(packed, SHARD, axis=0, tiled=True)
    packed = lax.dynamic_slice_in_dim(packed, mine * own, own, 0)
    ids_all = lax.all_gather(seg_ids, EVERY, axis=0, tiled=True).reshape(2, lines, run)

    gain_one = gains[0].astype(F32)
    gain_two = gains[1].astype(F32)
    taps = packed[:, :5].T.astype(F32)
    bias = packed[:, 5:7].T.astype(F32)
    decay_own = packed[:, 7].astype(F32)
    gates = packed[:, 8:].reshape(blocks, block_size, 2 * block_size)

    inputs = tokens.astype(F32)
    normed_one = norm_rows(inputs, gain_one).astype(BF)
    all_one = plane_gather(normed_one)

    by_half = mix_in.reshape(rows, 2, 2, 4, own)
    by_half = lax.dynamic_index_in_dim(by_half, half, 2, keepdims=False)
    in_matrix = columns_in(mix_in, by_half)
    out_matrix = lax.dynamic_slice_in_dim(
        lax.all_gather(out_proj, SHARD, axis=0, tiled=True), mine * own, own, 0
    )
    by_half = mlp_in.reshape(rows, 2 * lines, 4, 2, share)
    by_half = lax.dynamic_index_in_dim(by_half, half, 3, keepdims=False)
    up_matrix = columns_in(mlp_in, by_half)
    down_matrix = lax.all_gather(
        lax.dynamic_slice_in_dim(mlp_out, half * share, share, 0), "l", axis=0, tiled=True
    )
    all_cot = plane_gather(cotangent)

    projected = jnp.dot(all_one, in_matrix, preferred_element_type=F32)
    branch = projected[:, :own].reshape(2, run, own)
    conv_in = projected[:, own:].astype(BF).reshape(2, run, own)

    ids = lax.dynamic_index_in_dim(ids_all, line, 1, keepdims=False)
    ids_before = lax.dynamic_index_in_dim(
        ids_all, jnp.maximum(line - 1, 0), 1, keepdims=False
    )[:, -3:]
    ids_before = jnp.where(line > 0, ids_before, -1)
    route = [(i, i + 1) for i in range(lines - 1)]
    rows_before = lax.ppermute(conv_in[:, -3:], "l", route)
    extended = jnp.concatenate([ids_before, ids], axis=1)
    places = (half * 0 + line * run + lax.broadcasted_iota(jnp.int32, (2, run), 1)) % SEQ_LEN
    fresh = (extended[:, 3:] != extended[:, 2:-1]) | (places == 0)
    keep = 1.0 - fresh.astype(F32)
    before_start = jnp.concatenate(
        [(extended[:, 1:3] == extended[:, 0:2]).astype(F32), keep], axis=1
    )
    padded_in = jnp.concatenate([rows_before, conv_in], axis=1).astype(F32)
    factors = [None]
    factor = jnp.ones((2, run), F32)
    conv_sum = taps[4] + taps[0] * padded_in[:, 3:]
    for offset in range(1, 4):
        factor = factor * before_start[:, 3 - offset : 3 - offset + run]
        factors.append(factor[:, :, None])
        conv_sum = (
            conv_sum
            + taps[offset] * padded_in[:, 3 - offset : 3 - offset + run] * factors[offset]
        )
    conv_out = conv_sum.astype(BF)
    conv_blocks = conv_out.reshape(plane, blocks, block_size)
    pre_sum = jnp.einsum("tbj,bjk->btk", conv_blocks, gates, preferred_element_type=F32)
    recur_pre = jnp.moveaxis(pre_sum[:, :, :block_size], 0, 1).reshape(2, run, own) + bias[0]
    input_pre = jnp.moveaxis(pre_sum[:, :, block_size:], 0, 1).reshape(2, run, own) + bias[1]
    pre_sum = jnp.concatenate([recur_pre, input_pre], axis=-1)
    (coefficient, drive), gate_pull = jax.vjp(
        lambda pre_in, decay_in, conv_value: gate_terms(
            pre_in, decay_in, conv_value, fresh[:, :, None], keep[:, :, None], own
        ),
        pre_sum,
        decay_own,
        conv_out.astype(F32),
    )
    prefix_coef, local_state = scan_pairs(coefficient, drive, False)
    ends = lax.all_gather(
        jnp.stack([prefix_coef[:, -1], local_state[:, -1]]), "l", axis=0, tiled=False
    )
    state_in = jnp.zeros((2, own), F32)
    for other in range(lines - 1):
        longer = ends[other, 0] * state_in + ends[other, 1]
        state_in = jnp.where(other < line, longer, state_in)
    state = local_state + prefix_coef * state_in[:, None]
    mixed = (state * jax.nn.gelu(branch)).astype(BF).reshape(plane, own)
    residual = inputs + plane_scatter(
        jnp.dot(mixed, out_matrix, preferred_element_type=F32)
    ).astype(F32)

    normed_two = norm_rows(residual, gain_two).astype(BF)
    all_two = plane_gather(normed_two)
    hidden = jnp.dot(all_two, up_matrix, preferred_element_type=F32)
    part = ff // 8
    activated = gated_product(hidden[:, :part], hidden[:, part:]).astype(BF)
    output = (
        residual
        + plane_scatter(jnp.dot(activated, down_matrix, preferred_element_type=F32)).astype(F32)
    ).astype(BF)

    act_grad = times_transposed(all_cot, down_matrix)
    _, act_pull = jax.vjp(gated_product, hidden[:, :part], hidden[:, part:])
    hidden_grad = jnp.concatenate(act_pull(act_grad), axis=1).astype(BF)
    normed_two_grad = plane_scatter(times_transposed(hidden_grad, up_matrix)).astype(F32)
    down_grad = contract_rows(activated, all_cot).astype(BF)
    down_grad = lax.psum_scatter(down_grad, "l", scatter_dimension=0, tiled=True)
    down_grad = lax.all_gather(down_grad, "x", axis=0, tiled=True).astype(F32)
    up_grad = contract_rows(all_two, hidden_grad).astype(BF)

    def columns_out(grad):
        grad = lax.psum_scatter(grad, "l", scatter_dimension=0, tiled=True)
        grad = lax.all_to_all(
            grad.reshape(4, rows, -1), ("y", "c"), split_axis=0, concat_axis=0, tiled=True
        )
        return lax.all_gather(grad, "x", axis=0, tiled=False)

    up_grad = columns_out(up_grad).reshape(2, 4, rows, 2 * lines, share)
    up_grad = up_grad.transpose(2, 3, 1, 0, 4).reshape(rows, 2 * ff).astype(F32)

    _, norm_two_pull = jax.vjp(norm_rows, residual, gain_two)
    residual_norm_grad, gain_two_grad = norm_two_pull(normed_two_grad)
    residual_grad = cotangent.astype(F32) + residual_norm_grad
    all_res = plane_gather(residual_grad.astype(BF))
    mixed_grad = times_transposed(all_res, out_matrix).reshape(2, run, own)
    out_grad = contract_rows(mixed, all_res)
    _, mix_pull = jax.vjp(
        lambda state_value, branch_value: state_value * jax.nn.gelu(branch_value), state, branch
    )
    state_grad, branch_grad = mix_pull(mixed_grad)
    next_coef = jnp.concatenate([coefficient[:, 1:], jnp.ones((2, 1, own), F32)], axis=1)
    suffix_coef, local_grad = scan_pairs(next_coef, state_grad, True)
    first = coefficient[:, 0]
    ends = lax.all_gather(
        jnp.stack([first * suffix_coef[:, 0], first * local_grad[:, 0]]), "l", axis=0, tiled=False
    )
    from_right = jnp.zeros((2, own), F32)
    for other in reversed(range(1, lines)):
        longer = ends[other, 0] * from_right + ends[other, 1]
        from_right = jnp.where(other > line, longer, from_right)
    total = local_grad + suffix_coef * from_right[:, None]
    prev_state = jnp.concatenate([state_in[:, None], state[:, :-1]], axis=1)
    pre_grad, decay_grad, conv_rec_grad = gate_pull((total * prev_state, total))
    pre_low = pre_grad.astype(BF)
    bias_grad = jnp.sum(pre_low.astype(F32), axis=(0, 1)).reshape(2, own)
    pre_low = pre_low.reshape(plane, 2, blocks, block_size)
    pre_low = pre_low.transpose(2, 0, 1, 3).reshape(blocks, plane, 2 * block_size)
    gate_grad = jnp.einsum(
        "tbj,btk->bjk", conv_blocks, pre_low, preferred_element_type=F32
    ).reshape(own, 2 * block_size)
    conv_grad = conv_rec_grad + jnp.einsum(
        "btk,bjk->tbj", pre_low, gates, preferred_element_type=F32
    ).reshape(2, run, own)
    edge_sum = jnp.zeros((2, run + 3, own), F32)
    tap_list = []
    for offset in range(4):
        masked = conv_grad if offset == 0 else conv_grad * factors[offset]
        edge_sum = edge_sum + jnp.pad(
            taps[offset] * masked, ((0, 0), (3 - offset, offset), (0, 0))
        )
        tap_list.append(
            jnp.sum(masked * padded_in[:, 3 - offset : 3 - offset + run], axis=(0, 1))
        )
    tap_list.append(jnp.sum(conv_grad, axis=(0, 1)))
    tap_grads = jnp.stack(tap_list)
    back_edge = lax.ppermute(edge_sum[:, :3], "l", [(i + 1, i) for i in range(lines - 1)])
    conv_in_grad = edge_sum[:, 3:] + jnp.pad(back_edge, ((0, 0), (run - 3, 0), (0, 0)))
    proj_grad = jnp.concatenate([branch_grad, conv_in_grad], axis=-1).astype(BF)
    proj_grad = proj_grad.reshape(plane, 2 * own)
    normed_one_grad = plane_scatter(times_transposed(proj_grad, in_matrix)).astype(F32)
    in_grad = columns_out(contract_rows(all_one, proj_grad).astype(BF))
    in_grad = in_grad.reshape(2, 4, rows, 2, own).transpose(2, 3, 0, 1, 4)
    in_grad = in_grad.reshape(rows, 2 * channels).astype(F32)
    _, norm_one_pull = jax.vjp(norm_rows, inputs, gain_one)
    input_norm_grad, gain_one_grad = norm_one_pull(normed_one_grad)
    input_grad = residual_grad + input_norm_grad

    def to_owners(values):
        padded = jnp.zeros((channels,) + values.shape[1:], values.dtype)
        padded = lax.dynamic_update_slice_in_dim(padded, values, mine * own, 0)
        return lax.psum(lax.psum_scatter(padded, SHARD, scatter_dimension=0, tiled=True), "x")

    out_grad = to_owners(out_grad.astype(BF)).astype(F32)
    small = jnp.concatenate(
        [tap_grads.T, bias_grad.T, decay_grad[:, None], gate_grad], axis=1
    )
    small = to_owners(small)
    gain_grads = lax.psum(
        lax.psum_scatter(
            jnp.stack([gain_one_grad, gain_two_grad], axis=1), SHARD, scatter_dimension=0, tiled=True
        ),
        "x",
    )
    return (
        output,
        input_grad,
        gain_grads[:, 0],
        in_grad,
        small[:, :5].T,
        small[:, 8:],
        small[:, 5:7].T,
        small[:, 7],
        out_grad,
        gain_grads[:, 1],
        up_grad,
        down_grad,
    )


def solution(mesh):
    count = mesh.shape["shard"]
    fine = Mesh(mesh.devices.reshape(2, count // 4, 2, 2), EVERY)
    rows, cols = P(EVERY, None), P(SHARD, None)
    placed = (
        rows,
        P(EVERY),
        P(SHARD),
        cols,
        P(None, SHARD),
        cols,
        P(None, SHARD),
        P(SHARD),
        cols,
        P(SHARD),
        cols,
        cols,
        rows,
    )
    return jax.shard_map(
        on_device,
        mesh=fine,
        in_specs=placed,
        out_specs=(
            rows,
            rows,
            P(SHARD),
            cols,
            P(None, SHARD),
            cols,
            P(None, SHARD),
            P(SHARD),
            cols,
            P(SHARD),
            cols,
            cols,
        ),
        check_vma=False,
    )
```

time: 3550 us -> 1640 us (0.46)
  waiting for transfers between devices: 2490 us -> 1040 us
  local copies, waits for them, and re-layouts: 416 us -> 147 us
  matrix products: 239 us -> 157 us
  blocking collectives: 226 us -> 144 us
    unnamed x16 -> x26, waiting for transfers between devices: 963 us -> 125 us
    reduce_scatter x4 -> x8, waiting for transfers between devices: 1030 us -> 457 us  [the longest x4 253 us: plane_scatter(): lax.psum_scatter(partial.astype(BF), PLANE, scatter_dimension=0, tiled=True)]
    psum x1 -> x2, waiting for transfers between devices: 307 us -> 42.3 us  [to_owners(): lax.psum(lax.psum_scatter(padded, SHARD, scatter_dimension=0, tiled=True)...]
    all_gather x5 -> x12, waiting for transfers between devices: 191 us -> 416 us  [the longest x4 193 us: plane_gather(): return lax.all_gather(block, PLANE, axis=0, tiled=True)]
    slice x116 -> x13, local copies, waits for them, and re-layouts: 227 us -> 17.2 us  [the longest x2 7.17 us: on_device(): branch = projected[:, :own].reshape(2, run, own)]
    pad x56 -> x0, local copies, waits for them, and re-layouts: 92.4 us -> none  [the longest x28 47.4 us: on_device(): lax.associative_scan(combine_pairs, (next_coef, state_grad), reverse=True)]
    unnamed x2 -> x0, blocking collectives: 73.6 us -> none
    all_gather x8 -> x4, blocking collectives: 146 us -> 74.2 us  [the longest x1 35.9 us: on_device(): lax.all_gather(seg_ids, EVERY, axis=0, tiled=True).reshape(2, lines, run)]
  transfers between devices with their start and end apart: 16 -> 27, of which waited for: 12 -> 21; matrix products, arithmetic and copies ran while one was open for 12% -> 20% of each run, Pallas kernels for 0% -> 1%
where the time goes in v1:
time: 1640 us; the launch traced here: 1630 us
  waiting for transfers between devices  1040 us (63%)
  matrix products  157 us (10%)
  local copies, waits for them, and re-layouts  147 us (9%)
  blocking collectives  144 us (9%)
  other arithmetic  102 us (6%)
    reduce_scatter x4, waiting for transfers between devices, plane_scatter(): lax.psum_scatter(partial.astype(BF), PLANE, scatter_dimension=0, tiled=True)  253 us
    all_gather x4, waiting for transfers between devices, plane_gather(): return lax.all_gather(block, PLANE, axis=0, tiled=True)  193 us
    all_gather x2, waiting for transfers between devices, columns_in(): return lax.all_gather(got.reshape(4 * rows, -1), 'l', axis=0, tiled=True)  127 us
    unnamed x26, waiting for transfers between devices  125 us
    reduce_scatter x1, waiting for transfers between devices, to_owners(): lax.psum_scatter(padded, SHARD, scatter_dimension=0, tiled=True)  119 us
    reduce_scatter x2, waiting for transfers between devices, columns_out(): grad = lax.psum_scatter(grad, 'l', scatter_dimension=0, tiled=True)  84.3 us
    dot_general x4, matrix products, times_transposed(): lax.dot_general(left_in, matrix, (((1,), (1,)), ((), ())), preferred_elem...  54.6 us
    all_gather x2, waiting for transfers between devices, columns_out(): return lax.all_gather(grad, 'x', axis=0, tiled=False)  52.5 us
  transfers between devices with their start and end apart: 27, of which 21 were waited for; matrix products, arithmetic and copies ran while one was open for 20% of the time, Pallas kernels for 1%

profile of v1, /device:TPU:11, one launch (start us, length us, event | category | flops | bytes accessed | tf_op | source)
XLA Modules:
  0.0 1630.3 jit_solution(4728168073771029504)
XLA Ops:
  13.4 14.3 all_to_all.20
  29.4 18.0 %all_gather.61 = bf16[2,2048]{1,0:T(2,128)(2,1)S(1)} all-gather(bf16[2,128]{1,0:T(2,128)(2,1)S(1)} %pad_maximum_fusion.12), channel_id=1, replica_groups=mesh['x'=2,'l'=4,'y'=2,'c'=2] {'l','y','c'}, dimensions={1}, use_global_device_ids=true | all-gather | bytes 8704 | tf_op jit(solution)/shard_map/all_gather | solution.py:156
  50.2 35.9 %all-gather.4 = s32[32,1,256]{2,1,0:T(1,128)S(1)} all-gather(s32[1,1,256]{2,1,0:T(1,128)S(1)} %bitcast.260), channel_id=1, replica_groups=mesh['x'=2,'l'=4,'y'=2,'c'=2] {'x','l','y','c'}, dimensions={0}, use_global_device_ids=true | all-gather | bytes 33792 | tf_op jit(solution)/shard_map/all_gather | solution.py:160
  90.1 18.7 %all-gather.22.cloned.1.call-done = bf16[2048,640]{0,1:T(8,128)(2,1)} async-done(((bf16[512,640]{0,1:T(8,128)(2,1)}), bf16[2048,640]{0,1:T(8,128)(2,1)}) %all-gather.22.cloned.1.call-update) | async-done | bytes 2621456 | tf_op jit(solution)/shard_map/all_gather | solution.py:121
  108.8 58.1 %all-gather.20.cloned.1.call-done = bf16[2048,2048]{1,0:T(8,128)(2,1)} async-done(((bf16[256,2048]{1,0:T(8,128)(2,1)}), bf16[2048,2048]{1,0:T(8,128)(2,1)}) %all-gather.20.cloned.1.call-update) | async-done | bytes 8388624 | tf_op jit(solution)/shard_map/all_gather | solution.py:109
  166.8 8.8 fusion.71
  197.9 7.9 add_convert_fusion.1
  241.4 11.9 convert_multiply_fusion.5
  258.6 8.6 all-gather
  271.4 9.6 convolution_convert_fusion.3
  287.4 27.1 %all_to_all.21 = bf16[4,128,8,192]{1,3,2,0:T(8,128)(2,1)S(1)} all-to-all(bf16[4,128,8,192]{1,3,2,0:T(8,128)(2,1)S(1)} %copy.165), channel_id=1, replica_groups=mesh['x'=2,'l'=4,'y'=2,'c'=2] {'y','c'}, dimensions={0} | all-to-all | bytes 3145728 | tf_op jit(solution)/shard_map/all_to_all | solution.py:120
  317.3 39.6 %reduce-scatter.15.cloned.1.call-done = bf16[256,2048]{1,0:T(8,128)(2,1)} async-done(((bf16[2048,2048]{1,0:T(8,128)(2,1)}), bf16[256,2048]{1,0:T(8,128)(2,1)}) %reduce-scatter.15.cloned.1.call-update) | async-done | bytes 1048592 | tf_op jit(solution)/shard_map/reduce_scatter | solution.py:113
  363.2 108.5 %all-gather.28.cloned.1.call-done = bf16[2048,1536]{0,1:T(8,128)(2,1)} async-done(((bf16[512,1536]{0,1:T(8,128)(2,1)}), bf16[2048,1536]{0,1:T(8,128)(2,1)}) %all-gather.28.cloned.1.call-update) | async-done | bytes 6291472 | tf_op jit(solution)/shard_map/all_gather | solution.py:121
  471.7 58.4 %all-gather.26.cloned.1.call-done = bf16[2048,2048]{1,0:T(8,128)(2,1)} async-done(((bf16[256,2048]{1,0:T(8,128)(2,1)}), bf16[2048,2048]{1,0:T(8,128)(2,1)}) %all-gather.26.cloned.1.call-update) | async-done | bytes 8388624 | tf_op jit(solution)/shard_map/all_gather | solution.py:109
  530.1 19.0 %fusion.73 = f32[2048,1536]{0,1:T(8,128)} fusion(bf16[2048,2048]{1,0:T(8,128)(2,1)} %all-gather.26.cloned.1.call-done, bf16[2048,1536]{0,1:T(8,128)(2,1)} %all-gather.28.cloned.1.call-done), kind=kOutput, calls=%fused_computation.215 | convolution fusion | flops 12884901888 | bytes 27262976 | tf_op jit(solution)/shard_map/dot_general | solution.py:246
  549.1 43.9 %all-gather.30.cloned.1.call-done = bf16[768,2048]{1,0:T(8,128)(2,1)} async-done(((bf16[192,2048]{1,0:T(8,128)(2,1)}), bf16[768,2048]{1,0:T(8,128)(2,1)}) %all-gather.30.cloned.1.call-update) | async-done | bytes 3145744 | tf_op jit(solution)/shard_map/all_gather | solution.py:182
  593.1 57.9 %all-gather.32.cloned.1.call-done = bf16[2048,2048]{1,0:T(8,128)(2,1)} async-done(((bf16[256,2048]{1,0:T(8,128)(2,1)}), bf16[2048,2048]{1,0:T(8,128)(2,1)}) %all-gather.32.cloned.1.call-update) | async-done | bytes 8388624 | tf_op jit(solution)/shard_map/all_gather | solution.py:109
  651.0 18.8 %fusion.6 = (bf16[2048,768]{0,1:T(8,128)(2,1)S(1)}, bf16[2048,768]{0,1:T(8,128)(2,1)}, bf16[2048,768]{0,1:T(8,128)(2,1)}) fusion(f32[2048,1536]{0,1:T(8,128)} %fusion.73, bf16[768,2048]{1,0:T(8,128)(2,1)} %all-gather.30.cloned.1.call-done, bf16[2048,2048]{1,0:T(8,128)(2,1)} %all-gather.32.cloned.1.call-done), kind=kOutput, calls=%fused_computation.13 | convolution fusion | flops 6483345408 | bytes 33554432 | tf_op jit(solution)/shard_map/dot_general | solution.py:33
  671.5 17.5 %convolution_convert_fusion.1 = bf16[2048,2048]{1,0:T(8,128)(2,1)} fusion(bf16[2048,1536]{0,1:T(8,128)(2,1)S(1)} %copy-done.70, bf16[2048,768]{0,1:T(8,128)(2,1)} %get-tuple-element.111, bf16[2048,768]{0,1:T(8,128)(2,1)S(1)} %get-tuple-element.110), kind=kOutput, calls=%fused_computation.3 | convolution fusion | flops 12901679104 | bytes 20971520 | tf_op jit(solution)/shard_map/dot_general | solution.py:33
  689.4 70.5 %reduce-scatter.19.cloned.1.call-done = bf16[256,2048]{1,0:T(8,128)(2,1)} async-done(((bf16[2048,2048]{1,0:T(8,128)(2,1)}), bf16[256,2048]{1,0:T(8,128)(2,1)}) %reduce-scatter.19.cloned.1.call-update) | async-done | bytes 1048592 | tf_op jit(solution)/shard_map/reduce_scatter | solution.py:113
  766.0 11.9 convolution_convert_fusion.5
  779.8 18.3 %convolution_convert_fusion.4 = bf16[2048,1536]{1,0:T(8,128)(2,1)} fusion(bf16[2048,2048]{1,0:T(8,128)(2,1)} %all-gather.26.cloned.1.call-done, bf16[2048,768]{0,1:T(8,128)(2,1)} %get-tuple-element.111, bf16[2048,768]{0,1:T(8,128)(2,1)S(1)} %copy-done.75), kind=kOutput, calls=%fused_computation.6 | convolution fusion | flops 12900630528 | bytes 20971520 | tf_op jit(solution)/shard_map/dot_general | solution.py:27
  802.7 18.3 %all-gather.34.cloned.1.call-done = bf16[2048,2048]{1,0:T(8,128)(2,1)} async-done(((bf16[256,2048]{1,0:T(8,128)(2,1)}), bf16[2048,2048]{1,0:T(8,128)(2,1)}) %all-gather.34.cloned.1.call-update) | async-done | bytes 8388624 | tf_op jit(solution)/shard_map/all_gather | solution.py:109
  821.1 7.4 fusion.37
  837.5 11.6 all-gather.1
  849.3 12.7 multiply_reduce_fusion
  862.0 10.4 fusion.15
  874.8 6.2 copy.172
  892.5 6.6 copy.174
  899.1 11.9 multiply_reduce_fusion.1
  918.8 10.9 convolution_convert_fusion.6
  943.0 54.4 %reduce-scatter.27.cloned.1.call-done = bf16[512,1536]{1,0:T(8,128)(2,1)} async-done(((bf16[2048,1536]{1,0:T(8,128)(2,1)}), bf16[512,1536]{1,0:T(8,128)(2,1)}) %reduce-scatter.27.cloned.1.call-update) | async-done | bytes 1572880 | tf_op jit(solution)/shard_map/reduce_scatter | solution.py:264
  997.4 24.5 %all_to_all.22 = bf16[4,128,1536]{2,1,0:T(8,128)(2,1)} all-to-all(bf16[4,128,1536]{2,1,0:T(8,128)(2,1)} %bitcast.235), channel_id=1, replica_groups=mesh['x'=2,'l'=4,'y'=2,'c'=2] {'y','c'}, dimensions={0} | all-to-all | bytes 3145728 | tf_op jit(solution)/shard_map/all_to_all | solution.py:265
  1021.9 29.9 %reduce-scatter.23.cloned.1.call-done = bf16[512,640]{1,0:T(8,128)(2,1)} async-done(((bf16[2048,640]{1,0:T(8,128)(2,1)}), bf16[512,640]{1,0:T(8,128)(2,1)}) %reduce-scatter.23.cloned.1.call-update) | async-done | bytes 655376 | tf_op jit(solution)/shard_map/reduce_scatter | solution.py:264
  1056.0 68.5 %reduce-scatter.33.cloned.1.call-done = f32[160,328]{1,0:T(8,128)} async-done(((f32[2560,328]{1,0:T(8,128)}), f32[160,328]{1,0:T(8,128)}) %reduce-scatter.33.cloned.1.call-update) | async-done | bytes 209936
  1127.4 10.9 convolution_convert_fusion
  1143.8 7.5 fusion.22
  1153.2 10.9 convolution_convert_fusion.2
  1167.8 31.8 %all-gather.40.cloned.1.call-done = bf16[8,128,1536]{2,1,0:T(8,128)(2,1)} async-done(((bf16[4,128,1536]{2,1,0:T(8,128)(2,1)}), bf16[8,128,1536]{2,1,0:T(8,128)(2,1)}) %all-gather.40.cloned.1.call-update) | async-done | bytes 3145744 | tf_op jit(solution)/shard_map/all_gather | solution.py:268
  1206.9 6.6 copy.182
  1213.4 13.7 all-reduce.11.cloned.1.call-done
  1232.8 20.7 %all-gather.38.cloned.1.call-done = bf16[8,128,640]{2,1,0:T(8,128)(2,1)} async-done(((bf16[4,128,640]{2,1,0:T(8,128)(2,1)}), bf16[8,128,640]{2,1,0:T(8,128)(2,1)}) %all-gather.38.cloned.1.call-update) | async-done | bytes 1310736 | tf_op jit(solution)/shard_map/all_gather | solution.py:268
  1260.6 68.7 %reduce-scatter.21.cloned.1.call-done = bf16[256,2048]{1,0:T(8,128)(2,1)} async-done(((bf16[2048,2048]{1,0:T(8,128)(2,1)}), bf16[256,2048]{1,0:T(8,128)(2,1)}) %reduce-scatter.21.cloned.1.call-update) | async-done | bytes 1048592 | tf_op jit(solution)/shard_map/reduce_scatter | solution.py:113
  1333.1 119.4 %reduce-scatter.25.cloned.1.call-done = bf16[160,2048]{1,0:T(8,128)(2,1)} async-done(((bf16[2560,2048]{1,0:T(8,128)(2,1)}), bf16[160,2048]{1,0:T(8,128)(2,1)}) %reduce-scatter.25.cloned.1.call-update) | async-done | bytes 655376 | tf_op jit(solution)/shard_map/reduce_scatter | solution.py:333
  1452.5 74.5 %reduce-scatter.17.cloned.1.call-done = bf16[256,2048]{1,0:T(8,128)(2,1)} async-done(((bf16[2048,2048]{1,0:T(8,128)(2,1)}), bf16[256,2048]{1,0:T(8,128)(2,1)}) %reduce-scatter.17.cloned.1.call-update) | async-done | bytes 1048592 | tf_op jit(solution)/shard_map/reduce_scatter | solution.py:113
  1527.0 5.9 fusion.32
  1532.9 54.3 %reduce-scatter.31.cloned.1.call-done = f32[128,2]{1,0:T(8,128)} async-done(((f32[2048,2]{1,0:T(8,128)}), f32[128,2]{1,0:T(8,128)}) %reduce-scatter.31.cloned.1.call-update) | async-done | bytes 1040
  1592.4 28.6 %all-reduce.13.cloned.1.call-done = bf16[160,2048]{1,0:T(8,128)(2,1)} async-done(((bf16[160,2048]{1,0:T(8,128)(2,1)}), bf16[160,2048]{1,0:T(8,128)(2,1)}) %all-reduce.13.cloned.1.call-update) | async-done | bytes 655376 | tf_op jit(solution)/shard_map/psum | solution.py:333
  (337 shorter events, 204.2 us)
Async XLA Ops:
  7.2 354.0 %copy-start = (bf16[384,2048]{1,0:T(8,128)(2,1)S(1)}, bf16[384,2048]{1,0:T(8,128)(2,1)}, u32[]{:S(2)}) copy-start(bf16[384,2048]{1,0:T(8,128)(2,1)} %param.24) | copy-start | bytes 4718596
  7.2 79.5 %all-gather.18.cloned.1.call-start = ((), (), s32[]{:S(2)}) async-start(), calls=%async_computation.14 | async-start | bytes 2088960 | tf_op jit(solution)/shard_map/all_gather | solution.py:158
  11.5 97.3 %all-gather.22.cloned.1.call-start = ((), (), s32[]{:S(2)}) async-start(), calls=%async_computation.16 | async-start | bytes 3276800 | tf_op jit(solution)/shard_map/all_gather | solution.py:121
  29.3 137.6 %all-gather.20.cloned.1.call-start = ((), (), s32[]{:S(2)}) async-start(), calls=%async_computation.15 | async-start | bytes 9437184 | tf_op jit(solution)/shard_map/all_gather | solution.py:109
  48.2 714.5 %copy-start.32 = (f32[1,2048]{1,0:T(1,128)}, f32[1,2048]{1,0:T(1,128)S(1)}, u32[]{:S(2)}) copy-start(f32[1,2048]{1,0:T(1,128)S(1)} %get-tuple-element.133) | copy-start | bytes 24580
  49.5 221.8 %all-gather.24.cloned.1.call-start = ((), (), s32[]{:S(2)}) async-start(), calls=%async_computation.17 | async-start | bytes 11141120 | tf_op jit(solution)/shard_map/all_gather | solution.py:177
  50.1 306.8 %reduce-scatter.15.cloned.1.call-start = ((), (), s32[]{:S(2)}) async-start(), calls=%async_computation.18 | async-start | bytes 9437184 | tf_op jit(solution)/shard_map/reduce_scatter | solution.py:113
  86.6 154.7 %copy-start.26 = (f32[2,1024]{1,0:T(2,128)}, f32[2,1024]{1,0:T(2,128)S(1)}, u32[]{:S(2)}) copy-start(f32[2,1024]{1,0:T(2,128)S(1)} %get-tuple-element.108) | copy-start | bytes 24580
  86.6 154.7 %copy-start.37 = (pred[2,1024]{1,0:T(4,128)(4,1)}, pred[2,1024]{1,0:T(4,128)(4,1)S(1)}, u32[]{:S(2)}) copy-start(pred[2,1024]{1,0:T(4,128)(4,1)S(1)} %get-tuple-element.109) | copy-start | bytes 6148
  86.7 154.6 %copy-start.28 = (f32[2,1024]{1,0:T(2,128)}, f32[2,1024]{1,0:T(2,128)S(1)}, u32[]{:S(2)}) copy-start(f32[2,1024]{1,0:T(2,128)S(1)} %get-tuple-element.106) | copy-start | bytes 24580
  86.7 154.6 %copy-start.30 = (f32[2,1024]{1,0:T(2,128)}, f32[2,1024]{1,0:T(2,128)S(1)}, u32[]{:S(2)}) copy-start(f32[2,1024]{1,0:T(2,128)S(1)} %get-tuple-element.107) | copy-start | bytes 24580
  89.9 85.8 %copy-start.62 = (bf16[320,1]{0,1:T(2,128)(2,1)}, bf16[320,1]{0,1:T(2,128)(2,1)S(1)}, u32[]{:S(2)}) copy-start(bf16[320,1]{0,1:T(2,128)(2,1)S(1)} %copy.192) | copy-start | bytes 1924
  90.0 151.3 %copy-start.39 = (f32[320]{0:T(512)}, f32[320]{0:T(512)S(1)}, u32[]{:S(2)}) copy-start(f32[320]{0:T(512)S(1)} %get-tuple-element.90) | copy-start | bytes 3844
  90.0 151.3 %copy-start.41 = (f32[320]{0:T(512)}, f32[320]{0:T(512)S(1)}, u32[]{:S(2)}) copy-start(f32[320]{0:T(512)S(1)} %get-tuple-element.91) | copy-start | bytes 3844
  90.0 151.3 %copy-start.43 = (f32[320]{0:T(512)}, f32[320]{0:T(512)S(1)}, u32[]{:S(2)}) copy-start(f32[320]{0:T(512)S(1)} %get-tuple-element.92) | copy-start | bytes 3844
  90.1 151.3 %copy-start.45 = (f32[320]{0:T(512)}, f32[320]{0:T(512)S(1)}, u32[]{:S(2)}) copy-start(f32[320]{0:T(512)S(1)} %get-tuple-element.93) | copy-start | bytes 3844
  90.1 151.3 %copy-start.53 = (f32[320]{0:T(512)}, f32[320]{0:T(512)S(1)}, u32[]{:S(2)}) copy-start(f32[320]{0:T(512)S(1)} %get-tuple-element.89) | copy-start | bytes 3844
  90.1 151.3 %copy-start.47 = (f32[320]{0:T(512)}, f32[320]{0:T(512)S(1)}, u32[]{:S(2)}) copy-start(f32[320]{0:T(512)S(1)} %fusion.56) | copy-start | bytes 3844
  182.6 11.9 collective-permute-start
  281.1 190.6 %all-gather.28.cloned.1.call-start = ((), (), s32[]{:S(2)}) async-start(), calls=%async_computation.20 | async-start | bytes 7864320 | tf_op jit(solution)/shard_map/all_gather | solution.py:121
  317.2 212.9 %all-gather.26.cloned.1.call-start = ((), (), s32[]{:S(2)}) async-start(), calls=%async_computation.19 | async-start | bytes 9437184 | tf_op jit(solution)/shard_map/all_gather | solution.py:109
  358.5 404.2 %copy-start.58 = (f32[256]{0:T(256)}, f32[256]{0:T(256)S(1)}, u32[]{:S(2)}) copy-start(f32[256]{0:T(256)S(1)} %fusion.62) | copy-start | bytes 3076
  361.2 231.9 %all-gather.30.cloned.1.call-start = ((), (), s32[]{:S(2)}) async-start(), calls=%async_computation.21 | async-start | bytes 3932160 | tf_op jit(solution)/shard_map/all_gather | solution.py:182
  362.2 288.8 %all-gather.32.cloned.1.call-start = ((), (), s32[]{:S(2)}) async-start(), calls=%async_computation.23 | async-start | bytes 9437184 | tf_op jit(solution)/shard_map/all_gather | solution.py:109
  362.9 396.9 %reduce-scatter.19.cloned.1.call-start = ((), (), s32[]{:S(2)}) async-start(), calls=%async_computation.24 | async-start | bytes 9437184 | tf_op jit(solution)/shard_map/reduce_scatter | solution.py:113
  688.9 132.1 %all-gather.34.cloned.1.call-start = ((), (), s32[]{:S(2)}) async-start(), calls=%async_computation.25 | async-start | bytes 9437184 | tf_op jit(solution)/shard_map/all_gather | solution.py:109
  766.0 176.4 %reduce-scatter.29.cloned.1.call-start = ((), (), s32[]{:S(2)}) async-start(), calls=%async_computation.32 | async-start | bytes 3932160 | tf_op jit(solution)/shard_map/reduce_scatter | solution.py:259
  777.9 219.4 %reduce-scatter.27.cloned.1.call-start = ((), (), s32[]{:S(2)}) async-start(), calls=%async_computation.31 | async-start | bytes 7864320 | tf_op jit(solution)/shard_map/reduce_scatter | solution.py:264
  798.1 253.7 %reduce-scatter.23.cloned.1.call-start = ((), (), s32[]{:S(2)}) async-start(), calls=%async_computation.27 | async-start | bytes 3276800 | tf_op jit(solution)/shard_map/reduce_scatter | solution.py:264
  912.1 5.2 collective-permute-start.1
  929.7 194.8 %reduce-scatter.33.cloned.1.call-start = ((), (), s32[]{:S(2)}) async-start(), calls=%async_computation.37 | async-start | bytes 4177920
  942.3 221.8 %all-gather.36.cloned.1.call-start = ((), (), s32[]{:S(2)}) async-start(), calls=%async_computation.33 | async-start | bytes 2359296 | tf_op jit(solution)/shard_map/all_gather | solution.py:260
  942.9 256.6 %all-gather.40.cloned.1.call-start = ((), (), s32[]{:S(2)}) async-start(), calls=%async_computation.35 | async-start | bytes 4718592 | tf_op jit(solution)/shard_map/all_gather | solution.py:268
  997.4 130.0 %copy-start.23 = (bf16[2,1024,320]{2,1,0:T(8,128)(2,1)S(1)}, bf16[2,1024,320]{2,1,0:T(8,128)(2,1)}, u32[]{:S(2)}) copy-start(bf16[2,1024,320]{2,1,0:T(8,128)(2,1)} %get-tuple-element.113) | copy-start | bytes 3932164
  1051.8 74.7 %all-to-all-start.2 = ((bf16[4,128,640]{2,1,0:T(8,128)(2,1)}), bf16[4,128,640]{2,1,0:T(8,128)(2,1)S(1)}, u32[]{:S(2)}, u32[]{:S(2)}) async-start(bf16[4,128,640]{2,1,0:T(8,128)(2,1)} %bitcast.240), calls=%async_computation.7 | async-start | bytes 1310720 | tf_op jit(solution)/shard_map/all_to_all | solution.py:265
  1056.0 171.1 %all-reduce.11.cloned.1.call-start = ((), (), s32[]{:S(2)}) async-start(), calls=%async_computation.28 | async-start | bytes 671744 | tf_op jit(solution)/shard_map/psum | solution.py:333
  1126.4 127.1 %all-gather.38.cloned.1.call-start = ((), (), s32[]{:S(2)}) async-start(), calls=%async_computation.34 | async-start | bytes 1966080 | tf_op jit(solution)/shard_map/all_gather | solution.py:268
  1127.3 202.1 %reduce-scatter.21.cloned.1.call-start = ((), (), s32[]{:S(2)}) async-start(), calls=%async_computation.26 | async-start | bytes 9437184 | tf_op jit(solution)/shard_map/reduce_scatter | solution.py:113
  1138.3 314.2 %reduce-scatter.25.cloned.1.call-start = ((), (), s32[]{:S(2)}) async-start(), calls=%async_computation.29 | async-start | bytes 11141120 | tf_op jit(solution)/shard_map/reduce_scatter | solution.py:333
  1151.3 375.7 %reduce-scatter.17.cloned.1.call-start = ((), (), s32[]{:S(2)}) async-start(), calls=%async_computation.22 | async-start | bytes 9437184 | tf_op jit(solution)/shard_map/reduce_scatter | solution.py:113
  1164.1 423.1 %reduce-scatter.31.cloned.1.call-start = ((), (), s32[]{:S(2)}) async-start(), calls=%async_computation.36 | async-start | bytes 1114112
  1257.3 74.3 %copy-start.55 = (f32[2048]{0:T(1024)S(1)}, f32[2048]{0:T(1024)}, u32[]{:S(2)}) copy-start(f32[2048]{0:T(1024)} %get-tuple-element.85) | copy-start | bytes 24580
  1260.6 72.5 %copy-start.68 = (f32[256]{0:T(256)S(1)}, f32[256]{0:T(256)}, u32[]{:S(2)}) copy-start(f32[256]{0:T(256)} %copy-done.67) | copy-start | bytes 3076
  1260.6 266.4 %copy-start.33 = (f32[1,2048]{1,0:T(1,128)S(1)}, f32[1,2048]{1,0:T(1,128)}, u32[]{:S(2)}) copy-start(f32[1,2048]{1,0:T(1,128)} %copy-done.32) | copy-start | bytes 24580
  1260.6 266.4 %copy-start.59 = (f32[256]{0:T(256)S(1)}, f32[256]{0:T(256)}, u32[]{:S(2)}) copy-start(f32[256]{0:T(256)} %copy-done.58) | copy-start | bytes 3076
  1260.6 266.4 %copy-start.66 = (f32[256]{0:T(256)S(1)}, f32[256]{0:T(256)}, u32[]{:S(2)}) copy-start(f32[256]{0:T(256)} %copy-done.65) | copy-start | bytes 3076
  1333.0 287.9 %all-reduce.13.cloned.1.call-start = ((), (), s32[]{:S(2)}) async-start(), calls=%async_computation.30 | async-start | bytes 1310720 | tf_op jit(solution)/shard_map/psum | solution.py:333
  1527.0 96.2 %copy-start.1 = (bf16[384,2048]{1,0:T(8,128)(2,1)S(1)}, bf16[384,2048]{1,0:T(8,128)(2,1)}, u32[]{:S(2)}) copy-start(bf16[384,2048]{1,0:T(8,128)(2,1)} %param.24) | copy-start | bytes 4718596
  (55 other events, 893.8 us)
Sparse Core Ops, SparseCore 0:
  11.6 42.5 all-gather.17
  56.4 52.3 all-gather.21
  111.2 55.5 all-gather.19
  169.0 86.9 all-gather.23
  281.2 75.6 reduce-scatter.14
  359.0 112.6 all-gather.27
  474.3 55.7 all-gather.25
  532.3 60.6 all-gather.29
  595.1 55.8 all-gather.31
  689.1 70.7 reduce-scatter.18
  766.1 54.8 all-gather.33
  823.2 59.7 reduce-scatter.28
  885.9 111.4 reduce-scatter.26
  1000.1 51.6 reduce-scatter.22
  1055.5 68.9 reduce-scatter.32
  1126.0 27.0 all-gather.35
  1154.6 44.9 all-gather.39
  1202.4 24.7 all-reduce.10
  1229.3 24.1 all-gather.37
  1257.2 72.0 reduce-scatter.20
  1333.4 119.0 reduce-scatter.24
  1455.9 71.0 reduce-scatter.16
  1531.7 55.4 reduce-scatter.30
  1589.3 31.5 all-reduce.12

commit v2 on v1

--- a/solution.py
+++ b/solution.py
@@ -111,6 +111,532 @@
 
 def plane_scatter(partial):
     return lax.psum_scatter(partial.astype(BF), PLANE, scatter_dimension=0, tiled=True)
+
+
+MESH = pl.DeviceIdType.MESH
+
+
+class Wires:
+    def __init__(self, send_sems, recv_sems):
+        self.send_sems, self.recv_sems, self.used = send_sems, recv_sems, 0
+
+    def far(self, src, dst, device):
+        at = self.used
+        self.used += 1
+        return pltpu.make_async_remote_copy(
+            src_ref=src,
+            dst_ref=dst,
+            send_sem=self.send_sems.at[at],
+            recv_sem=self.recv_sems.at[at],
+            device_id=device,
+            device_id_type=MESH,
+        )
+
+    def near(self, src, dst):
+        at = self.used
+        self.used += 1
+        return pltpu.make_async_copy(src, dst, self.send_sems.at[at])
+
+
+def greet(devices):
+    barrier = pltpu.get_barrier_semaphore()
+    for device in devices:
+        pl.semaphore_signal(barrier, inc=1, device_id=device, device_id_type=MESH)
+    pl.semaphore_wait(barrier, len(devices))
+
+
+def sides():
+    x, l, y, c = tuple(lax.axis_index(name) for name in EVERY)
+    x_a, y_a = x + (1 - c) * (1 - 2 * x), y + c * (1 - 2 * y)
+    x_b, y_b = x + c * (1 - 2 * x), y + (1 - c) * (1 - 2 * y)
+    return (x, l, y, c), (x, l, y, 1 - c), (x_a, l, y_a, c), (x_b, l, y_b, c)
+
+
+def slot_of(device):
+    return device[0] * 4 + device[2] * 2 + device[3]
+
+
+def over_rows(length, rows, step):
+    @pl.loop(0, length // rows)
+    def _(i):
+        step(pl.ds(pl.multiple_of(i * rows, rows), rows))
+
+
+class PlaneSum:
+    def __init__(self, wires, partial, own, got, hop_a, hop_b, cuts):
+        self.own, self.got, self.hop_a, self.hop_b = own, got, hop_a, hop_b
+        self.cuts, self.part = cuts, own.shape[1] // cuts
+        me, core, side_a, side_b = sides()
+        diag = (1 - me[0], me[1], 1 - me[2], me[3])
+        self.chips = [me, side_a, side_b, diag]
+        self.theirs = {0: 0, 1: 2, 2: 1, 3: 3}
+        self.order = [3, 1, 2, 0]
+        self.swaps, self.loads = {}, {}
+        self.far_a, self.near_a, self.far_b = {}, {}, {}
+        for piece in range(cuts):
+            rows = pl.ds(piece * self.part, self.part)
+            for rel in self.order:
+                chip = self.chips[rel]
+                away = slot_of((chip[0], chip[1], chip[2], 1 - me[3]))
+                self.swaps[rel, piece] = wires.far(
+                    partial.at[away, rows], got.at[self.theirs[rel], rows], core
+                )
+                self.loads[rel, piece] = wires.near(
+                    partial.at[slot_of(chip), rows], own.at[rel, rows]
+                )
+            self.far_a[piece] = wires.far(own.at[3, rows], hop_a.at[0, rows], side_a)
+            self.near_a[piece] = wires.far(own.at[1, rows], hop_a.at[1, rows], side_a)
+            self.far_b[piece] = wires.far(own.at[2, rows], hop_b.at[rows], side_b)
+
+    def start(self):
+        for rel in self.order:
+            for piece in range(self.cuts):
+                self.swaps[rel, piece].start()
+                self.loads[rel, piece].start()
+
+    def landed(self, rel, piece):
+        self.loads[rel, piece].wait()
+        self.swaps[self.theirs[rel], piece].wait_recv()
+
+    def join(self, rel, piece, hopped):
+        @pl.loop(0, self.part // 16)
+        def _(i):
+            rows = pl.ds(pl.multiple_of(piece * self.part + i * 16, 16), 16)
+            total = self.own[rel, rows].astype(F32) + self.got[rel, rows].astype(F32)
+            if hopped:
+                total = total + self.hop_a[0, rows].astype(F32)
+            self.own[rel, rows] = total.astype(BF)
+
+    def first_side(self):
+        for rel, copies in ((3, self.far_a), (1, self.near_a)):
+            for piece in range(self.cuts):
+                self.landed(rel, piece)
+                self.join(rel, piece, False)
+                copies[piece].start()
+
+    def second_side(self):
+        for piece in range(self.cuts):
+            self.landed(2, piece)
+            self.far_a[piece].wait_recv()
+            self.join(2, piece, True)
+            self.far_b[piece].start()
+
+    def finish(self, piece, use):
+        self.landed(0, piece)
+        self.near_a[piece].wait_recv()
+        self.far_b[piece].wait_recv()
+
+        @pl.loop(0, self.part // 16)
+        def _(i):
+            rows = pl.ds(pl.multiple_of(piece * self.part + i * 16, 16), 16)
+            total = self.own[0, rows].astype(F32) + self.got[0, rows].astype(F32)
+            total = total + self.hop_a[1, rows].astype(F32) + self.hop_b[rows].astype(F32)
+            use(rows, total)
+
+    def drain(self):
+        for piece in range(self.cuts):
+            for rel in self.order:
+                self.swaps[rel, piece].wait_send()
+            for copy in (self.far_a[piece], self.near_a[piece], self.far_b[piece]):
+                copy.wait_send()
+
+
+class LineSum:
+    def __init__(self, wires, lines, own, from_left, from_right, root):
+        x, l, y, c = (lax.axis_index(name) for name in EVERY)
+        self.own, self.from_left, self.from_right = own, from_left, from_right
+        self.l, self.root, self.lines = l, root, lines
+        self.to_right = wires.far(own, from_left, (x, l + 1, y, c))
+        self.to_left = wires.far(own, from_right, (x, l - 1, y, c))
+
+    def add(self, other):
+        @pl.loop(0, self.own.shape[0] // 16)
+        def _(i):
+            at = pl.ds(pl.multiple_of(i * 16, 16), 16)
+            self.own[at] = (self.own[at].astype(F32) + other[at].astype(F32)).astype(BF)
+
+    def rightward(self):
+        @pl.when(self.l < self.root)
+        def _():
+            @pl.when(self.l > 0)
+            def _():
+                self.to_right.wait_recv()
+                self.add(self.from_left)
+
+            self.to_right.start()
+
+    def leftward(self):
+        @pl.when(self.l > self.root)
+        def _():
+            @pl.when(self.l < self.lines - 1)
+            def _():
+                self.to_left.wait_recv()
+                self.add(self.from_right)
+
+            self.to_left.start()
+
+    def end(self):
+        @pl.when(self.l == self.root)
+        def _():
+            @pl.when(self.l > 0)
+            def _():
+                self.to_right.wait_recv()
+                self.add(self.from_left)
+
+            @pl.when(self.l < self.lines - 1)
+            def _():
+                self.to_left.wait_recv()
+                self.add(self.from_right)
+
+    def drain(self):
+        @pl.when(self.l < self.root)
+        def _():
+            self.to_right.wait_send()
+
+        @pl.when(self.l > self.root)
+        def _():
+            self.to_left.wait_send()
+
+
+def back_rows(base_ref, up_ref, gain_ref, out_ref, gain_out, mine):
+    def use(rows, total):
+        base = base_ref[rows].astype(F32)
+        scale = lax.rsqrt(jnp.mean(base * base, axis=-1, keepdims=True) + EPSILON)
+        lean = total * gain_ref[...]
+        along = jnp.mean(lean * base, axis=-1, keepdims=True)
+        grad = up_ref[rows].astype(F32) + scale * lean
+        grad = grad - base * (scale * scale * scale * along)
+        out_ref[rows] = grad
+        if mine is not None:
+            mine[rows] = grad.astype(BF)
+        share = total * base * scale
+        gain_out[...] += share[:8] + share[8:]
+
+    return use
+
+
+def forward_rows(base_ref, gain_ref, out_ref, mine):
+    def use(rows, total):
+        base = base_ref[rows].astype(F32) + total
+        out_ref[rows] = base
+        scale = lax.rsqrt(jnp.mean(base * base, axis=-1, keepdims=True) + EPSILON)
+        mine[rows] = (base * scale * gain_ref[...]).astype(BF)
+
+    return use
+
+
+class PlaneGather:
+    def __init__(self, wires, mine, everything, cuts):
+        me, core, side_a, side_b = sides()
+        diag = (1 - me[0], me[1], 1 - me[2], me[3])
+        here, from_a, from_b, from_diag = [slot_of(at) for at in (me, side_a, side_b, diag)]
+        self.cuts, self.copies = cuts, {}
+        part = mine.shape[0] // cuts
+        for piece in range(cuts):
+            rows = pl.ds(piece * part, part)
+            for name, src, slot, target in (
+                ("a", mine.at[rows], here, side_a),
+                ("b", mine.at[rows], here, side_b),
+                ("c", mine.at[rows], here, core),
+                ("ab", everything.at[from_a, rows], from_a, side_b),
+                ("ac", everything.at[from_a, rows], from_a, core),
+                ("bc", everything.at[from_b, rows], from_b, core),
+                ("dc", everything.at[from_diag, rows], from_diag, core),
+            ):
+                self.copies[name, piece] = wires.far(src, everything.at[slot, rows], target)
+            self.copies["own", piece] = wires.near(mine.at[rows], everything.at[here, rows])
+
+    def start(self, piece):
+        for name in ("a", "b", "c", "own"):
+            self.copies[name, piece].start()
+
+    def forward(self, came, goes):
+        for piece in range(self.cuts):
+            self.copies[came, piece].wait_recv()
+            for name in goes:
+                self.copies[name, piece].start()
+
+    def finish(self):
+        for piece in range(self.cuts):
+            for name in ("c", "ac", "bc", "dc"):
+                self.copies[name, piece].wait_recv()
+            self.copies["own", piece].wait()
+            for name in ("a", "b", "c", "ab", "ac", "bc", "dc"):
+                self.copies[name, piece].wait_send()
+
+
+def plane_kernel(mode, cuts, *refs):
+    refs = list(refs)
+    partial, base_ref = refs.pop(0), refs.pop(0)
+    up_ref = refs.pop(0) if mode == "back" else None
+    gain_ref, out_ref = refs.pop(0), refs.pop(0)
+    gain_out = refs.pop(0) if mode == "back" else None
+    all_ref, own, got, hop_a, hop_b, mine, send_sems, recv_sems = refs
+    _, core, side_a, side_b = sides()
+    wires = Wires(send_sems, recv_sems)
+    greet([core, side_a, side_b])
+    total = PlaneSum(wires, partial, own, got, hop_a, hop_b, cuts)
+    spread = PlaneGather(wires, mine, all_ref, cuts)
+    total.start()
+    total.first_side()
+    total.second_side()
+    if mode == "back":
+        gain_out[...] = jnp.zeros_like(gain_out)
+        use = back_rows(base_ref, up_ref, gain_ref, out_ref, gain_out, mine)
+    else:
+        use = forward_rows(base_ref, gain_ref, out_ref, mine)
+    for piece in range(cuts):
+        total.finish(piece, use)
+        spread.start(piece)
+    spread.forward("a", ("ab", "ac"))
+    spread.forward("b", ("bc",))
+    spread.forward("ab", ("dc",))
+    spread.finish()
+    total.drain()
+
+
+def sum_scratch(length, width):
+    return [
+        pltpu.VMEM((4, length, width), BF),
+        pltpu.VMEM((4, length, width), BF),
+        pltpu.VMEM((2, length, width), BF),
+        pltpu.VMEM((length, width), BF),
+    ]
+
+
+def plane_sum(partial, base, up, gain, number):
+    mode = "forward" if up is None else "back"
+    length, width = base.shape
+    cuts = 2
+    vmem, left = pl.BlockSpec(memory_space=pltpu.VMEM), pl.BlockSpec(memory_space=pl.ANY)
+    args, specs = [partial.reshape(8, length, width), base], [left, vmem]
+    outs, out_specs = [jax.ShapeDtypeStruct((length, width), F32)], [vmem]
+    if mode == "back":
+        args.append(up)
+        specs.append(vmem)
+        outs.append(jax.ShapeDtypeStruct((8, width), F32))
+        out_specs.append(vmem)
+    args.append(gain.reshape(1, width))
+    specs.append(vmem)
+    outs.append(jax.ShapeDtypeStruct((8, length, width), BF))
+    out_specs.append(left)
+    sems = cuts * (8 + 3 + 8)
+    got = list(
+        pl.pallas_call(
+            functools.partial(plane_kernel, mode, cuts),
+            out_shape=outs,
+            in_specs=specs,
+            out_specs=out_specs,
+            scratch_shapes=sum_scratch(length, width)
+            + [
+                pltpu.VMEM((length, width), BF),
+                pltpu.SemaphoreType.DMA((sems,)),
+                pltpu.SemaphoreType.DMA((sems,)),
+            ],
+            compiler_params=pltpu.CompilerParams(
+                collective_id=number, has_side_effects=True, vmem_limit_bytes=40 << 20
+            ),
+            cost_estimate=pl.CostEstimate(
+                flops=20 * base.size, bytes_accessed=400 * base.size, transcendentals=0
+            ),
+            name=f"plane_{mode}_{number}",
+        )(*args)
+    )
+    got[-1] = got[-1].reshape(8 * length, width)
+    return got
+
+
+def tail_kernel(lines, cuts, *refs):
+    (partial, base_ref, up_ref, gain_ref, other_gain, in_ref, chan_ref, upz, downz) = refs[:9]
+    (out_ref, in_all, chan_out, up_all, down_all, gains) = refs[9:15]
+    (own, got, hop_a, hop_b, gain_out, in_own, in_left, in_right) = refs[15:23]
+    (chan_own, chan_left, chan_right, chan_got, tiny, tiny_line, send_sems, recv_sems) = refs[23:]
+    me, core, side_a, side_b = sides()
+    x, l, y, c = me
+    k = 2 * y + c
+    mates = [core, (x, l, 1 - y, c), (x, l, 1 - y, 1 - c)]
+    twin = (1 - x, l, y, c)
+    twins = [(1 - x, l, at[2], at[3]) for at in mates]
+    wires = Wires(send_sems, recv_sems)
+    others = [(x, lax.rem(l + d, lines), y, c) for d in range(1, lines)]
+    greet(mates + [twin] + twins + others)
+
+    total = PlaneSum(wires, partial, own, got, hop_a, hop_b, cuts)
+    per = chan_ref.shape[0]
+    owner = (4 * x + k) * per
+    load_in = wires.near(in_ref, in_own)
+    load_chan = wires.near(chan_ref, chan_own)
+    in_sums = [
+        LineSum(wires, lines, in_own.at[q], in_left.at[q], in_right.at[q], q)
+        for q in range(lines)
+    ]
+    chan_roots = [(owner + i) // 4 for i in range(per)]
+    chan_sums = [
+        LineSum(wires, lines, chan_own.at[i], chan_left.at[i], chan_right.at[i], chan_roots[i])
+        for i in range(per)
+    ]
+
+    def deliver(block, target):
+        copies = [wires.near(block(k), target.at[x, k])]
+        for at in [twin] + mates + twins:
+            copies.append(wires.far(block(2 * at[2] + at[3]), target.at[x, k], at))
+        return copies
+
+    total.start()
+    load_in.start()
+    load_chan.start()
+    up_copies = deliver(lambda to: upz.at[to], up_all)
+    down_copies = [wires.near(downz, down_all.at[x]), wires.far(downz, down_all.at[x], twin)]
+    load_in.wait()
+    q = lines - 1
+    in_sums[q].rightward()
+    in_sums[lines - 1 - q].leftward()
+    total.first_side()
+    for copy in down_copies + up_copies:
+        copy.start()
+    total.second_side()
+    for q in reversed(range(1, lines - 1)):
+        in_sums[q].rightward()
+        in_sums[lines - 1 - q].leftward()
+    gain_out[...] = jnp.zeros_like(gain_out)
+    use = back_rows(base_ref, up_ref, gain_ref, out_ref, gain_out, None)
+    for piece in range(cuts):
+        total.finish(piece, use)
+    load_chan.wait()
+    for one in chan_sums:
+        one.rightward()
+        one.leftward()
+    for q in range(lines):
+        in_sums[q].end()
+    rows = in_all.shape[2]
+    in_copies = deliver(
+        lambda to: in_own.at[l, pl.ds(pl.multiple_of(to * rows, rows), rows)], in_all
+    )
+    for copy in in_copies:
+        copy.start()
+    lane = lax.broadcasted_iota(jnp.int32, tiny.shape[1:], 0)
+    first = jnp.sum(gain_out[...], axis=0, keepdims=True)
+    second = jnp.sum(other_gain[...], axis=0, keepdims=True)
+    tiny[0] = jnp.where(lane == 0, first, jnp.where(lane == 1, second, 0.0))
+    for step, at in enumerate((core, twin, (x, l, 1 - y, c))):
+        copy = wires.far(tiny.at[2 * step], tiny.at[2 * step + 1], at)
+        copy.start()
+        copy.wait()
+        tiny[2 * step + 2] = tiny[2 * step] + tiny[2 * step + 1]
+    line_copies = []
+    for d, device in enumerate(others):
+        line_copies.append(wires.far(tiny.at[6], tiny_line.at[l], device))
+        line_copies[-1].start()
+    tiny_line[l] = tiny[6]
+    for one in chan_sums:
+        one.end()
+    goal = 4 * l + k
+    holds = goal // (4 * per) == x
+    chan_far, chan_near = [], []
+    for i in range(per):
+        s = owner + i
+        mate = (x, l, lax.rem(s, 4) // 2, lax.rem(s, 2))
+        far = wires.far(chan_own.at[i], chan_got, mate)
+        near = wires.near(chan_own.at[i], chan_got)
+        at_root = chan_roots[i] == l
+        away = jnp.logical_and(at_root, lax.rem(s, 4) != k)
+        stay = jnp.logical_and(at_root, lax.rem(s, 4) == k)
+        chan_far.append((far, away))
+        chan_near.append((near, stay))
+
+        @pl.when(away)
+        def _():
+            far.start()
+
+        @pl.when(stay)
+        def _():
+            near.start()
+            near.wait()
+
+    holder = lax.rem(goal // per, 4)
+    for i in range(per):
+        mine_here = jnp.logical_and(holds, lax.rem(goal, per) == i)
+
+        @pl.when(jnp.logical_and(mine_here, holder != k))
+        def _():
+            chan_far[i][0].wait_recv()
+
+    to_twin = wires.far(chan_got, chan_out, twin)
+    keep = wires.near(chan_got, chan_out)
+
+    @pl.when(holds)
+    def _():
+        to_twin.start()
+        keep.start()
+        keep.wait()
+
+    @pl.when(jnp.logical_not(holds))
+    def _():
+        to_twin.wait_recv()
+
+    for copy in line_copies:
+        copy.wait()
+    gains[...] = tiny_line[0]
+    for q in range(1, lines):
+        gains[...] += tiny_line[q]
+    for copies in (in_copies, up_copies, down_copies):
+        for copy in copies:
+            copy.wait()
+
+    @pl.when(holds)
+    def _():
+        to_twin.wait_send()
+
+    for far, away in chan_far:
+
+        @pl.when(away)
+        def _():
+            far.wait_send()
+
+    for one in in_sums + chan_sums:
+        one.drain()
+    total.drain()
+
+
+def tail(partial, base, up, gain, other_gain, in_grad, chan, upz, downz, lines):
+    length, width = base.shape
+    cuts = 2
+    vmem, left = pl.BlockSpec(memory_space=pltpu.VMEM), pl.BlockSpec(memory_space=pl.ANY)
+    rows = in_grad.shape[0] // (4 * lines)
+    pieces = in_grad.reshape(lines, 4 * rows, in_grad.shape[1])
+    per = chan.shape[0]
+    sems = cuts * 11 + 2 + 2 * (lines + per) + 16 + 2 + 8 + 3 + lines + 2 * per + 4
+    return pl.pallas_call(
+        functools.partial(tail_kernel, lines, cuts),
+        out_shape=[
+            jax.ShapeDtypeStruct((length, width), F32),
+            jax.ShapeDtypeStruct((2, 4, rows, in_grad.shape[1]), BF),
+            jax.ShapeDtypeStruct(chan.shape[1:], BF),
+            jax.ShapeDtypeStruct((2,) + upz.shape, BF),
+            jax.ShapeDtypeStruct((2,) + downz.shape, BF),
+            jax.ShapeDtypeStruct((8, width), F32),
+        ],
+        in_specs=[left, vmem, vmem, vmem, vmem, left, left, left, left],
+        out_specs=[vmem, left, left, left, left, vmem],
+        scratch_shapes=sum_scratch(length, width)
+        + [pltpu.VMEM((8, width), F32)]
+        + [pltpu.VMEM(pieces.shape, BF)] * 3
+        + [pltpu.VMEM(chan.shape, BF)] * 3
+        + [
+            pltpu.VMEM(chan.shape[1:], BF),
+            pltpu.VMEM((7, 8, width), F32),
+            pltpu.VMEM((lines, 8, width), F32),
+            pltpu.SemaphoreType.DMA((sems,)),
+            pltpu.SemaphoreType.DMA((sems,)),
+        ],
+        compiler_params=pltpu.CompilerParams(
+            collective_id=3, has_side_effects=True, vmem_limit_bytes=56 << 20
+        ),
+        cost_estimate=pl.CostEstimate(
+            flops=20 * base.size, bytes_accessed=400 * base.size, transcendentals=0
+        ),
+        name="tail",
+    )(partial.reshape(8, length, width), base, up, gain.reshape(1, width), other_gain, pieces, chan, upz, downz)
 
 
 def columns_in(weight, pieces):
@@ -237,43 +763,25 @@
         state_in = jnp.where(other < line, longer, state_in)
     state = local_state + prefix_coef * state_in[:, None]
     mixed = (state * jax.nn.gelu(branch)).astype(BF).reshape(plane, own)
-    residual = inputs + plane_scatter(
-        jnp.dot(mixed, out_matrix, preferred_element_type=F32)
-    ).astype(F32)
-
-    normed_two = norm_rows(residual, gain_two).astype(BF)
-    all_two = plane_gather(normed_two)
+    partial = jnp.dot(mixed, out_matrix, preferred_element_type=F32).astype(BF)
+    residual, all_two = plane_sum(partial, tokens, None, gain_two, 1)
     hidden = jnp.dot(all_two, up_matrix, preferred_element_type=F32)
     part = ff // 8
     activated = gated_product(hidden[:, :part], hidden[:, part:]).astype(BF)
-    output = (
-        residual
-        + plane_scatter(jnp.dot(activated, down_matrix, preferred_element_type=F32)).astype(F32)
-    ).astype(BF)
+    out_partial = jnp.dot(activated, down_matrix, preferred_element_type=F32).astype(BF)
+    out_partial, all_cot = lax.optimization_barrier((out_partial, all_cot))
+    output = (residual + plane_scatter(out_partial).astype(F32)).astype(BF)
 
     act_grad = times_transposed(all_cot, down_matrix)
     _, act_pull = jax.vjp(gated_product, hidden[:, :part], hidden[:, part:])
     hidden_grad = jnp.concatenate(act_pull(act_grad), axis=1).astype(BF)
-    normed_two_grad = plane_scatter(times_transposed(hidden_grad, up_matrix)).astype(F32)
+    partial = times_transposed(hidden_grad, up_matrix).astype(BF)
     down_grad = contract_rows(activated, all_cot).astype(BF)
-    down_grad = lax.psum_scatter(down_grad, "l", scatter_dimension=0, tiled=True)
-    down_grad = lax.all_gather(down_grad, "x", axis=0, tiled=True).astype(F32)
     up_grad = contract_rows(all_two, hidden_grad).astype(BF)
-
-    def columns_out(grad):
-        grad = lax.psum_scatter(grad, "l", scatter_dimension=0, tiled=True)
-        grad = lax.all_to_all(
-            grad.reshape(4, rows, -1), ("y", "c"), split_axis=0, concat_axis=0, tiled=True
-        )
-        return lax.all_gather(grad, "x", axis=0, tiled=False)
-
-    up_grad = columns_out(up_grad).reshape(2, 4, rows, 2 * lines, share)
-    up_grad = up_grad.transpose(2, 3, 1, 0, 4).reshape(rows, 2 * ff).astype(F32)
-
-    _, norm_two_pull = jax.vjp(norm_rows, residual, gain_two)
-    residual_norm_grad, gain_two_grad = norm_two_pull(normed_two_grad)
-    residual_grad = cotangent.astype(F32) + residual_norm_grad
-    all_res = plane_gather(residual_grad.astype(BF))
+    partial, down_grad, up_grad = lax.optimization_barrier((partial, down_grad, up_grad))
+    down_line = lax.psum_scatter(down_grad, "l", scatter_dimension=0, tiled=True)
+    up_line = lax.psum_scatter(up_grad, "l", scatter_dimension=0, tiled=True)
+    residual_grad, gain_two_grad, all_res = plane_sum(partial, residual, cotangent, gain_two, 2)
     mixed_grad = times_transposed(all_res, out_matrix).reshape(2, run, own)
     out_grad = contract_rows(mixed, all_res)
     _, mix_pull = jax.vjp(
@@ -319,41 +827,47 @@
     conv_in_grad = edge_sum[:, 3:] + jnp.pad(back_edge, ((0, 0), (run - 3, 0), (0, 0)))
     proj_grad = jnp.concatenate([branch_grad, conv_in_grad], axis=-1).astype(BF)
     proj_grad = proj_grad.reshape(plane, 2 * own)
-    normed_one_grad = plane_scatter(times_transposed(proj_grad, in_matrix)).astype(F32)
-    in_grad = columns_out(contract_rows(all_one, proj_grad).astype(BF))
-    in_grad = in_grad.reshape(2, 4, rows, 2, own).transpose(2, 3, 0, 1, 4)
+    partial = times_transposed(proj_grad, in_matrix).astype(BF)
+    in_grad = contract_rows(all_one, proj_grad).astype(BF)
+    owned = channels // owners
+    chan = jnp.concatenate(
+        [out_grad, tap_grads.T, bias_grad.T, decay_grad[:, None], gate_grad], axis=1
+    ).astype(BF)
+    used = chan.shape[1]
+    chan = jnp.pad(
+        chan.reshape(own // owned, owned, used), ((0, 0), (0, -owned % 16), (0, -used % 128))
+    )
+    input_grad, in_all, chan, up_all, down_all, gain_grads = tail(
+        partial,
+        tokens,
+        residual_grad,
+        gain_one,
+        gain_two_grad,
+        in_grad,
+        chan,
+        up_line.reshape(4, rows, -1),
+        down_line,
+        lines,
+    )
+    in_grad = in_all.reshape(2, 4, rows, 2, own).transpose(2, 3, 0, 1, 4)
     in_grad = in_grad.reshape(rows, 2 * channels).astype(F32)
-    _, norm_one_pull = jax.vjp(norm_rows, inputs, gain_one)
-    input_norm_grad, gain_one_grad = norm_one_pull(normed_one_grad)
-    input_grad = residual_grad + input_norm_grad
-
-    def to_owners(values):
-        padded = jnp.zeros((channels,) + values.shape[1:], values.dtype)
-        padded = lax.dynamic_update_slice_in_dim(padded, values, mine * own, 0)
-        return lax.psum(lax.psum_scatter(padded, SHARD, scatter_dimension=0, tiled=True), "x")
-
-    out_grad = to_owners(out_grad.astype(BF)).astype(F32)
-    small = jnp.concatenate(
-        [tap_grads.T, bias_grad.T, decay_grad[:, None], gate_grad], axis=1
-    )
-    small = to_owners(small)
-    gain_grads = lax.psum(
-        lax.psum_scatter(
-            jnp.stack([gain_one_grad, gain_two_grad], axis=1), SHARD, scatter_dimension=0, tiled=True
-        ),
-        "x",
-    )
+    up_grad = up_all.reshape(2, 4, rows, 2 * lines, share).transpose(2, 3, 1, 0, 4)
+    up_grad = up_grad.reshape(rows, 2 * ff).astype(F32)
+    down_grad = down_all.reshape(2 * share, width).astype(F32)
+    out_grad = chan[:owned, :width].astype(F32)
+    small = chan[:owned, width:used].astype(F32)
+    gain_grads = lax.dynamic_slice_in_dim(gain_grads[:2], me * rows, rows, 1)
     return (
         output,
         input_grad,
-        gain_grads[:, 0],
+        gain_grads[0],
         in_grad,
         small[:, :5].T,
         small[:, 8:],
         small[:, 5:7].T,
         small[:, 7],
         out_grad,
-        gain_grads[:, 1],
+        gain_grads[1],
         up_grad,
         down_grad,
     )

time: 1640 us -> 1030 us (0.63)
  waiting for transfers between devices: 1040 us -> 145 us
  Pallas kernels: 10.7 us -> 356 us
  blocking collectives: 144 us -> 114 us
  other arithmetic: 102 us -> 80.5 us
    pallas_call x0 -> x3, Pallas kernels: none -> 345 us  [the longest x1 191 us: tail(): pl.pallas_call(functools.partial(tail_kernel, lines, cuts), out_shape=[ja...]
    reduce_scatter x4 -> x1, waiting for transfers between devices: 253 us -> 0.01 us  [plane_scatter(): lax.psum_scatter(partial.astype(BF), PLANE, scatter_dimension=0, tiled=True)]
    reduce_scatter x3 -> x1, waiting for transfers between devices: 204 us -> 0.01 us  [on_device(): up_line = lax.psum_scatter(up_grad, 'l', scatter_dimension=0, tiled=True)]
    unnamed x26 -> x10, waiting for transfers between devices: 125 us -> 2.01 us
    all_gather x2, waiting for transfers between devices: 127 us -> 13.6 us  [columns_in(): return lax.all_gather(got.reshape(4 * rows, -1), 'l', axis=0, tiled=True)]
    all_gather x4 -> x2, waiting for transfers between devices: 193 us -> 90.2 us  [plane_gather(): return lax.all_gather(block, PLANE, axis=0, tiled=True)]
    all_gather x3 -> x0, waiting for transfers between devices: 52.5 us -> none  [the longest x2 52.5 us: columns_out(): return lax.all_gather(grad, 'x', axis=0, tiled=False)]
    psum x2 -> x0, waiting for transfers between devices: 42.3 us -> none  [to_owners(): lax.psum(lax.psum_scatter(padded, SHARD, scatter_dimension=0, tiled=True)...]
  transfers between devices with their start and end apart: 27 -> 12, of which waited for: 21 -> 4; matrix products, arithmetic and copies ran while one was open for 20% -> 28% of each run, Pallas kernels for 1% -> 35%
where the time goes in v2:
time: 1030 us; the launch traced here: 1020 us
  Pallas kernels  356 us (35%)
  matrix products  152 us (15%)
  local copies, waits for them, and re-layouts  145 us (14%)
  waiting for transfers between devices  145 us (14%)
  blocking collectives  114 us (11%)
  other arithmetic  80.5 us (8%)
  between operations  15.7 us (2%)
    pallas_call x1, Pallas kernels, tail(): pl.pallas_call(functools.partial(tail_kernel, lines, cuts), out_shape=[ja...  191 us
    pallas_call x2, Pallas kernels, plane_sum(): pl.pallas_call(functools.partial(plane_kernel, mode, cuts), out_shape=out...  153 us
    all_gather x2, waiting for transfers between devices, plane_gather(): return lax.all_gather(block, PLANE, axis=0, tiled=True)  90.2 us
    dot_general x4, matrix products, times_transposed(): lax.dot_general(left_in, matrix, (((1,), (1,)), ((), ())), preferred_elem...  58.6 us
    unnamed x161, local copies, waits for them, and re-layouts  47.1 us
    dot_general x4, matrix products, contract_rows(): lax.dot_general(left_in, right_in, (((0,), (0,)), ((), ())), preferred_el...  44 us
    all_gather x1, waiting for transfers between devices, on_device(): lax.all_gather(lax.dynamic_slice_in_dim(mlp_out, half * share, share, 0),...  39 us
    all_gather x1, blocking collectives, on_device(): lax.all_gather(seg_ids, EVERY, axis=0, tiled=True).reshape(2, lines, run)  36.8 us
  transfers between devices with their start and end apart: 12, of which 4 were waited for; matrix products, arithmetic and copies ran while one was open for 28% of the time, Pallas kernels for 35%

profile of v2, /device:TPU:11, one launch (start us, length us, event | category | flops | bytes accessed | tf_op | source)
XLA Modules:
  0.0 1016.6 jit_solution(18144469966197847210)
XLA Ops:
  13.4 14.3 %all_to_all.10 = bf16[4,128,2,320]{1,3,2,0:T(8,128)(2,1)S(1)} all-to-all(bf16[4,128,2,320]{1,3,2,0:T(8,128)(2,1)S(1)} %copy.133), channel_id=1, replica_groups=mesh['x'=2,'l'=4,'y'=2,'c'=2] {'y','c'}, dimensions={0} | all-to-all | bytes 1310720 | tf_op jit(solution)/shard_map/all_to_all | solution.py:646
  29.3 18.0 %all_gather.40 = bf16[2,2048]{1,0:T(2,128)(2,1)S(1)} all-gather(bf16[2,128]{1,0:T(2,128)(2,1)S(1)} %pad_maximum_fusion.10), channel_id=1, replica_groups=mesh['x'=2,'l'=4,'y'=2,'c'=2] {'l','y','c'}, dimensions={1}, use_global_device_ids=true | all-gather | bytes 8704 | tf_op jit(solution)/shard_map/all_gather | solution.py:682
  50.2 4.7 copy.143
  56.5 21.7 %all_to_all.11 = bf16[4,128,8,192]{1,3,2,0:T(8,128)(2,1)S(1)} all-to-all(bf16[4,128,8,192]{1,3,2,0:T(8,128)(2,1)S(1)} %copy.144), channel_id=1, replica_groups=mesh['x'=2,'l'=4,'y'=2,'c'=2] {'y','c'}, dimensions={0} | all-to-all | bytes 3145728 | tf_op jit(solution)/shard_map/all_to_all | solution.py:646
  82.9 36.8 %all-gather.2 = s32[32,1,256]{2,1,0:T(1,128)S(1)} all-gather(s32[1,1,256]{2,1,0:T(1,128)S(1)} %bitcast.264), channel_id=1, replica_groups=mesh['x'=2,'l'=4,'y'=2,'c'=2] {'x','l','y','c'}, dimensions={0}, use_global_device_ids=true | all-gather | bytes 33792 | tf_op jit(solution)/shard_map/all_gather | solution.py:686
  123.7 43.3 %all-gather.13.cloned.1.call-done = bf16[2048,2048]{1,0:T(8,128)(2,1)} async-done(((bf16[256,2048]{1,0:T(8,128)(2,1)}), bf16[2048,2048]{1,0:T(8,128)(2,1)}) %all-gather.13.cloned.1.call-update) | async-done | bytes 8388624 | tf_op jit(solution)/shard_map/all_gather | solution.py:109
  166.9 8.9 fusion.59
  185.9 3.6 slice.276
  194.9 7.2 add_convert_fusion.1
  205.1 3.5 reshape.346
  212.7 4.8 reshape.349
  217.6 5.6 copy.139
  223.2 4.9 reshape.348
  228.1 5.5 copy.138
  233.7 11.8 %convert_multiply_fusion.1 = (f32[2,1024,320]{2,1,0:T(8,128)S(1)}, f32[2,1024,320]{2,1,0:T(8,128)S(1)}) fusion(f32[320]{0:T(512)S(1)} %fusion.46, pred[2,1024]{1,0:T(4,128)(4,1)S(1)} %get-tuple-element.125, f32[2,1024,320]{2,1,0:T(8,128)} %copy.139, f32[320]{0:T(512)S(1)} %get-tuple-element.110, f32[2,1024,320]{2,1,0:T(8,128)} %copy.138, ...), kind=kLoop, calls=%fused_computation.24 | loop fusion | flops 18350080 | bytes 21008384 | tf_op jit(solution)/shard_map/jvp()/mul | solution.py:101
  245.5 5.3 scan_fwd.1
  250.9 9.0 all-gather
  264.1 8.7 convolution_convert_fusion.3
  272.8 78.0 %plane_forward_1.1 = (f32[256,2048]{1,0:T(8,128)S(1)}, bf16[8,256,2048]{2,1,0:T(8,128)(2,1)S(1)}) custom-call(bf16[8,256,2048]{2,1,0:T(8,128)(2,1)} %bitcast.233, bf16[256,2048]{1,0:T(8,128)(2,1)S(1)} %copy-done.4, f32[1,2048]{1,0:T(1,128)S(1)} %get-tuple-element.146.refs_2_.refs_3_), custom_call_target="tpu_custom_call" | custom-call | flops 10485760 | bytes 209715200 | tf_op jit(solution)/shard_map/plane_forward_1/pallas_call | solution.py:425
  355.3 13.6 %all-gather.19.cloned.1.call-done = bf16[2048,1536]{0,1:T(8,128)(2,1)} async-done(((bf16[512,1536]{0,1:T(8,128)(2,1)}), bf16[2048,1536]{0,1:T(8,128)(2,1)}) %all-gather.19.cloned.1.call-update) | async-done | bytes 6291472 | tf_op jit(solution)/shard_map/all_gather | solution.py:647
  368.9 17.7 %fusion.61 = f32[2048,1536]{0,1:T(8,128)S(1)} fusion(bf16[2048,2048]{1,0:T(8,128)(2,1)} %bitcast.219, bf16[2048,1536]{0,1:T(8,128)(2,1)} %all-gather.19.cloned.1.call-done), kind=kOutput, calls=%fused_computation.189 | convolution fusion | flops 12884901888 | bytes 27262976 | tf_op jit(solution)/shard_map/dot_general | solution.py:768
  386.7 4.6 copy-done.20
  393.4 39.0 %all-gather.21.cloned.1.call-done = bf16[768,2048]{1,0:T(8,128)(2,1)} async-done(((bf16[192,2048]{1,0:T(8,128)(2,1)}), bf16[768,2048]{1,0:T(8,128)(2,1)}) %all-gather.21.cloned.1.call-update) | async-done | bytes 3145744 | tf_op jit(solution)/shard_map/all_gather | solution.py:708
  432.4 10.8 %convolution_convert_fusion.2 = bf16[2048,2048]{1,0:T(8,128)(2,1)} fusion(bf16[2048,768]{0,1:T(8,128)(2,1)S(1)} %multiply_convert_fusion.1, bf16[768,2048]{1,0:T(8,128)(2,1)} %all-gather.21.cloned.1.call-done), kind=kOutput, calls=%fused_computation.4 | convolution fusion | flops 6446645248 | bytes 14680064 | tf_op jit(solution)/shard_map/dot_general | solution.py:771
  443.3 46.9 %all-gather.23.cloned.1.call-done = bf16[2048,2048]{1,0:T(8,128)(2,1)} async-done(((bf16[256,2048]{1,0:T(8,128)(2,1)}), bf16[2048,2048]{1,0:T(8,128)(2,1)}) %all-gather.23.cloned.1.call-update) | async-done | bytes 8388624 | tf_op jit(solution)/shard_map/all_gather | solution.py:109
  490.2 10.4 %convolution_convert_fusion.5 = bf16[768,2048]{1,0:T(8,128)(2,1)} fusion(bf16[2048,768]{0,1:T(8,128)(2,1)S(1)} %multiply_convert_fusion.1, bf16[2048,2048]{1,0:T(8,128)(2,1)} %all-gather.23.cloned.1.call-done), kind=kOutput, calls=%fused_computation.25 | convolution fusion | flops 6444023808 | bytes 14680064 | tf_op jit(solution)/shard_map/dot_general | solution.py:27
  500.6 17.9 %fusion.6 = (bf16[2048,768]{0,1:T(8,128)(2,1)S(1)}, bf16[2048,768]{0,1:T(8,128)(2,1)S(1)}) fusion(f32[2048,1536]{0,1:T(8,128)} %copy-done.20, bf16[2048,2048]{1,0:T(8,128)(2,1)} %all-gather.23.cloned.1.call-done, bf16[768,2048]{1,0:T(8,128)(2,1)} %all-gather.21.cloned.1.call-done), kind=kOutput, calls=%fused_computation.13 | convolution fusion | flops 6480199680 | bytes 30408704 | tf_op jit(solution)/shard_map/dot_general | solution.py:33
  520.2 17.3 %convolution_convert_fusion.4 = bf16[2048,1536]{1,0:T(8,128)(2,1)} fusion(bf16[2048,2048]{1,0:T(8,128)(2,1)} %bitcast.220, bf16[2048,768]{0,1:T(8,128)(2,1)S(1)} %get-tuple-element.127, bf16[2048,768]{0,1:T(8,128)(2,1)S(1)} %get-tuple-element.126), kind=kOutput, calls=%fused_computation.6 | convolution fusion | flops 12900630528 | bytes 20971520 | tf_op jit(solution)/shard_map/dot_general | solution.py:27
  537.5 18.7 %convolution_convert_fusion.1 = bf16[2048,2048]{1,0:T(8,128)(2,1)} fusion(bf16[2048,1536]{0,1:T(8,128)(2,1)} %all-gather.19.cloned.1.call-done, bf16[2048,768]{0,1:T(8,128)(2,1)} %copy-done.70, bf16[2048,768]{0,1:T(8,128)(2,1)S(1)} %get-tuple-element.126), kind=kOutput, calls=%fused_computation.3 | convolution fusion | flops 12901679104 | bytes 20971520 | tf_op jit(solution)/shard_map/dot_general | solution.py:33
  565.6 75.3 %plane_back_2.1 = (f32[256,2048]{1,0:T(8,128)S(1)}, f32[8,2048]{1,0:T(8,128)S(1)}, bf16[8,256,2048]{2,1,0:T(8,128)(2,1)S(1)}) custom-call(bf16[8,256,2048]{2,1,0:T(8,128)(2,1)} %bitcast.232, f32[256,2048]{1,0:T(8,128)S(1)} %copy-done.6, bf16[256,2048]{1,0:T(8,128)(2,1)S(1)} %copy-done.7, f32[1,2048]{1,0:T(1,128)S(1)} %copy-done.12), custom_call_target="tpu_custom_call" | custom-call | flops 10485760 | bytes 209715200 | tf_op jit(solution)/shard_map/plane_back_2/pallas_call | solution.py:425
  641.0 13.1 %fusion.13 = (bf16[2,1024,320]{2,1,0:T(8,128)(2,1)}, f32[2,1024,320]{2,1,0:T(8,128)S(1)}) fusion(f32[2,1024,320]{2,1,0:T(8,128)} %bitcast.224, f32[2,1024,320]{2,1,0:T(8,128)} %get-tuple-element.121, bf16[2,1024,2048]{2,1,0:T(8,128)(2,1)S(1)} %bitcast.215, bf16[2560,2048]{1,0:T(8,128)(2,1)} %all-gather.17.cloned.1.call-done, s32[]{:T(128)S(6)} %select_n.156), kind=kOutput, calls=%fused_computation.34 | convolution fusion | flops 2699427840 | bytes 19922948 | tf_op jit(solution)/shard_map/dot_general | solution.py:33
  654.1 6.4 scan_back.1
  662.1 14.2 %all-gather.1 = f32[8,2,320]{2,1,0:T(2,128)S(1)} all-gather(f32[2,2,320]{2,1,0:T(2,128)S(1)} %copy.148), channel_id=3, replica_groups=mesh['x'=2,'l'=4,'y'=2,'c'=2] {'l'}, dimensions={0}, use_global_device_ids=true | all-gather | bytes 25600 | tf_op jit(solution)/shard_map/all_gather | solution.py:794
  678.4 15.5 %multiply_reduce_fusion = (f32[320]{0:T(512)S(1)}, f32[2,1024,320]{2,1,0:T(8,128)S(1)}, f32[2,1024,320]{2,1,0:T(8,128)S(1)}) fusion(f32[2,1024,320]{2,1,0:T(8,128)} %copy.138, f32[320]{0:T(512)S(1)} %copy-done.57, f32[2,1024]{1,0:T(2,128)S(1)} %copy-done.35, f32[2,1023,320]{2,1,0:T(8,128)} %bitcast.223, f32[2,1,320]{2,1,0:T(1,128)S(1)} %broadcast_select_fusion.1, ...), kind=kLoop, calls=%fused_computation.43 | loop fusion | flops 26869440 | bytes 28876544 | tf_op jit(solution)/shard_map/transpose(jvp())/reduce_sum | solution.py:98
  693.9 10.5 %fusion.14 = (f32[2,1024,320]{2,1,0:T(8,128)S(1)}, f32[2,1024,320]{2,1,0:T(8,128)S(1)}) fusion(f32[2,1024,320]{2,1,0:T(8,128)S(1)} %get-tuple-element.114, f32[320]{0:T(512)S(1)} %copy-done.53, pred[2,1024]{1,0:T(4,128)(4,1)S(1)} %copy-done.42, f32[2,1024,320]{2,1,0:T(8,128)S(1)} %copy-done.16, f32[320]{0:T(512)S(1)} %copy-done.55, ...), kind=kLoop, calls=%fused_computation.35 | loop fusion | flops 22282240 | bytes 26251264 | tf_op jit(solution)/shard_map/transpose(jvp())/mul | solution.py:97
  705.5 4.9 copy.152
  710.3 4.3 reshape.357
  720.5 5.6 copy.154
  726.1 11.1 %multiply_reduce_fusion.1 = (bf16[320]{0:T(512)(128)(2,1)S(1)}, bf16[320]{0:T(512)(128)(2,1)S(1)}, bf16[320]{0:T(512)(128)(2,1)S(1)}, bf16[320]{0:T(512)(128)(2,...) fusion(f32[2,1027,320]{2,1,0:T(8,128)} %maximum_convert_fusion, f32[2,1024]{1,0:T(2,128)S(1)} %copy-done.37, ...), kind=kLoop, calls=%fused_computation.44 | loop fusion | flops 17693120 | bytes 23626624 | tf_op jit(solution)/shard_map/reduce_sum | solution.py:822
  738.3 4.4 collective-permute-start.1
  748.1 5.4 convolution_convert_fusion.7
  754.3 3.7 concatenate.55
  762.0 10.9 %convolution_convert_fusion.6 = bf16[2048,640]{1,0:T(8,128)(2,1)} fusion(bf16[2048,2048]{1,0:T(8,128)(2,1)} %all-gather.13.cloned.1.call-done, bf16[2048,320]{1,0:T(8,128)(2,1)S(1)} %bitcast.248, bf16[2048,320]{1,0:T(8,128)(2,1)S(1)} %bitcast.267), kind=kOutput, calls=%fused_computation.26 | convolution fusion | flops 5375262720 | bytes 13631488 | tf_op jit(solution)/shard_map/dot_general | solution.py:27
  772.9 9.0 convolution_convert_fusion
  781.9 191.4 %tail.1 = (f32[256,2048]{1,0:T(8,128)}, bf16[2,4,128,640]{3,2,1,0:T(8,128)(2,1)}, bf16[160,2432]{1,0:T(8,128)(2,1)}, bf16[2,4,128,1536]{3,2,1,0:T(8,128)(2,1)}, ...) custom-call(bf16[8,256,2048]{2,1,0:T(8,128)(2,1)} %bitcast.231, bf16[256,2048]{1,0:T(8,128)(2,1)} %refs_1_.3, ...), custom_call_target="tpu_custom_call" | custom-call | flops 10485760 | bytes 209715200 | tf_op jit(solution)/shard_map/tail/pallas_call | solution.py:609
  983.9 3.5 copy.161
  987.5 6.2 copy.162
  993.6 6.7 copy.166
  (280 shorter events, 106.4 us)
Async XLA Ops:
  7.2 73.8 %copy-start = (bf16[384,2048]{1,0:T(8,128)(2,1)S(1)}, bf16[384,2048]{1,0:T(8,128)(2,1)}, u32[]{:S(2)}) copy-start(bf16[384,2048]{1,0:T(8,128)(2,1)} %param.24) | copy-start | bytes 4718596
  7.2 113.0 %all-gather.11.cloned.1.call-start = ((), (), s32[]{:S(2)}) async-start(), calls=%async_computation.5 | async-start | bytes 2088960 | tf_op jit(solution)/shard_map/all_gather | solution.py:684
  11.5 112.2 %all-gather.15.cloned.1.call-start = ((), (), s32[]{:S(2)}) async-start(), calls=%async_computation.7 | async-start | bytes 3276800 | tf_op jit(solution)/shard_map/all_gather | solution.py:647
  13.4 15.9 %copy-start.67 = (bf16[128]{0:T(256)(128)(2,1)S(1)}, bf16[128]{0:T(256)(128)(2,1)}, u32[]{:S(2)}) copy-start(bf16[128]{0:T(256)(128)(2,1)} %param.22) | copy-start | bytes 772
  13.4 15.9 %copy-start.68 = (bf16[128]{0:T(256)(128)(2,1)S(1)}, bf16[128]{0:T(256)(128)(2,1)}, u32[]{:S(2)}) copy-start(bf16[128]{0:T(256)(128)(2,1)} %param.15) | copy-start | bytes 772
  13.4 34.0 %copy-start.4 = (bf16[256,2048]{1,0:T(8,128)(2,1)S(1)}, bf16[256,2048]{1,0:T(8,128)(2,1)}, u32[]{:S(2)}) copy-start(bf16[256,2048]{1,0:T(8,128)(2,1)} %refs_1_.3) | copy-start | bytes 3145732
  29.3 137.7 %all-gather.13.cloned.1.call-start = ((), (), s32[]{:S(2)}) async-start(), calls=%async_computation.6 | async-start | bytes 9437184 | tf_op jit(solution)/shard_map/all_gather | solution.py:109
  47.7 225.1 %copy-start.11 = (f32[1,2048]{1,0:T(1,128)}, f32[1,2048]{1,0:T(1,128)S(1)}, u32[]{:S(2)}) copy-start(f32[1,2048]{1,0:T(1,128)S(1)} %get-tuple-element.146.refs_2_.refs_3_) | copy-start | bytes 24580
  49.6 214.5 %all-gather.17.cloned.1.call-start = ((), (), s32[]{:S(2)}) async-start(), calls=%async_computation.8 | async-start | bytes 11141120 | tf_op jit(solution)/shard_map/all_gather | solution.py:703
  50.2 318.7 %all-gather.19.cloned.1.call-start = ((), (), s32[]{:S(2)}) async-start(), calls=%async_computation.9 | async-start | bytes 7864320 | tf_op jit(solution)/shard_map/all_gather | solution.py:647
  80.9 351.5 %all-gather.21.cloned.1.call-start = ((), (), s32[]{:S(2)}) async-start(), calls=%async_computation.10 | async-start | bytes 3932160 | tf_op jit(solution)/shard_map/all_gather | solution.py:708
  82.0 408.2 %all-gather.23.cloned.1.call-start = ((), (), s32[]{:S(2)}) async-start(), calls=%async_computation.11 | async-start | bytes 9437184 | tf_op jit(solution)/shard_map/all_gather | solution.py:109
  82.8 699.1 %reduce-scatter.8.cloned.1.call-start = ((), (), s32[]{:S(2)}) async-start(), calls=%async_computation.14 | async-start | bytes 3932160 | tf_op jit(solution)/shard_map/reduce_scatter | solution.py:782
  120.0 113.6 %copy-start.34 = (f32[2,1024]{1,0:T(2,128)}, f32[2,1024]{1,0:T(2,128)S(1)}, u32[]{:S(2)}) copy-start(f32[2,1024]{1,0:T(2,128)S(1)} %get-tuple-element.124) | copy-start | bytes 24580
  120.0 113.6 %copy-start.41 = (pred[2,1024]{1,0:T(4,128)(4,1)}, pred[2,1024]{1,0:T(4,128)(4,1)S(1)}, u32[]{:S(2)}) copy-start(pred[2,1024]{1,0:T(4,128)(4,1)S(1)} %get-tuple-element.125) | copy-start | bytes 6148
  120.2 113.4 %copy-start.36 = (f32[2,1024]{1,0:T(2,128)}, f32[2,1024]{1,0:T(2,128)S(1)}, u32[]{:S(2)}) copy-start(f32[2,1024]{1,0:T(2,128)S(1)} %get-tuple-element.122) | copy-start | bytes 24580
  120.2 113.4 %copy-start.38 = (f32[2,1024]{1,0:T(2,128)}, f32[2,1024]{1,0:T(2,128)S(1)}, u32[]{:S(2)}) copy-start(f32[2,1024]{1,0:T(2,128)S(1)} %get-tuple-element.123) | copy-start | bytes 24580
  121.3 54.5 %copy-start.62 = (bf16[320,1]{0,1:T(2,128)(2,1)}, bf16[320,1]{0,1:T(2,128)(2,1)S(1)}, u32[]{:S(2)}) copy-start(bf16[320,1]{0,1:T(2,128)(2,1)S(1)} %copy.172) | copy-start | bytes 1924
  123.6 110.1 %copy-start.44 = (f32[320]{0:T(512)}, f32[320]{0:T(512)S(1)}, u32[]{:S(2)}) copy-start(f32[320]{0:T(512)S(1)} %get-tuple-element.106) | copy-start | bytes 3844
  123.6 110.1 %copy-start.46 = (f32[320]{0:T(512)}, f32[320]{0:T(512)S(1)}, u32[]{:S(2)}) copy-start(f32[320]{0:T(512)S(1)} %get-tuple-element.107) | copy-start | bytes 3844
  123.6 110.1 %copy-start.48 = (f32[320]{0:T(512)}, f32[320]{0:T(512)S(1)}, u32[]{:S(2)}) copy-start(f32[320]{0:T(512)S(1)} %get-tuple-element.108) | copy-start | bytes 3844
  123.6 110.1 %copy-start.50 = (f32[320]{0:T(512)}, f32[320]{0:T(512)S(1)}, u32[]{:S(2)}) copy-start(f32[320]{0:T(512)S(1)} %get-tuple-element.109) | copy-start | bytes 3844
  123.6 110.1 %copy-start.58 = (f32[320]{0:T(512)}, f32[320]{0:T(512)S(1)}, u32[]{:S(2)}) copy-start(f32[320]{0:T(512)S(1)} %get-tuple-element.105) | copy-start | bytes 3844
  123.6 110.0 %copy-start.52 = (f32[320]{0:T(512)}, f32[320]{0:T(512)S(1)}, u32[]{:S(2)}) copy-start(f32[320]{0:T(512)S(1)} %fusion.46) | copy-start | bytes 3844
  181.3 11.7 %collective-permute-start = (bf16[2,3,320]{2,1,0:T(4,128)(2,1)S(1)}, bf16[2,3,320]{2,1,0:T(4,128)(2,1)S(1)}, u32[]{:S(2)}, u32[]{:S(2)}) collective-permute-start(bf16[2,3,320]{2,1,0:T(4,128)(2,1)S(1)} %slice.255), channel_id=1, source_target_pairs={{0,4},{4,8},{8,12},{1,5},{5,9},{9,13},{2,6},{6,10},{10,14},{3,7},{... | collective-permute-start | bytes 11528 | tf_op jit(solution)/shard_map/ppermute | solution.py:723
  184.7 49.0 %copy-start.54 = (f32[320]{0:T(512)}, f32[320]{0:T(512)S(1)}, u32[]{:S(2)}) copy-start(f32[320]{0:T(512)S(1)} %get-tuple-element.110) | copy-start | bytes 3844
  184.7 49.0 %copy-start.56 = (f32[320]{0:T(512)}, f32[320]{0:T(512)S(1)}, u32[]{:S(2)}) copy-start(f32[320]{0:T(512)S(1)} %get-tuple-element.111) | copy-start | bytes 3844
  185.8 22.9 %copy-start.29 = (bf16[320,320]{1,0:T(8,128)(2,1)}, bf16[320,320]{1,0:T(8,128)(2,1)S(1)}, u32[]{:S(2)}) copy-start(bf16[320,320]{1,0:T(8,128)(2,1)S(1)} %dynamic-slice.2) | copy-start | bytes 614404
  245.5 5.3 copy-start.2
  245.5 15.5 %copy-start.21 = (f32[2048,320]{1,0:T(8,128)S(1)}, f32[2048,320]{1,0:T(8,128)}, u32[]{:S(2)}) copy-start(f32[2048,320]{1,0:T(8,128)} %copy.142) | copy-start | bytes 7864324
  264.1 8.7 copy-start.24
  386.6 4.6 copy-start.20
  556.2 225.7 %reduce-scatter.6.cloned.1.call-start = ((), (), s32[]{:S(2)}) async-start(), calls=%async_computation.13 | async-start | bytes 7864320 | tf_op jit(solution)/shard_map/reduce_scatter | solution.py:783
  556.9 448.0 %reduce-scatter.4.cloned.1.call-start = ((), (), s32[]{:S(2)}) async-start(), calls=%async_computation.12 | async-start | bytes 9437184 | tf_op jit(solution)/shard_map/reduce_scatter | solution.py:113
  640.9 13.1 %copy-start.10 = (f32[256,2048]{1,0:T(8,128)}, f32[256,2048]{1,0:T(8,128)S(1)}, u32[]{:S(2)}) copy-start(f32[256,2048]{1,0:T(8,128)S(1)} %get-tuple-element.42.refs_2_) | copy-start | bytes 6291460
  640.9 13.1 %copy-start.13 = (f32[8,2048]{1,0:T(8,128)}, f32[8,2048]{1,0:T(8,128)S(1)}, u32[]{:S(2)}) copy-start(f32[8,2048]{1,0:T(8,128)S(1)} %get-tuple-element.43.refs_4_) | copy-start | bytes 196612
  640.9 13.1 %copy-start.14 = (bf16[8,256,2048]{2,1,0:T(8,128)(2,1)}, bf16[8,256,2048]{2,1,0:T(8,128)(2,1)S(1)}, u32[]{:S(2)}) copy-start(bf16[8,256,2048]{2,1,0:T(8,128)(2,1)S(1)} %get-tuple-element.39) | copy-start | bytes 25165828
  678.4 15.5 %copy-start.16 = (f32[2,1024,320]{2,1,0:T(8,128)S(1)}, f32[2,1024,320]{2,1,0:T(8,128)}, u32[]{:S(2)}) copy-start(f32[2,1024,320]{2,1,0:T(8,128)} %copy.139) | copy-start | bytes 7864324
  678.4 15.5 %copy-start.18 = (f32[2,1024,320]{2,1,0:T(8,128)S(1)}, f32[2,1024,320]{2,1,0:T(8,128)}, u32[]{:S(2)}) copy-start(f32[2,1024,320]{2,1,0:T(8,128)} %copy.138) | copy-start | bytes 7864324
  693.9 10.6 %copy-start.19 = (f32[2,1024,320]{2,1,0:T(8,128)}, f32[2,1024,320]{2,1,0:T(8,128)S(1)}, u32[]{:S(2)}) copy-start(f32[2,1024,320]{2,1,0:T(8,128)S(1)} %get-tuple-element.114) | copy-start | bytes 7864324
  720.5 5.6 copy-start.17
  738.3 22.3 %collective-permute-start.1 = (f32[2,3,320]{2,1,0:T(4,128)S(1)}, f32[2,3,320]{2,1,0:T(4,128)S(1)}, u32[]{:S(2)}, u32[]{:S(2)}) collective-permute-start(f32[2,3,320]{2,1,0:T(4,128)S(1)} %pad_add_fusion.1), channel_id=1, source_target_pairs={{4,0},{8,4},{12,8},{5,1},{9,5},{13,9},{6,2},{10,6},{14,10},{7,3},{... | collective-permute-start | bytes 23048 | tf_op jit(solution)/shard_map/ppermute | solution.py:826
  748.1 5.4 copy-start.63
  762.0 10.9 %copy-start.66 = (bf16[2048,640]{0,1:T(8,128)(2,1)S(1)}, bf16[2048,640]{0,1:T(8,128)(2,1)}, u32[]{:S(2)}) copy-start(bf16[2048,640]{0,1:T(8,128)(2,1)} %all-gather.15.cloned.1.call-done) | copy-start | bytes 7864324
  977.4 6.5 copy-start.27
  993.6 8.0 copy-start.33
  993.6 9.2 copy-start.32
  1005.0 4.6 copy-start.1
  (37 other events, 82.1 us)
Sparse Core Ops, SparseCore 0:
  11.6 42.5 all-gather.10
  56.4 52.3 all-gather.14
  111.3 55.6 all-gather.12
  169.1 86.9 all-gather.16
  257.5 111.3 all-gather.18
  370.3 62.0 all-gather.20
  434.3 55.8 all-gather.22
  556.3 59.4 reduce-scatter.7
  618.6 111.6 reduce-scatter.5
  733.6 71.6 reduce-scatter.3

commit v3 on v2

--- a/solution.py
+++ b/solution.py
@@ -33,72 +33,6 @@
     return lax.dot_general(
         left_in, matrix, (((1,), (1,)), ((), ())), preferred_element_type=F32
     )
-
-
-def scan_kernel(rows, backward, a_ref, b_ref, pa_ref, pb_ref, carry):
-    @pl.when(pl.program_id(1) == 0)
-    def _():
-        carry[0] = jnp.ones_like(carry[0])
-        carry[1] = jnp.zeros_like(carry[1])
-
-    place = lax.broadcasted_iota(jnp.int32, (8, a_ref.shape[-1]), 0)
-    tiles = rows // 8
-
-    def step(i, state):
-        before_a, before_b = state
-        tile = tiles - 1 - i if backward else i
-        at = pl.ds(pl.multiple_of(tile * 8, 8), 8)
-        a, b = a_ref[0, at, :], b_ref[0, at, :]
-        for gap in (1, 2, 4):
-            turn = 8 - gap if backward else gap
-            inside = place < 8 - gap if backward else place >= gap
-            near_a = jnp.where(inside, pltpu.roll(a, turn, 0), 1.0)
-            near_b = jnp.where(inside, pltpu.roll(b, turn, 0), 0.0)
-            b = b + a * near_b
-            a = a * near_a
-        b = b + a * before_b
-        a = a * before_a
-        pa_ref[0, at, :] = a
-        pb_ref[0, at, :] = b
-        last = 0 if backward else 7
-        return (
-            jnp.broadcast_to(a[last : last + 1], a.shape),
-            jnp.broadcast_to(b[last : last + 1], b.shape),
-        )
-
-    end = lax.fori_loop(0, tiles, step, (carry[0], carry[1]))
-    carry[0] = end[0]
-    carry[1] = end[1]
-
-
-def scan_pairs(a, b, backward):
-    runs, length, channels = a.shape
-    rows = 256
-    steps = length // rows
-    place = (lambda i, j: (i, steps - 1 - j, 0)) if backward else (lambda i, j: (i, j, 0))
-    spec = pl.BlockSpec((1, rows, channels), place)
-    return pl.pallas_call(
-        functools.partial(scan_kernel, rows, backward),
-        out_shape=[jax.ShapeDtypeStruct(a.shape, F32)] * 2,
-        grid=(runs, steps),
-        in_specs=[spec, spec],
-        out_specs=[spec, spec],
-        scratch_shapes=[pltpu.VMEM((2, 8, channels), F32)],
-        compiler_params=pltpu.CompilerParams(vmem_limit_bytes=16 << 20),
-        cost_estimate=pl.CostEstimate(
-            flops=20 * a.size, bytes_accessed=16 * a.size, transcendentals=0
-        ),
-        name="scan_back" if backward else "scan_fwd",
-    )(a, b)
-
-
-def gate_terms(pre_sum, decay_in, conv_out, fresh, keep, width):
-    recur_gate = jax.nn.sigmoid(pre_sum[..., :width])
-    input_gate = jax.nn.sigmoid(pre_sum[..., width:])
-    log_decay = -DECAY_RATE * jax.nn.softplus(-decay_in) * recur_gate
-    coefficient = jnp.exp(log_decay) * keep
-    scaling = jnp.where(fresh, 1.0, jnp.sqrt(-jnp.expm1(2.0 * log_decay)))
-    return (coefficient, scaling * input_gate * conv_out)
 
 
 def gated_product(first_in, second_in):
@@ -255,24 +189,26 @@
             at = pl.ds(pl.multiple_of(i * 16, 16), 16)
             self.own[at] = (self.own[at].astype(F32) + other[at].astype(F32)).astype(BF)
 
-    def rightward(self):
-        @pl.when(self.l < self.root)
-        def _():
-            @pl.when(self.l > 0)
-            def _():
-                self.to_right.wait_recv()
-                self.add(self.from_left)
-
+    def begin(self):
+        @pl.when(jnp.logical_and(self.l == 0, self.l < self.root))
+        def _():
             self.to_right.start()
 
-    def leftward(self):
-        @pl.when(self.l > self.root)
-        def _():
-            @pl.when(self.l < self.lines - 1)
-            def _():
-                self.to_left.wait_recv()
-                self.add(self.from_right)
-
+        @pl.when(jnp.logical_and(self.l == self.lines - 1, self.l > self.root))
+        def _():
+            self.to_left.start()
+
+    def through(self):
+        @pl.when(jnp.logical_and(self.l > 0, self.l < self.root))
+        def _():
+            self.to_right.wait_recv()
+            self.add(self.from_left)
+            self.to_right.start()
+
+        @pl.when(jnp.logical_and(self.l < self.lines - 1, self.l > self.root))
+        def _():
+            self.to_left.wait_recv()
+            self.add(self.from_right)
             self.to_left.start()
 
     def end(self):
@@ -488,24 +424,57 @@
     up_copies = deliver(lambda to: upz.at[to], up_all)
     down_copies = [wires.near(downz, down_all.at[x]), wires.far(downz, down_all.at[x], twin)]
     load_in.wait()
-    q = lines - 1
-    in_sums[q].rightward()
-    in_sums[lines - 1 - q].leftward()
+    load_chan.wait()
+
+    def pass_right(q):
+        one = in_sums[q]
+
+        @pl.when(jnp.logical_and(l > 0, l < q))
+        def _():
+            one.to_right.wait_recv()
+            one.add(one.from_left)
+            one.to_right.start()
+
+    def pass_left(q):
+        one = in_sums[q]
+
+        @pl.when(jnp.logical_and(l < lines - 1, l > q))
+        def _():
+            one.to_left.wait_recv()
+            one.add(one.from_right)
+            one.to_left.start()
+
+    def send_ends(q):
+        @pl.when(jnp.logical_and(l == 0, q > 0))
+        def _():
+            in_sums[q].to_right.start()
+
+        @pl.when(jnp.logical_and(l == lines - 1, q > 0))
+        def _():
+            in_sums[lines - 1 - q].to_left.start()
+
+    send_ends(lines - 1)
     total.first_side()
+    if lines > 2:
+        send_ends(lines - 2)
+    pass_right(lines - 1)
+    pass_left(0)
+    total.second_side()
+    for q in reversed(range(1, lines - 2)):
+        send_ends(q)
     for copy in down_copies + up_copies:
         copy.start()
-    total.second_side()
     for q in reversed(range(1, lines - 1)):
-        in_sums[q].rightward()
-        in_sums[lines - 1 - q].leftward()
+        pass_right(q)
+        pass_left(lines - 1 - q)
+    for one in chan_sums:
+        one.begin()
     gain_out[...] = jnp.zeros_like(gain_out)
     use = back_rows(base_ref, up_ref, gain_ref, out_ref, gain_out, None)
     for piece in range(cuts):
         total.finish(piece, use)
-    load_chan.wait()
     for one in chan_sums:
-        one.rightward()
-        one.leftward()
+        one.through()
     for q in range(lines):
         in_sums[q].end()
     rows = in_all.shape[2]
@@ -639,12 +608,745 @@
     )(partial.reshape(8, length, width), base, up, gain.reshape(1, width), other_gain, pieces, chan, upz, downz)
 
 
-def columns_in(weight, pieces):
-    rows = weight.shape[0]
-    pieces = pieces.reshape(rows, -1, 4, pieces.shape[-1])
-    sent = jnp.moveaxis(pieces, 2, 0)
-    got = lax.all_to_all(sent, ("y", "c"), split_axis=0, concat_axis=0, tiled=True)
-    return lax.all_gather(got.reshape(4 * rows, -1), "l", axis=0, tiled=True)
+class LineGather:
+    def __init__(self, wires, lines, blocks):
+        x, l, y, c = (lax.axis_index(name) for name in EVERY)
+        self.l, self.lines = l, lines
+        self.right, self.left = [], []
+        for d in range(lines - 1):
+            block = blocks.at[jnp.maximum(l - d, 0)]
+            self.right.append(wires.far(block, block, (x, l + 1, y, c)))
+            block = blocks.at[jnp.minimum(l + d, lines - 1)]
+            self.left.append(wires.far(block, block, (x, l - 1, y, c)))
+
+    def step(self, d):
+        l, last = self.l, self.lines - 1
+
+        @pl.when(l >= d)
+        def _():
+            if d > 0:
+                self.right[d - 1].wait_recv()
+            if d < last:
+
+                @pl.when(l < last)
+                def _():
+                    self.right[d].start()
+
+        @pl.when(l + d <= last)
+        def _():
+            if d > 0:
+                self.left[d - 1].wait_recv()
+            if d < last:
+
+                @pl.when(l > 0)
+                def _():
+                    self.left[d].start()
+
+    def drain(self):
+        l, last = self.l, self.lines - 1
+        for d in range(last):
+
+            @pl.when(jnp.logical_and(l >= d, l < last))
+            def _():
+                self.right[d].wait_send()
+
+            @pl.when(jnp.logical_and(l + d <= last, l > 0))
+            def _():
+                self.left[d].wait_send()
+
+
+class FromRoot:
+    def __init__(self, wires, lines, source, target, i, per):
+        x, l, y, c = (lax.axis_index(name) for name in EVERY)
+        k = 2 * y + c
+        s = 4 * l + k
+        self.l, self.lines = l, lines
+        wanted = (4 * x + k) * per + i
+        self.root = wanted // 4
+        mine = jnp.logical_and(s // (4 * per) == x, lax.rem(s, per) == i)
+        goal = lax.rem(s // per, 4)
+        self.leaves = jnp.logical_and(mine, goal != k)
+        self.stays = jnp.logical_and(mine, goal == k)
+        self.comes = jnp.logical_and(self.root == l, lax.rem(wanted, 4) != k)
+        self.far = wires.far(source, target.at[i], (x, l, goal // 2, lax.rem(goal, 2)))
+        self.near = wires.near(source, target.at[i])
+        self.right = wires.far(target.at[i], target.at[i], (x, l + 1, y, c))
+        self.left = wires.far(target.at[i], target.at[i], (x, l - 1, y, c))
+
+    def start(self):
+        @pl.when(self.leaves)
+        def _():
+            self.far.start()
+
+        @pl.when(self.stays)
+        def _():
+            self.near.start()
+
+    def onward(self):
+        l, root, last = self.l, self.root, self.lines - 1
+
+        @pl.when(jnp.logical_and(l >= root, l < last))
+        def _():
+            self.right.start()
+
+        @pl.when(jnp.logical_and(l <= root, l > 0))
+        def _():
+            self.left.start()
+
+    def from_owner(self):
+        @pl.when(self.stays)
+        def _():
+            self.near.wait()
+
+        @pl.when(self.comes)
+        def _():
+            self.far.wait_recv()
+
+        @pl.when(self.l == self.root)
+        def _():
+            self.onward()
+
+    def from_line(self):
+        @pl.when(self.l > self.root)
+        def _():
+            self.right.wait_recv()
+            self.onward()
+
+        @pl.when(self.l < self.root)
+        def _():
+            self.left.wait_recv()
+            self.onward()
+
+    def drain(self):
+        l, root, last = self.l, self.root, self.lines - 1
+
+        @pl.when(self.leaves)
+        def _():
+            self.far.wait_send()
+
+        @pl.when(jnp.logical_and(l >= root, l < last))
+        def _():
+            self.right.wait_send()
+
+        @pl.when(jnp.logical_and(l <= root, l > 0))
+        def _():
+            self.left.wait_send()
+
+
+def start_kernel(lines, cuts, *refs):
+    (tok, mix, up, small, out, tiny) = refs[:6]
+    (tok_all, halo, mix_all, up_all, small_all, out_all, tiny_all) = refs[6:13]
+    send_sems, recv_sems = refs[13:]
+    me, core, side_a, side_b = sides()
+    x, l, y, c = me
+    k = 2 * y + c
+    other_y, cross, twin = (x, l, 1 - y, c), (x, l, 1 - y, 1 - c), (1 - x, l, y, c)
+    mates = [core, other_y, cross]
+    others = [(x, lax.rem(l + d, lines), y, c) for d in range(1, lines)]
+    per = small_all.shape[0]
+    wires = Wires(send_sems, recv_sems)
+    greet(mates + [twin] + others)
+
+    def exchange(source, target):
+        copies = [wires.near(source.at[k], target.at[k])]
+        for at in mates:
+            copies.append(wires.far(source.at[2 * at[2] + at[3]], target.at[k], at))
+        return copies
+
+    mix_swap = exchange(mix, mix_all.at[l])
+    up_swap = exchange(up, up_all)
+    spread = PlaneGather(wires, tok, tok_all, cuts)
+    walk = LineGather(wires, lines, mix_all)
+    roots = []
+    for i in range(per):
+        roots.append(FromRoot(wires, lines, small, small_all, i, per))
+        roots.append(FromRoot(wires, lines, out, out_all, i, per))
+    tiny_own = wires.near(tiny, tiny_all.at[x, c, y, l])
+    tiny_line = [wires.far(tiny, tiny_all.at[x, c, y, l], at) for at in others]
+    tiny_steps = [
+        wires.far(tiny_all.at[x, c, y], tiny_all.at[x, c, y], other_y),
+        wires.far(tiny_all.at[x, c], tiny_all.at[x, c], core),
+        wires.far(tiny_all.at[x], tiny_all.at[x], twin),
+    ]
+    length = tok.shape[0]
+    edge = pl.ds(length - 8, 8)
+    halo_far = [
+        wires.far(tok_all.at[4 * run + 3, edge], halo.at[run], (x, l + 1, y, c))
+        for run in range(2)
+    ]
+    halo_near = [wires.near(tok.at[edge], halo.at[run]) for run in range(2)]
+
+    for copy in mix_swap + [tiny_own] + tiny_line:
+        copy.start()
+    for piece in range(cuts):
+        spread.start(piece)
+    for one in roots:
+        one.start()
+    for copy in up_swap:
+        copy.start()
+    for copy in mix_swap:
+        copy.wait()
+    walk.step(0)
+    for one in roots[:2]:
+        one.from_owner()
+    for copy in [tiny_own] + tiny_line:
+        copy.wait()
+    for copy in tiny_steps[:2]:
+        copy.start()
+        copy.wait()
+    walk.step(1)
+    for one in roots[2:]:
+        one.from_owner()
+    tiny_steps[2].start()
+    tiny_steps[2].wait()
+    for d in range(2, lines - 1):
+        walk.step(d)
+    spread.forward("a", ("ab", "ac"))
+    for one in roots[:2]:
+        one.from_line()
+    if lines > 2:
+        walk.step(lines - 1)
+    spread.forward("b", ("bc",))
+    for one in roots[2:]:
+        one.from_line()
+    spread.forward("ab", ("dc",))
+    spread.finish()
+
+    @pl.when(l < lines - 1)
+    def _():
+        for copy in halo_far:
+            copy.start()
+
+    @pl.when(l == 0)
+    def _():
+        for copy in halo_near:
+            copy.start()
+            copy.wait()
+
+    for copy in up_swap:
+        copy.wait()
+
+    @pl.when(l > 0)
+    def _():
+        for copy in halo_far:
+            copy.wait_recv()
+
+    @pl.when(l < lines - 1)
+    def _():
+        for copy in halo_far:
+            copy.wait_send()
+
+    walk.drain()
+    for one in roots:
+        one.drain()
+
+
+def spread_inputs(tok, mix, up, small, out, tiny, lines, per):
+    length, width = tok.shape
+    cuts = 2
+    vmem, left = pl.BlockSpec(memory_space=pltpu.VMEM), pl.BlockSpec(memory_space=pl.ANY)
+    sems = 8 + cuts * 8 + 2 * lines + 2 * per * 4 + lines + 1 + 3 + 4
+    return pl.pallas_call(
+        functools.partial(start_kernel, lines, cuts),
+        out_shape=[
+            jax.ShapeDtypeStruct((8, length, width), BF),
+            jax.ShapeDtypeStruct((2, 8, width), BF),
+            jax.ShapeDtypeStruct((lines,) + mix.shape, BF),
+            jax.ShapeDtypeStruct(up.shape, BF),
+            jax.ShapeDtypeStruct((per,) + small.shape, BF),
+            jax.ShapeDtypeStruct((per,) + out.shape, BF),
+            jax.ShapeDtypeStruct((2, 2, 2, lines) + tiny.shape, F32),
+        ],
+        in_specs=[left] * 5 + [vmem],
+        out_specs=[left] * 6 + [vmem],
+        scratch_shapes=[
+            pltpu.SemaphoreType.DMA((sems,)),
+            pltpu.SemaphoreType.DMA((sems,)),
+        ],
+        compiler_params=pltpu.CompilerParams(
+            collective_id=4, has_side_effects=True, vmem_limit_bytes=16 << 20
+        ),
+        cost_estimate=pl.CostEstimate(
+            flops=20 * tok.size, bytes_accessed=400 * tok.size, transcendentals=0
+        ),
+        name="spread",
+    )(tok, mix, up, small, out, tiny)
+
+
+def gelu_parts(value):
+    slope = 0.7978845608028654
+    bend = jnp.tanh(slope * (value + 0.044715 * value * value * value))
+    gelu = 0.5 * value * (1.0 + bend)
+    inner = slope * (1.0 + 0.134145 * value * value)
+    return gelu, 0.5 * (1.0 + bend) + 0.5 * value * (1.0 - bend * bend) * inner
+
+
+def recur_parts(conv_out, chan, gate_ref, keep):
+    pre = jnp.dot(conv_out, gate_ref[...], preferred_element_type=F32) + chan[5:6]
+    recur = jax.nn.sigmoid(pre)
+    log_decay = chan[7:8] * recur
+    decayed = jnp.exp(log_decay)
+    twice = -2.0 * log_decay
+    return recur, decayed, decayed * keep, twice
+
+
+def below_one(decayed, twice):
+    series = 1.0 / 5040.0
+    for term in (-1.0 / 720.0, 1.0 / 120.0, -1.0 / 24.0, 1.0 / 6.0, -0.5, 1.0):
+        series = series * twice + term
+    return jnp.where(twice < 0.5, twice * series, 1.0 - decayed * decayed)
+
+
+def scan_tiles(rows, backward, first, second, out_first, out_second, carry):
+    channels = first.shape[-1]
+    where = lax.broadcasted_iota(jnp.int32, (8, channels), 0)
+    tiles = rows // 8
+
+    def step(i, state):
+        before_a, before_b = state
+        tile = tiles - 1 - i if backward else i
+        at = pl.ds(pl.multiple_of(tile * 8, 8), 8)
+        a, b = first[at], second[at]
+        for gap in (1, 2, 4):
+            turn = 8 - gap if backward else gap
+            inside = where < 8 - gap if backward else where >= gap
+            near_a = jnp.where(inside, pltpu.roll(a, turn, 0), 1.0)
+            near_b = jnp.where(inside, pltpu.roll(b, turn, 0), 0.0)
+            b = b + a * near_b
+            a = a * near_a
+        b = b + a * before_b
+        a = a * before_a
+        out_first[at] = a
+        out_second[at] = b
+        last = 0 if backward else 7
+        return (
+            jnp.broadcast_to(a[last : last + 1], a.shape),
+            jnp.broadcast_to(b[last : last + 1], b.shape),
+        )
+
+    end = lax.fori_loop(0, tiles, step, (carry[0], carry[1]), unroll=4)
+    carry[0] = end[0]
+    carry[1] = end[1]
+
+
+def mix_forward_kernel(*refs):
+    (tok, halo, weight, gain, chan_ref, gate_r, gate_i, fac) = refs[:8]
+    (normed, branch, conv_in, conv_out, pa, pb, ends) = refs[8:15]
+    (rows_in, coef, drive, carry) = refs[15:]
+    length, own = branch.shape
+    chunk = pl.program_id(1)
+    chan = chan_ref[...]
+
+    def norm_of(values):
+        values = values.astype(F32)
+        scale = lax.rsqrt(jnp.mean(values * values, axis=-1, keepdims=True) + EPSILON)
+        return (values * scale * gain[...]).astype(BF)
+
+    @pl.when(chunk == 0)
+    def _():
+        carry[0] = jnp.ones_like(carry[0])
+        carry[1] = jnp.zeros_like(carry[1])
+        edge = jnp.dot(norm_of(halo[0]), weight[...], preferred_element_type=F32)
+        rows_in[8:16] = pltpu.roll(edge, own, 1)[:, :own].astype(BF).astype(F32)
+        rows_in[0:8] = jnp.zeros((8, own), F32)
+        conv_in[0, 0:16] = rows_in[0:16].astype(BF)
+
+    @pl.when(chunk > 0)
+    def _():
+        rows_in[0:16] = rows_in[length : length + 16]
+
+    @pl.loop(0, length // 16)
+    def _(i):
+        at = pl.ds(pl.multiple_of(i * 16, 16), 16)
+        normed[0, at] = norm_of(tok[0, at])
+
+    projected = jnp.dot(normed[0], weight[...], preferred_element_type=F32)
+    branch[...] = projected[:, :own]
+    rounded = pltpu.roll(projected, own, 1)[:, :own].astype(BF)
+    conv_in[0, pl.ds(pl.multiple_of(16 + chunk * length, 16), length)] = rounded
+    rows_in[16 : 16 + length] = rounded.astype(F32)
+    window = rows_in[8 : 16 + length]
+    total = chan[4:5] + chan[0:1] * window[8:]
+    for gap in range(1, 4):
+        total = total + chan[gap : gap + 1] * pltpu.roll(window, gap, 0)[8:] * fac[:, gap - 1 : gap]
+    low = total.astype(BF)
+    conv_out[...] = low
+    keep = fac[:, 0:1]
+    _, decayed, coefficient, twice = recur_parts(low, chan, gate_r, keep)
+    coef[...] = coefficient
+    input_gate = jax.nn.sigmoid(
+        jnp.dot(low, gate_i[...], preferred_element_type=F32) + chan[6:7]
+    )
+    scaling = jnp.where(keep == 0.0, 1.0, jnp.sqrt(below_one(decayed, twice)))
+    drive[...] = scaling * input_gate * low.astype(F32)
+    scan_tiles(length, False, coef, drive, pa, pb, carry)
+    ends[0, 0:8] = carry[0]
+    ends[0, 8:16] = carry[1]
+
+
+def mix_state_kernel(*refs):
+    (res, weight, branch, pa, pb, state_in, conv_out, chan_ref, gate_r, fac) = refs[:10]
+    (branch_grad, ta, tb, ends) = refs[10:14]
+    (coef, grad, carry, first_coef) = refs[14:]
+    length, own = branch.shape
+    chan = chan_ref[...]
+    turn = pl.program_id(1)
+
+    @pl.when(turn == 0)
+    def _():
+        carry[0] = jnp.ones_like(carry[0])
+        carry[1] = jnp.zeros_like(carry[1])
+        first_coef[...] = jnp.ones_like(first_coef)
+
+    mixed_grad = lax.dot_general(
+        res[...], weight[...], (((1,), (1,)), ((), ())), preferred_element_type=F32
+    )
+    state = pb[...] + pa[...] * state_in[0, 0:1]
+    gelu, slope = gelu_parts(branch[...])
+    branch_grad[...] = (mixed_grad * state * slope).astype(BF)
+    grad[...] = mixed_grad * gelu
+    _, _, coefficient, _ = recur_parts(conv_out[...], chan, gate_r, fac[:, 0:1])
+    row = lax.broadcasted_iota(jnp.int32, (length, own), 0)
+    shifted = pltpu.roll(coefficient, length - 1, 0)
+    coef[...] = jnp.where(row == length - 1, first_coef[0:1], shifted)
+    first = jnp.broadcast_to(coefficient[0:1], first_coef.shape)
+    first_coef[...] = first
+    scan_tiles(length, True, coef, grad, ta, tb, carry)
+    ends[0, 0:8] = first * carry[0]
+    ends[0, 8:16] = first * carry[1]
+
+
+def mix_gates_kernel(*refs):
+    (ta, tb, from_right, pa, pb, pa_before, pb_before, state_in) = refs[:8]
+    (conv_in, conv_out, branch_grad, chan_ref, gate_r, gate_i, fac) = refs[8:15]
+    (proj_grad, last_rows, edges, sums, gate_grad) = refs[15:20]
+    (after,) = refs[20:]
+    length, own = ta.shape
+    turn, turns = pl.program_id(1), pl.num_programs(1)
+    chunk = turns - 1 - turn
+    chan = chan_ref[...]
+
+    @pl.when(jnp.logical_and(turn == 0, pl.program_id(0) == 0))
+    def _():
+        sums[...] = jnp.zeros_like(sums)
+        gate_grad[...] = jnp.zeros_like(gate_grad)
+
+    @pl.when(turn == 0)
+    def _():
+        after[...] = jnp.zeros_like(after)
+
+    start = state_in[0, 0:1]
+    total = tb[...] + ta[...] * from_right[0, 0:1]
+    state = pb[...] + pa[...] * start
+    row = lax.broadcasted_iota(jnp.int32, (length, own), 0)
+    before = pb_before[7:8] + pa_before[7:8] * start
+    before = jnp.where(chunk == 0, start, before)
+    prev_state = jnp.where(row == 0, before, pltpu.roll(state, 1, 0))
+    keep = fac[:, 0:1]
+    low = conv_out[...]
+    conv = low.astype(F32)
+    recur, decayed, coefficient, twice = recur_parts(low, chan, gate_r, keep)
+    input_gate = jax.nn.sigmoid(
+        jnp.dot(low, gate_i[...], preferred_element_type=F32) + chan[6:7]
+    )
+    rest = below_one(decayed, twice)
+    fresh = keep == 0.0
+    scaling = jnp.where(fresh, 1.0, jnp.sqrt(rest))
+    gated = total * input_gate
+    by_scaling = jnp.where(fresh, 0.0, gated * conv * decayed * decayed * lax.rsqrt(rest))
+    decay_grad = total * prev_state * coefficient - by_scaling
+    recur_grad = (chan[7:8] * decay_grad * recur * (1.0 - recur)).astype(BF)
+    input_grad = (total * scaling * conv * input_gate * (1.0 - input_gate)).astype(BF)
+
+    def fold(values):
+        return jnp.sum(values.reshape(length // 8, 8, own), axis=0)
+
+    sums[5] += fold(recur_grad.astype(F32))
+    sums[6] += fold(input_grad.astype(F32))
+    sums[7] += fold(decay_grad * recur)
+    contract = (((0,), (0,)), ((), ()))
+    gate_grad[0] += lax.dot_general(low, recur_grad, contract, preferred_element_type=F32)
+    gate_grad[1] += lax.dot_general(low, input_grad, contract, preferred_element_type=F32)
+    across = (((1,), (1,)), ((), ()))
+    conv_grad = gated * scaling
+    conv_grad = conv_grad + lax.dot_general(
+        recur_grad, gate_r[...], across, preferred_element_type=F32
+    )
+    conv_grad = conv_grad + lax.dot_general(
+        input_grad, gate_i[...], across, preferred_element_type=F32
+    )
+    window = conv_in[0, pl.ds(pl.multiple_of(chunk * length, 16), length + 16)].astype(F32)[8:]
+    sums[4] += fold(conv_grad)
+    sums[0] += fold(conv_grad * window[8:])
+    conv_in_grad = chan[0:1] * conv_grad
+    edge_row = lax.broadcasted_iota(jnp.int32, (8, own), 0)
+    edge = jnp.zeros((8, own), F32)
+    for gap in range(1, 4):
+        masked = conv_grad * fac[:, gap - 1 : gap]
+        sums[gap] += fold(masked * pltpu.roll(window, gap, 0)[8:])
+        moved = pltpu.roll(jnp.concatenate([masked, after[gap - 1]], axis=0), length + 8 - gap, 0)
+        conv_in_grad = conv_in_grad + chan[gap : gap + 1] * moved[:length]
+        head = masked[0:8]
+        after[gap - 1] = head
+        given = pltpu.roll(head, 3 - gap, 0)
+        given = jnp.where((edge_row >= 3 - gap) & (edge_row < 3), given, 0.0)
+        edge = edge + chan[gap : gap + 1] * given
+    edges[0] = edge
+
+    @pl.when(turn == 0)
+    def _():
+        last_rows[0] = conv_in_grad[length - 8 :]
+
+    proj_grad[:, :own] = branch_grad[...]
+    proj_grad[:, own:] = conv_in_grad.astype(BF)
+
+
+def line_kernel(lines, backward, ends, start, got, send_sems, recv_sems):
+    x, l, y, c = (lax.axis_index(name) for name in EVERY)
+    wires = Wires(send_sems, recv_sems)
+    others = [(x, lax.rem(l + d, lines), y, c) for d in range(1, lines)]
+    greet(others)
+    copies = [wires.far(ends, got.at[l], at) for at in others]
+    for copy in copies:
+        copy.start()
+    for copy in copies:
+        copy.wait()
+    for run in range(2):
+        value = jnp.zeros(start.shape[1:], F32)
+        order = reversed(range(1, lines)) if backward else range(lines - 1)
+        for other in order:
+            longer = got[other, run, 0:8] * value + got[other, run, 8:16]
+            reached = other > l if backward else other < l
+            value = jnp.where(reached, longer, value)
+        start[run] = value
+
+
+def line_start(ends, lines, backward, number):
+    vmem = pl.BlockSpec(memory_space=pltpu.VMEM)
+    own = ends.shape[-1]
+    return pl.pallas_call(
+        functools.partial(line_kernel, lines, backward),
+        out_shape=jax.ShapeDtypeStruct((2, 8, own), F32),
+        in_specs=[vmem],
+        out_specs=vmem,
+        scratch_shapes=[
+            pltpu.VMEM((lines,) + ends.shape, F32),
+            pltpu.SemaphoreType.DMA((lines,)),
+            pltpu.SemaphoreType.DMA((lines,)),
+        ],
+        compiler_params=pltpu.CompilerParams(
+            collective_id=number, has_side_effects=True, vmem_limit_bytes=8 << 20
+        ),
+        name=f"line_{number}",
+    )(ends)
+
+
+def mix_specs(run, length, own, backward):
+    steps = run // length
+
+    def turn(j):
+        return steps - 1 - j if backward else j
+
+    def rows(width):
+        return pl.BlockSpec((length, width), lambda i, j: (i * steps + turn(j), 0))
+
+    def slots(width):
+        return pl.BlockSpec((1, length, width), lambda i, j: (i * steps + turn(j), 0, 0))
+
+    def whole(*shape):
+        return pl.BlockSpec(shape, lambda i, j: (0,) * len(shape), pipeline_mode=pl.Buffered(1))
+
+    def held(*shape):
+        return pl.BlockSpec((1,) + shape, lambda i, j: (i,) + (0,) * len(shape))
+
+    return steps, rows, slots, whole, held
+
+
+def mix_forward(tok_all, halo, weight, gain, chan, gate_r, gate_i, fac):
+    slots_in, length, width = tok_all.shape
+    own, run = chan.shape[1], 4 * length
+    steps, rows, slots, whole, held = mix_specs(run, length, own, False)
+    flat = jax.ShapeDtypeStruct((2 * run, own), F32)
+    return pl.pallas_call(
+        mix_forward_kernel,
+        grid=(2, steps),
+        in_specs=[
+            slots(width),
+            held(8, width),
+            whole(width, 2 * own),
+            whole(1, width),
+            whole(8, own),
+            whole(own, own),
+            whole(own, own),
+            rows(fac.shape[1]),
+        ],
+        out_specs=[
+            slots(width),
+            rows(own),
+            held(16 + run, own),
+            rows(own),
+            rows(own),
+            rows(own),
+            held(16, own),
+        ],
+        out_shape=[
+            jax.ShapeDtypeStruct(tok_all.shape, BF),
+            flat,
+            jax.ShapeDtypeStruct((2, 16 + run, own), BF),
+            jax.ShapeDtypeStruct((2 * run, own), BF),
+            flat,
+            flat,
+            jax.ShapeDtypeStruct((2, 16, own), F32),
+        ],
+        scratch_shapes=[
+            pltpu.VMEM((16 + length, own), F32),
+            pltpu.VMEM((length, own), F32),
+            pltpu.VMEM((length, own), F32),
+            pltpu.VMEM((2, 8, own), F32),
+        ],
+        compiler_params=pltpu.CompilerParams(vmem_limit_bytes=40 << 20),
+        cost_estimate=pl.CostEstimate(
+            flops=4 * run * width * 2 * own, bytes_accessed=60 << 20, transcendentals=0
+        ),
+        name="mix_forward",
+    )(tok_all, halo, weight, gain.reshape(1, width), chan, gate_r, gate_i, fac)
+
+
+def mix_state(res, weight, branch, pa, pb, state_in, conv_out, chan, gate_r, fac, length):
+    own, width = weight.shape
+    run = res.shape[0] // 2
+    steps, rows, slots, whole, held = mix_specs(run, length, own, True)
+    flat = jax.ShapeDtypeStruct((2 * run, own), F32)
+    return pl.pallas_call(
+        mix_state_kernel,
+        grid=(2, steps),
+        in_specs=[
+            rows(width),
+            whole(own, width),
+            rows(own),
+            rows(own),
+            rows(own),
+            held(8, own),
+            rows(own),
+            whole(8, own),
+            whole(own, own),
+            rows(fac.shape[1]),
+        ],
+        out_specs=[rows(own), rows(own), rows(own), held(16, own)],
+        out_shape=[
+            jax.ShapeDtypeStruct((2 * run, own), BF),
+            flat,
+            flat,
+            jax.ShapeDtypeStruct((2, 16, own), F32),
+        ],
+        scratch_shapes=[
+            pltpu.VMEM((length, own), F32),
+            pltpu.VMEM((length, own), F32),
+            pltpu.VMEM((2, 8, own), F32),
+            pltpu.VMEM((8, own), F32),
+        ],
+        compiler_params=pltpu.CompilerParams(vmem_limit_bytes=40 << 20),
+        cost_estimate=pl.CostEstimate(
+            flops=4 * run * width * own, bytes_accessed=40 << 20, transcendentals=0
+        ),
+        name="mix_state",
+    )(res, weight, branch, pa, pb, state_in, conv_out, chan, gate_r, fac)
+
+
+def mix_gates(
+    ta, tb, from_right, pa, pb, state_in, conv_in, conv_out, branch_grad, chan, gate_r, gate_i, fac, length
+):
+    own = chan.shape[1]
+    run = ta.shape[0] // 2
+    steps, rows, slots, whole, held = mix_specs(run, length, own, True)
+    eights = length // 8
+    earlier = pl.BlockSpec(
+        (8, own), lambda i, j: (jnp.maximum((i * steps + steps - 1 - j) * eights - 1, 0), 0)
+    )
+    return pl.pallas_call(
+        mix_gates_kernel,
+        grid=(2, steps),
+        in_specs=[
+            rows(own),
+            rows(own),
+            held(8, own),
+            rows(own),
+            rows(own),
+            earlier,
+            earlier,
+            held(8, own),
+            held(16 + run, own),
+            rows(own),
+            rows(own),
+            whole(8, own),
+            whole(own, own),
+            whole(own, own),
+            rows(fac.shape[1]),
+        ],
+        out_specs=[
+            rows(2 * own),
+            held(8, own),
+            held(8, own),
+            pl.BlockSpec((8, 8, own), lambda i, j: (0, 0, 0)),
+            pl.BlockSpec((2, own, own), lambda i, j: (0, 0, 0)),
+        ],
+        out_shape=[
+            jax.ShapeDtypeStruct((2 * run, 2 * own), BF),
+            jax.ShapeDtypeStruct((2, 8, own), F32),
+            jax.ShapeDtypeStruct((2, 8, own), F32),
+            jax.ShapeDtypeStruct((8, 8, own), F32),
+            jax.ShapeDtypeStruct((2, own, own), F32),
+        ],
+        scratch_shapes=[pltpu.VMEM((3, 8, own), F32)],
+        compiler_params=pltpu.CompilerParams(vmem_limit_bytes=40 << 20),
+        cost_estimate=pl.CostEstimate(
+            flops=16 * run * own * own, bytes_accessed=40 << 20, transcendentals=0
+        ),
+        name="mix_gates",
+    )(ta, tb, from_right, pa, pb, pa, pb, state_in, conv_in, conv_out, branch_grad, chan, gate_r, gate_i, fac)
+
+
+def settle_kernel(lines, up_all, in_all, down_all, chan, up_out, in_out, down_out, out_out):
+    share = up_all.shape[-1] // (2 * lines)
+    own = in_all.shape[-1] // 2
+    ups = [[up_all[x, k].astype(F32) for k in range(4)] for x in range(2)]
+    for part in range(2 * lines):
+        at = slice(part * share, (part + 1) * share)
+        row = [ups[x][k][:, at] for k in range(4) for x in range(2)]
+        up_out[:, part * 8 * share : (part + 1) * 8 * share] = jnp.concatenate(row, axis=1)
+    for part in range(2):
+        at = slice(part * own, (part + 1) * own)
+        row = [in_all[x, k].astype(F32)[:, at] for x in range(2) for k in range(4)]
+        in_out[:, part * 8 * own : (part + 1) * 8 * own] = jnp.concatenate(row, axis=1)
+    down_out[...] = down_all[...].astype(F32)
+    out_out[...] = chan[:, : out_out.shape[1]].astype(F32)
+
+
+def settle(up_all, in_all, down_all, chan, owned, width, lines):
+    rows, share2 = up_all.shape[2], down_all.shape[0]
+    steps = 4 if not (rows % 64 or share2 % 64 or owned % 32) else 1
+    r, d, o = rows // steps, share2 // steps, owned // steps
+    wide, narrow = up_all.shape[-1], in_all.shape[-1]
+    shapes = [(rows, 8 * wide), (rows, 8 * narrow), (share2, width), (owned, width)]
+    return pl.pallas_call(
+        functools.partial(settle_kernel, lines),
+        grid=(steps,),
+        in_specs=[
+            pl.BlockSpec((2, 4, r, wide), lambda i: (0, 0, i, 0)),
+            pl.BlockSpec((2, 4, r, narrow), lambda i: (0, 0, i, 0)),
+            pl.BlockSpec((d, width), lambda i: (i, 0)),
+            pl.BlockSpec((o, chan.shape[1]), lambda i: (i, 0)),
+        ],
+        out_specs=[
+            pl.BlockSpec((n // steps, w), lambda i: (i, 0)) for n, w in shapes
+        ],
+        out_shape=[jax.ShapeDtypeStruct(one, F32) for one in shapes],
+        compiler_params=pltpu.CompilerParams(vmem_limit_bytes=40 << 20),
+        cost_estimate=pl.CostEstimate(
+            flops=0, bytes_accessed=6 * sum(a * b for a, b in shapes), transcendentals=0
+        ),
+        name="settle",
+    )(up_all, in_all, down_all, chan[:owned])
 
 
 def on_device(
@@ -679,159 +1381,124 @@
     share = mlp_out.shape[0] // 2
     rows = mix_in.shape[0]
 
-    gains = lax.all_gather(jnp.stack([mix_gain, mlp_gain]), SHARD, axis=1, tiled=True)
-    packed = jnp.concatenate([conv_par.T, gate_bias.T, decay[:, None], gate_w], axis=1)
-    packed = lax.all_gather(packed, SHARD, axis=0, tiled=True)
-    packed = lax.dynamic_slice_in_dim(packed, mine * own, own, 0)
-    ids_all = lax.all_gather(seg_ids, EVERY, axis=0, tiled=True).reshape(2, lines, run)
-
-    gain_one = gains[0].astype(F32)
-    gain_two = gains[1].astype(F32)
-    taps = packed[:, :5].T.astype(F32)
-    bias = packed[:, 5:7].T.astype(F32)
-    decay_own = packed[:, 7].astype(F32)
-    gates = packed[:, 8:].reshape(blocks, block_size, 2 * block_size)
-
-    inputs = tokens.astype(F32)
-    normed_one = norm_rows(inputs, gain_one).astype(BF)
-    all_one = plane_gather(normed_one)
-
+    per = owners // 8
     by_half = mix_in.reshape(rows, 2, 2, 4, own)
     by_half = lax.dynamic_index_in_dim(by_half, half, 2, keepdims=False)
-    in_matrix = columns_in(mix_in, by_half)
-    out_matrix = lax.dynamic_slice_in_dim(
-        lax.all_gather(out_proj, SHARD, axis=0, tiled=True), mine * own, own, 0
-    )
+    mix_sent = jnp.moveaxis(by_half, 2, 0).reshape(4, rows, 2 * own)
     by_half = mlp_in.reshape(rows, 2 * lines, 4, 2, share)
     by_half = lax.dynamic_index_in_dim(by_half, half, 3, keepdims=False)
-    up_matrix = columns_in(mlp_in, by_half)
-    down_matrix = lax.all_gather(
-        lax.dynamic_slice_in_dim(mlp_out, half * share, share, 0), "l", axis=0, tiled=True
+    up_sent = jnp.moveaxis(by_half, 2, 0).reshape(4, rows, 2 * lines * share)
+    small = jnp.concatenate([conv_par.T, gate_bias.T, decay[:, None], gate_w], axis=1)
+    used = small.shape[1]
+    small = jnp.pad(small, ((0, 0), (0, -used % 128)))
+    tiny = jnp.concatenate([mix_gain.astype(F32), mlp_gain.astype(F32), seg_ids.astype(F32)])
+    tiny = jnp.pad(tiny, (0, -tiny.shape[0] % 1024)).reshape(-1, 128)
+    tok_all, halo, in_matrix, up_rows, packed, out_matrix, tiny = spread_inputs(
+        tokens, mix_sent, up_sent, small, out_proj, tiny, lines, per
     )
     all_cot = plane_gather(cotangent)
-
-    projected = jnp.dot(all_one, in_matrix, preferred_element_type=F32)
-    branch = projected[:, :own].reshape(2, run, own)
-    conv_in = projected[:, own:].astype(BF).reshape(2, run, own)
+    tok_all, all_cot = lax.optimization_barrier((tok_all, all_cot))
+    in_matrix = in_matrix.reshape(-1, 2 * own)
+    out_matrix = out_matrix.reshape(own, width)
+    packed = packed.reshape(own, -1)
+    tiny = tiny.transpose(0, 3, 2, 1, 4, 5).reshape(2, owners, -1)
+    gain_one = tiny[0, :, :rows].reshape(-1)
+    gain_two = tiny[0, :, rows : 2 * rows].reshape(-1)
+    ids_all = tiny[:, :, 2 * rows : 2 * rows + length].reshape(2, lines, run).astype(jnp.int32)
+    decay_own = packed[:, 7].astype(F32)
+    chan = packed[:, :8].T.astype(F32)
+    chan = chan.at[7].set(-DECAY_RATE * jax.nn.softplus(-decay_own))
+    gates = packed[:, 8:used].reshape(blocks, block_size, 2, block_size)
+    gate_r, gate_i = (
+        lax.dynamic_update_slice(
+            jnp.pad(gates[0, :, side], ((0, own - block_size), (0, own - block_size))),
+            gates[1, :, side],
+            (block_size, block_size),
+        )
+        for side in range(2)
+    )
 
     ids = lax.dynamic_index_in_dim(ids_all, line, 1, keepdims=False)
     ids_before = lax.dynamic_index_in_dim(
         ids_all, jnp.maximum(line - 1, 0), 1, keepdims=False
     )[:, -3:]
-    ids_before = jnp.where(line > 0, ids_before, -1)
-    route = [(i, i + 1) for i in range(lines - 1)]
-    rows_before = lax.ppermute(conv_in[:, -3:], "l", route)
     extended = jnp.concatenate([ids_before, ids], axis=1)
-    places = (half * 0 + line * run + lax.broadcasted_iota(jnp.int32, (2, run), 1)) % SEQ_LEN
+    places = (line * run + lax.broadcasted_iota(jnp.int32, (2, run), 1)) % SEQ_LEN
     fresh = (extended[:, 3:] != extended[:, 2:-1]) | (places == 0)
     keep = 1.0 - fresh.astype(F32)
-    before_start = jnp.concatenate(
+    same = jnp.concatenate(
         [(extended[:, 1:3] == extended[:, 0:2]).astype(F32), keep], axis=1
     )
-    padded_in = jnp.concatenate([rows_before, conv_in], axis=1).astype(F32)
-    factors = [None]
-    factor = jnp.ones((2, run), F32)
-    conv_sum = taps[4] + taps[0] * padded_in[:, 3:]
-    for offset in range(1, 4):
-        factor = factor * before_start[:, 3 - offset : 3 - offset + run]
-        factors.append(factor[:, :, None])
-        conv_sum = (
-            conv_sum
-            + taps[offset] * padded_in[:, 3 - offset : 3 - offset + run] * factors[offset]
-        )
-    conv_out = conv_sum.astype(BF)
-    conv_blocks = conv_out.reshape(plane, blocks, block_size)
-    pre_sum = jnp.einsum("tbj,bjk->btk", conv_blocks, gates, preferred_element_type=F32)
-    recur_pre = jnp.moveaxis(pre_sum[:, :, :block_size], 0, 1).reshape(2, run, own) + bias[0]
-    input_pre = jnp.moveaxis(pre_sum[:, :, block_size:], 0, 1).reshape(2, run, own) + bias[1]
-    pre_sum = jnp.concatenate([recur_pre, input_pre], axis=-1)
-    (coefficient, drive), gate_pull = jax.vjp(
-        lambda pre_in, decay_in, conv_value: gate_terms(
-            pre_in, decay_in, conv_value, fresh[:, :, None], keep[:, :, None], own
-        ),
-        pre_sum,
-        decay_own,
-        conv_out.astype(F32),
-    )
-    prefix_coef, local_state = scan_pairs(coefficient, drive, False)
-    ends = lax.all_gather(
-        jnp.stack([prefix_coef[:, -1], local_state[:, -1]]), "l", axis=0, tiled=False
-    )
-    state_in = jnp.zeros((2, own), F32)
-    for other in range(lines - 1):
-        longer = ends[other, 0] * state_in + ends[other, 1]
-        state_in = jnp.where(other < line, longer, state_in)
-    state = local_state + prefix_coef * state_in[:, None]
-    mixed = (state * jax.nn.gelu(branch)).astype(BF).reshape(plane, own)
+    fac = [keep]
+    for offset in range(2, 4):
+        fac.append(fac[-1] * same[:, 3 - offset : 3 - offset + run])
+    fac = jnp.stack(fac + [keep], axis=-1).reshape(plane, 4)
+    all_one, branch, conv_in, conv_out, pa, pb, ends = mix_forward(
+        tok_all, halo, in_matrix, gain_one, chan, gate_r, gate_i, fac
+    )
+    all_one = all_one.reshape(plane, width)
+    state_in = line_start(ends, lines, False, 5)
+    up_rows = up_rows.reshape(4 * rows, 2, -1)
+    first_up = lax.all_gather(up_rows[:, 0], "l", axis=0, tiled=True)
+    later, down_rows, state_in = lax.optimization_barrier((up_rows[:, 1], mlp_out, state_in))
+    second_up = lax.all_gather(later, "l", axis=0, tiled=True)
+    down_matrix = lax.all_gather(
+        lax.dynamic_slice_in_dim(down_rows, half * share, share, 0), "l", axis=0, tiled=True
+    )
+    state = pb.reshape(2, run, own) + pa.reshape(2, run, own) * state_in[:, :1]
+    mixed = (state * jax.nn.gelu(branch.reshape(2, run, own))).astype(BF).reshape(plane, own)
     partial = jnp.dot(mixed, out_matrix, preferred_element_type=F32).astype(BF)
     residual, all_two = plane_sum(partial, tokens, None, gain_two, 1)
-    hidden = jnp.dot(all_two, up_matrix, preferred_element_type=F32)
-    part = ff // 8
-    activated = gated_product(hidden[:, :part], hidden[:, part:]).astype(BF)
+    gate_part = jnp.dot(all_two, first_up, preferred_element_type=F32)
+    up_part = jnp.dot(all_two, second_up, preferred_element_type=F32)
+    activated = gated_product(gate_part, up_part).astype(BF)
     out_partial = jnp.dot(activated, down_matrix, preferred_element_type=F32).astype(BF)
     out_partial, all_cot = lax.optimization_barrier((out_partial, all_cot))
-    output = (residual + plane_scatter(out_partial).astype(F32)).astype(BF)
+    out_sum = plane_scatter(out_partial)
 
     act_grad = times_transposed(all_cot, down_matrix)
-    _, act_pull = jax.vjp(gated_product, hidden[:, :part], hidden[:, part:])
-    hidden_grad = jnp.concatenate(act_pull(act_grad), axis=1).astype(BF)
-    partial = times_transposed(hidden_grad, up_matrix).astype(BF)
+    _, act_pull = jax.vjp(gated_product, gate_part, up_part)
+    gate_back, up_back = (one.astype(BF) for one in act_pull(act_grad))
+    partial = times_transposed(gate_back, first_up) + times_transposed(up_back, second_up)
+    partial = partial.astype(BF)
     down_grad = contract_rows(activated, all_cot).astype(BF)
+    hidden_grad = jnp.concatenate([gate_back, up_back], axis=1)
     up_grad = contract_rows(all_two, hidden_grad).astype(BF)
-    partial, down_grad, up_grad = lax.optimization_barrier((partial, down_grad, up_grad))
+    partial, down_grad, up_grad, out_sum = lax.optimization_barrier(
+        (partial, down_grad, up_grad, out_sum)
+    )
+    output = (residual + out_sum.astype(F32)).astype(BF)
     down_line = lax.psum_scatter(down_grad, "l", scatter_dimension=0, tiled=True)
     up_line = lax.psum_scatter(up_grad, "l", scatter_dimension=0, tiled=True)
     residual_grad, gain_two_grad, all_res = plane_sum(partial, residual, cotangent, gain_two, 2)
-    mixed_grad = times_transposed(all_res, out_matrix).reshape(2, run, own)
     out_grad = contract_rows(mixed, all_res)
-    _, mix_pull = jax.vjp(
-        lambda state_value, branch_value: state_value * jax.nn.gelu(branch_value), state, branch
-    )
-    state_grad, branch_grad = mix_pull(mixed_grad)
-    next_coef = jnp.concatenate([coefficient[:, 1:], jnp.ones((2, 1, own), F32)], axis=1)
-    suffix_coef, local_grad = scan_pairs(next_coef, state_grad, True)
-    first = coefficient[:, 0]
-    ends = lax.all_gather(
-        jnp.stack([first * suffix_coef[:, 0], first * local_grad[:, 0]]), "l", axis=0, tiled=False
-    )
-    from_right = jnp.zeros((2, own), F32)
-    for other in reversed(range(1, lines)):
-        longer = ends[other, 0] * from_right + ends[other, 1]
-        from_right = jnp.where(other > line, longer, from_right)
-    total = local_grad + suffix_coef * from_right[:, None]
-    prev_state = jnp.concatenate([state_in[:, None], state[:, :-1]], axis=1)
-    pre_grad, decay_grad, conv_rec_grad = gate_pull((total * prev_state, total))
-    pre_low = pre_grad.astype(BF)
-    bias_grad = jnp.sum(pre_low.astype(F32), axis=(0, 1)).reshape(2, own)
-    pre_low = pre_low.reshape(plane, 2, blocks, block_size)
-    pre_low = pre_low.transpose(2, 0, 1, 3).reshape(blocks, plane, 2 * block_size)
-    gate_grad = jnp.einsum(
-        "tbj,btk->bjk", conv_blocks, pre_low, preferred_element_type=F32
-    ).reshape(own, 2 * block_size)
-    conv_grad = conv_rec_grad + jnp.einsum(
-        "btk,bjk->tbj", pre_low, gates, preferred_element_type=F32
-    ).reshape(2, run, own)
-    edge_sum = jnp.zeros((2, run + 3, own), F32)
-    tap_list = []
-    for offset in range(4):
-        masked = conv_grad if offset == 0 else conv_grad * factors[offset]
-        edge_sum = edge_sum + jnp.pad(
-            taps[offset] * masked, ((0, 0), (3 - offset, offset), (0, 0))
+    branch_grad, ta, tb, ends = mix_state(
+        all_res, out_matrix, branch, pa, pb, state_in, conv_out, chan, gate_r, fac, length
+    )
+    from_right = line_start(ends, lines, True, 6)
+    proj_grad, last_rows, edges, sums, gate_grad = mix_gates(
+        ta, tb, from_right, pa, pb, state_in, conv_in, conv_out, branch_grad, chan, gate_r, gate_i, fac, length
+    )
+    edges = lax.ppermute(edges, "l", [(i + 1, i) for i in range(lines - 1)])
+    last_rows = last_rows + jnp.pad(edges[:, :3], ((0, 0), (5, 0), (0, 0)))
+    for one in range(2):
+        proj_grad = lax.dynamic_update_slice(
+            proj_grad, last_rows[one].astype(BF), ((one + 1) * run - 8, own)
         )
-        tap_list.append(
-            jnp.sum(masked * padded_in[:, 3 - offset : 3 - offset + run], axis=(0, 1))
-        )
-    tap_list.append(jnp.sum(conv_grad, axis=(0, 1)))
-    tap_grads = jnp.stack(tap_list)
-    back_edge = lax.ppermute(edge_sum[:, :3], "l", [(i + 1, i) for i in range(lines - 1)])
-    conv_in_grad = edge_sum[:, 3:] + jnp.pad(back_edge, ((0, 0), (run - 3, 0), (0, 0)))
-    proj_grad = jnp.concatenate([branch_grad, conv_in_grad], axis=-1).astype(BF)
-    proj_grad = proj_grad.reshape(plane, 2 * own)
+    sums = jnp.sum(sums, axis=1)
+    sums = sums.at[7].multiply(DECAY_RATE * jax.nn.sigmoid(-decay_own))
+    gate_grad = jnp.stack(
+        [
+            gate_grad[:, b * block_size : (b + 1) * block_size, b * block_size : (b + 1) * block_size]
+            for b in range(blocks)
+        ]
+    )
+    gate_grad = gate_grad.transpose(0, 2, 1, 3).reshape(own, 2 * block_size)
     partial = times_transposed(proj_grad, in_matrix).astype(BF)
     in_grad = contract_rows(all_one, proj_grad).astype(BF)
     owned = channels // owners
     chan = jnp.concatenate(
-        [out_grad, tap_grads.T, bias_grad.T, decay_grad[:, None], gate_grad], axis=1
+        [out_grad, sums.T, gate_grad], axis=1
     ).astype(BF)
     used = chan.shape[1]
     chan = jnp.pad(
@@ -849,12 +1516,9 @@
         down_line,
         lines,
     )
-    in_grad = in_all.reshape(2, 4, rows, 2, own).transpose(2, 3, 0, 1, 4)
-    in_grad = in_grad.reshape(rows, 2 * channels).astype(F32)
-    up_grad = up_all.reshape(2, 4, rows, 2 * lines, share).transpose(2, 3, 1, 0, 4)
-    up_grad = up_grad.reshape(rows, 2 * ff).astype(F32)
-    down_grad = down_all.reshape(2 * share, width).astype(F32)
-    out_grad = chan[:owned, :width].astype(F32)
+    up_grad, in_grad, down_grad, out_grad = settle(
+        up_all, in_all, down_all.reshape(2 * share, width), chan, owned, width, lines
+    )
     small = chan[:owned, width:used].astype(F32)
     gain_grads = lax.dynamic_slice_in_dim(gain_grads[:2], me * rows, rows, 1)
     return (

time: 1030 us -> 866 us (0.84)
  Pallas kernels: 356 us -> 579 us
  waiting for transfers between devices: 145 us -> 4.22 us
  blocking collectives: 114 us -> 0 us
  other arithmetic: 80.5 us -> 11.9 us
  local copies, waits for them, and re-layouts: 145 us -> 96.1 us
    pallas_call x2 -> x7, Pallas kernels: 11.7 us -> 264 us  [the longest x1 165 us: spread_inputs(): pl.pallas_call(functools.partial(start_kernel, lines, cuts), out_shape=[j...]
    all_gather x2 -> x1, waiting for transfers between devices: 90.2 us -> 0.01 us  [plane_gather(): return lax.all_gather(block, PLANE, axis=0, tiled=True)]
    all_gather x4 -> x0, blocking collectives: 78 us -> none  [the longest x1 36.8 us: on_device(): lax.all_gather(seg_ids, EVERY, axis=0, tiled=True).reshape(2, lines, run)]
    all_gather x5 -> x3, waiting for transfers between devices: 52.6 us -> 2.75 us  [the longest x1 2.75 us: on_device(): lax.all_gather(lax.dynamic_slice_in_dim(down_rows, half * share, share, 0...]
    all_to_all x2 -> x0, blocking collectives: 36 us -> none  [columns_in(): lax.all_to_all(sent, ('y', 'c'), split_axis=0, concat_axis=0, tiled=True)]
    reshape x10 -> x5, local copies, waits for them, and re-layouts: 37.8 us -> 8.62 us  [the longest x1 4.6 us: on_device(): up_rows = up_rows.reshape(4 * rows, 2, -1)]
    pallas_call x1, Pallas kernels: 191 us -> 162 us  [tail(): pl.pallas_call(functools.partial(tail_kernel, lines, cuts), out_shape=[ja...]
    reduce_sum x4 -> x1, other arithmetic: 27.8 us -> 0.03 us  [on_device(): sums = jnp.sum(sums, axis=1)]
  transfers between devices with their start and end apart: 12 -> 8, of which waited for: 4 -> 1; matrix products, arithmetic and copies ran while one was open for 28% -> 23% of each run, Pallas kernels for 35% -> 48%
where the time goes in v3:
time: 866 us; the launch traced here: 857 us
  Pallas kernels  579 us (67%)
  matrix products  148 us (17%)
  local copies, waits for them, and re-layouts  96.1 us (11%)
  between operations  15.1 us (2%)
  other arithmetic  11.9 us (1%)
    pallas_call x1, Pallas kernels, spread_inputs(): pl.pallas_call(functools.partial(start_kernel, lines, cuts), out_shape=[j...  165 us
    pallas_call x1, Pallas kernels, tail(): pl.pallas_call(functools.partial(tail_kernel, lines, cuts), out_shape=[ja...  162 us
    pallas_call x2, Pallas kernels, plane_sum(): pl.pallas_call(functools.partial(plane_kernel, mode, cuts), out_shape=out...  153 us
    dot_general x4, matrix products, times_transposed(): lax.dot_general(left_in, matrix, (((1,), (1,)), ((), ())), preferred_elem...  56.6 us
    unnamed x124, local copies, waits for them, and re-layouts  54.4 us
    dot_general x4, matrix products, contract_rows(): lax.dot_general(left_in, right_in, (((0,), (0,)), ((), ())), preferred_el...  45.3 us
    pallas_call x1, Pallas kernels, mix_forward(): pl.pallas_call(mix_forward_kernel, grid=(2, steps), in_specs=[slots(width...  37.5 us
    pallas_call x2, Pallas kernels, line_start(): pl.pallas_call(functools.partial(line_kernel, lines, backward), out_shape...  21 us
  transfers between devices with their start and end apart: 8, of which 1 were waited for; matrix products, arithmetic and copies ran while one was open for 23% of the time, Pallas kernels for 48%

profile of v3, /device:TPU:11, one launch (start us, length us, event | category | flops | bytes accessed | tf_op | source)
XLA Modules:
  0.0 856.9 jit_solution(17689167608890767056)
XLA Ops:
  12.4 1.8 copy.109
  14.6 4.6 copy.111
  19.2 1.7 dynamic-slice_bitcast_fusion
  22.2 2.6 copy.117.refs_2_
  27.4 165.4 %spread.1 = (bf16[8,256,2048]{2,1,0:T(8,128)(2,1)S(1)}, bf16[2,8,2048]{2,1,0:T(8,128)(2,1)S(1)}, bf16[4,4,128,640]{3,2,1,0:T(8,128)(2,1)S(1)}, bf16[4,128,1536]{...) custom-call(bf16[256,2048]{1,0:T(8,128)(2,1)S(1)} %copy-done.4, ...), custom_call_target="tpu_custom_call" | custom-call | flops 10485760 | bytes 209715200 | tf_op jit(solution)/shard_map/spread/pallas_call | solution.py:849
  195.7 3.3 copy-done.33
  201.1 4.6 reshape.212
  205.7 5.3 fusion.45
  216.8 2.6 copy.157
  220.1 2.6 dynamic_update_slice.13.refs_6_.refs_13_
  222.7 2.7 dynamic_update_slice.12.refs_5_.refs_8_.refs_12_
  227.5 1.7 copy-done.36
  229.2 37.5 %mix_forward.1 = (bf16[8,256,2048]{2,1,0:T(8,128)(2,1)}, f32[2048,320]{1,0:T(8,128)S(1)}, bf16[2,1040,320]{2,1,0:T(8,128)(2,1)S(1)}, bf16[2048,320]{1,0:T(8,128)...) custom-call(bf16[8,256,2048]{2,1,0:T(8,128)(2,1)} %copy-done.33, ...), custom_call_target="tpu_custom_call" | custom-call | flops 5368709120 | bytes 62914560 | tf_op jit(solution)/shard_map/mix_forward/pallas_call | solution.py:1170
  266.7 1.7 copy-done.2
  268.5 1.6 copy-done.3
  272.5 4.9 line_5.1.refs_5_.refs_7_
  279.0 5.1 fusion.18
  284.2 6.7 convolution_convert_fusion.2
  290.9 77.2 %plane_forward_1.1 = (f32[256,2048]{1,0:T(8,128)S(1)}, bf16[8,256,2048]{2,1,0:T(8,128)(2,1)S(1)}) custom-call(bf16[8,256,2048]{2,1,0:T(8,128)(2,1)} %bitcast.162, bf16[256,2048]{1,0:T(8,128)(2,1)S(1)} %copy-done.4, f32[1,2048]{1,0:T(1,128)S(1)} %bitcast.151), custom_call_target="tpu_custom_call" | custom-call | flops 10485760 | bytes 209715200 | tf_op jit(solution)/shard_map/plane_forward_1/pallas_call | solution.py:361
  369.4 3.3 copy-done.34
  372.7 11.9 %fusion.21 = f32[2048,768]{0,1:T(8,128)} fusion(bf16[2048,2048]{1,0:T(8,128)(2,1)} %bitcast.155, bf16[2048,1,768]{2,0,1:T(8,128)(2,1)} %all-gather.12.cloned.1.call-done), kind=kOutput, calls=%fused_computation.34 | convolution fusion | flops 6442450944 | bytes 17825792 | tf_op jit(solution)/shard_map/dot_general | solution.py:1452
  384.5 15.7 %multiply_convert_fusion.1 = (bf16[2048,768]{0,1:T(8,128)(2,1)}, f32[2048,768]{0,1:T(8,128)}) fusion(f32[2048,768]{0,1:T(8,128)} %fusion.21, bf16[2048,2048]{1,0:T(8,128)(2,1)} %bitcast.156, bf16[2048,768]{1,0:T(8,128)(2,1)} %all-gather.8.cloned.1.call-done), kind=kOutput, calls=%fused_computation.18 | convolution fusion | flops 6458179584 | bytes 27262976 | tf_op jit(solution)/shard_map/dot_general | solution.py:1453
  400.3 2.7 all-gather.10.cloned.1.call-done
  403.0 11.5 %convolution_convert_fusion.1 = bf16[2048,2048]{1,0:T(8,128)(2,1)} fusion(bf16[2048,768]{0,1:T(8,128)(2,1)} %get-tuple-element.214, bf16[768,2048]{1,0:T(8,128)(2,1)} %all-gather.10.cloned.1.call-done), kind=kOutput, calls=%fused_computation.4 | convolution fusion | flops 6446645248 | bytes 14680064 | tf_op jit(solution)/shard_map/dot_general | solution.py:1455
  414.6 18.0 %multiply_convert_fusion = (bf16[2048,768]{0,1:T(8,128)(2,1)}, bf16[2048,768]{0,1:T(8,128)(2,1)S(1)}) fusion(f32[2048,768]{0,1:T(8,128)} %fusion.21, f32[2048,768]{0,1:T(8,128)} %get-tuple-element.215, bf16[2048,2048]{1,0:T(8,128)(2,1)} %all-gather.6.cloned.1.call-done, bf16[768,2048]{1,0:T(8,128)(2,1)} %all-gather.10.cloned.1.call-done), kind=kOutput, calls=%fused_computation.17 | convolution fusion | flops 6480199680 | bytes 30408704 | tf_op jit(solution)/shard_map/dot_general | solution.py:33
  432.6 10.6 %fusion.19 = f32[2048,2048]{1,0:T(8,128)} fusion(bf16[2048,768]{0,1:T(8,128)(2,1)S(1)} %get-tuple-element.195, bf16[2048,1,768]{2,0,1:T(8,128)(2,1)S(1)} %copy-done.49), kind=kOutput, calls=%fused_computation.32 | convolution fusion | flops 6442450944 | bytes 23068672 | tf_op jit(solution)/shard_map/dot_general | solution.py:33
  443.3 10.3 %convolution_convert_fusion.4 = bf16[768,2048]{1,0:T(8,128)(2,1)} fusion(bf16[2048,768]{0,1:T(8,128)(2,1)S(1)} %copy-done.53, bf16[2048,2048]{1,0:T(8,128)(2,1)} %all-gather.6.cloned.1.call-done), kind=kOutput, calls=%fused_computation.21 | convolution fusion | flops 6444023808 | bytes 14680064 | tf_op jit(solution)/shard_map/dot_general | solution.py:27
  453.6 16.6 %add_convert_fusion = bf16[2048,2048]{1,0:T(8,128)(2,1)} fusion(f32[2048,2048]{1,0:T(8,128)} %fusion.19, bf16[2048,768]{0,1:T(8,128)(2,1)} %get-tuple-element.194, bf16[2048,768]{1,0:T(8,128)(2,1)} %all-gather.8.cloned.1.call-done), kind=kOutput, calls=%fused_computation | convolution fusion | flops 6450839552 | bytes 31457280 | tf_op jit(solution)/shard_map/dot_general | solution.py:33
  470.2 17.3 %convolution_convert_fusion.3 = bf16[2048,1536]{1,0:T(8,128)(2,1)} fusion(bf16[2048,2048]{1,0:T(8,128)(2,1)} %bitcast.157, bf16[2048,768]{0,1:T(8,128)(2,1)S(1)} %copy-done.50, bf16[2048,768]{0,1:T(8,128)(2,1)S(1)} %copy-done.52), kind=kOutput, calls=%fused_computation.6 | convolution fusion | flops 12900630528 | bytes 20971520 | tf_op jit(solution)/shard_map/dot_general | solution.py:27
  488.9 1.9 copy.130
  490.9 1.6 copy-done.8
  492.5 75.8 %plane_back_2.1 = (f32[256,2048]{1,0:T(8,128)S(1)}, f32[8,2048]{1,0:T(8,128)S(1)}, bf16[8,256,2048]{2,1,0:T(8,128)(2,1)S(1)}) custom-call(bf16[8,256,2048]{2,1,0:T(8,128)(2,1)} %bitcast.161, f32[256,2048]{1,0:T(8,128)S(1)} %copy-done.8, bf16[256,2048]{1,0:T(8,128)(2,1)S(1)} %copy-done.13, f32[1,2048]{1,0:T(1,128)S(1)} %bitcast.152), custom_call_target="tpu_custom_call" | custom-call | flops 10485760 | bytes 209715200 | tf_op jit(solution)/shard_map/plane_back_2/pallas_call | solution.py:361
  568.3 3.3 copy-done.9
  573.0 13.7 %mix_state.1 = (bf16[2048,320]{1,0:T(8,128)(2,1)S(1)}, f32[2048,320]{1,0:T(8,128)S(1)}, f32[2048,320]{1,0:T(8,128)S(1)}, f32[2,16,320]{2,1,0:T(8,128)S(1)}) custom-call(bf16[2048,2048]{1,0:T(8,128)(2,1)} %bitcast.142, bf16[320,2048]{1,0:T(8,128)(2,1)S(1)} %bitcast.146, f32[2048,320]{1,0:T(8,128)} %copy-done.3, f32[2048,320]{1,0:T(8,128)} %copy-done.2, ...), custom_call_target="tpu_custom_call" | custom-call | flops 2684354560 | bytes 41943040 | tf_op jit(solution)/shard_map/mix_state/pallas_call | solution.py:1220
  586.8 1.6 copy-done.14
  588.4 16.1 %line_6.1.refs_2_ = f32[2,8,320]{2,1,0:T(8,128)S(1)} custom-call(f32[2,16,320]{2,1,0:T(8,128)S(1)} %get-tuple-element.111.ends), custom_call_target="tpu_custom_call" | custom-call | tf_op jit(solution)/shard_map/line_6/pallas_call | solution.py:1127
  604.5 20.7 %mix_gates.1 = (bf16[2048,640]{1,0:T(8,128)(2,1)S(1)}, f32[2,8,320]{2,1,0:T(8,128)S(1)}, f32[2,8,320]{2,1,0:T(8,128)S(1)}, f32[8,8,320]{2,1,0:T(8,128)S(1)}, f32[2,320,320]{2,1,0:T(8,128)S(1)}) custom-call(f32[2048,320]{1,0:T(8,128)S(1)} %get-tuple-element.109.refs_0_, f32[2048,320]{1,0:T(8,128)} %copy-done.14, f32[2,8,320]{2,1,0:T(8,128)S(1)} %line_6.1.refs_2_, ...), custom_call_target="tpu_custom_call" | custom-call | flops 1677721600 | bytes 41943040 | tf_op jit(solution)/shard_map/mix_gates/pallas_call | solution.py:1266
  626.9 1.9 collective-permute-start
  629.0 3.2 add_convert_fusion.1
  632.3 7.3 convolution_convert_fusion.6
  640.3 2.5 concatenate.36
  644.1 2.2 dynamic_update_slice.14
  646.3 1.6 dynamic_update_slice.15
  648.0 11.4 %convolution_convert_fusion = bf16[2048,2048]{1,0:T(8,128)(2,1)} fusion(bf16[2048,640]{1,0:T(8,128)(2,1)} %dynamic_update_slice.15, bf16[2048,640]{1,0:T(8,128)(2,1)} %bitcast.158), kind=kOutput, calls=%fused_computation.3 | convolution fusion | flops 5372903424 | bytes 13631488 | tf_op jit(solution)/shard_map/dot_general | solution.py:33
  659.4 10.3 %convolution_convert_fusion.5 = bf16[2048,640]{1,0:T(8,128)(2,1)} fusion(bf16[2048,2048]{1,0:T(8,128)(2,1)} %bitcast.180, bf16[2048,640]{1,0:T(8,128)(2,1)S(1)} %copy-done.38), kind=kOutput, calls=%fused_computation.22 | convolution fusion | flops 5370019840 | bytes 13631488 | tf_op jit(solution)/shard_map/dot_general | solution.py:27
  669.7 162.4 %tail.1 = (f32[256,2048]{1,0:T(8,128)}, bf16[2,4,128,640]{3,2,1,0:T(8,128)(2,1)}, bf16[160,2432]{1,0:T(8,128)(2,1)}, bf16[2,4,128,1536]{3,2,1,0:T(8,128)(2,1)}, ...) custom-call(bf16[8,256,2048]{2,1,0:T(8,128)(2,1)} %bitcast.160, bf16[256,2048]{1,0:T(8,128)(2,1)} %refs_1_.3, ...), custom_call_target="tpu_custom_call" | custom-call | flops 10485760 | bytes 209715200 | tf_op jit(solution)/shard_map/tail/pallas_call | solution.py:578
  837.4 1.9 copy-done.15
  843.2 5.4 settle.1
  (193 shorter events, 45.1 us)
Async XLA Ops:
  7.2 270.3 %copy-start = (bf16[384,2048]{1,0:T(8,128)(2,1)S(1)}, bf16[384,2048]{1,0:T(8,128)(2,1)}, u32[]{:S(2)}) copy-start(bf16[384,2048]{1,0:T(8,128)(2,1)} %param.28) | copy-start | bytes 4718596
  7.2 219.0 %all-gather.6.cloned.1.call-start = ((), (), s32[]{:S(2)}) async-start(), calls=%async_computation.3 | async-start | bytes 9437184 | tf_op jit(solution)/shard_map/all_gather | solution.py:43
  7.9 364.8 %all-gather.12.cloned.1.call-start = ((), (), s32[]{:S(2)}) async-start(), calls=%async_computation.9 | async-start | bytes 3932160 | tf_op jit(solution)/shard_map/all_gather | solution.py:1442
  20.9 3.9 copy-start.46
  20.9 4.0 copy-start.4
  24.9 1.4 copy-start.10
  195.7 3.3 copy-start.33
  199.0 1.5 copy-start.35
  211.0 3.3 copy-start.28
  212.0 172.5 %all-gather.8.cloned.1.call-start = ((), (), s32[]{:S(2)}) async-start(), calls=%async_computation.4 | async-start | bytes 3932160 | tf_op jit(solution)/shard_map/all_gather | solution.py:1444
  213.2 12.2 %copy-start.47 = (bf16[320,1]{0,1:T(2,128)(2,1)}, bf16[320,1]{0,1:T(2,128)(2,1)S(1)}, u32[]{:S(2)}) copy-start(bf16[320,1]{0,1:T(2,128)(2,1)S(1)} %copy.140) | copy-start | bytes 1924
  214.9 11.4 %copy-start.40 = (bf16[2,8,2048]{2,1,0:T(8,128)(2,1)S(1)}, bf16[2,8,2048]{2,1,0:T(8,128)(2,1)}, u32[]{:S(2)}) copy-start(bf16[2,8,2048]{2,1,0:T(8,128)(2,1)} %copy-done.39) | copy-start | bytes 196612
  225.5 41.2 %copy-start.29 = (f32[8,320]{1,0:T(8,128)}, f32[8,320]{1,0:T(8,128)S(1)}, u32[]{:S(2)}) copy-start(f32[8,320]{1,0:T(8,128)S(1)} %scatter.4.refs_4_.refs_7_.refs_11_) | copy-start | bytes 30724
  226.2 40.5 %copy-start.32 = (f32[1,16,128]{2,1,0:T(8,128)}, f32[1,16,128]{2,1,0:T(8,128)S(1)}, u32[]{:S(2)}) copy-start(f32[1,16,128]{2,1,0:T(8,128)S(1)} %get-tuple-element.205) | copy-start | bytes 24580
  227.5 1.7 copy-start.36
  266.7 1.7 copy-start.2
  268.5 1.6 copy-start.3
  277.4 125.6 %all-gather.10.cloned.1.call-start = ((), (), s32[]{:S(2)}) async-start(), calls=%async_computation.5 | async-start | bytes 3932160 | tf_op jit(solution)/shard_map/all_gather | solution.py:1445
  278.5 209.0 %reduce-scatter.4.cloned.1.call-start = ((), (), s32[]{:S(2)}) async-start(), calls=%async_computation.6 | async-start | bytes 9437184 | tf_op jit(solution)/shard_map/reduce_scatter | solution.py:47
  279.0 5.2 copy-start.23
  284.1 6.7 copy-start.41
  369.4 3.3 copy-start.34
  414.5 255.1 %reduce-scatter.8.cloned.1.call-start = ((), (), s32[]{:S(2)}) async-start(), calls=%async_computation.8 | async-start | bytes 3932160 | tf_op jit(solution)/shard_map/reduce_scatter | solution.py:1471
  414.6 18.0 %copy-start.49 = (bf16[2048,1,768]{2,0,1:T(8,128)(2,1)S(1)}, bf16[2048,1,768]{2,0,1:T(8,128)(2,1)}, u32[]{:S(2)}) copy-start(bf16[2048,1,768]{2,0,1:T(8,128)(2,1)} %all-gather.12.cloned.1.call-done) | copy-start | bytes 9437188
  432.6 10.6 %copy-start.51 = (bf16[2048,768]{0,1:T(8,128)(2,1)}, bf16[2048,768]{0,1:T(8,128)(2,1)S(1)}, u32[]{:S(2)}) copy-start(bf16[2048,768]{0,1:T(8,128)(2,1)S(1)} %get-tuple-element.195) | copy-start | bytes 9437188
  432.6 10.6 %copy-start.53 = (bf16[2048,768]{0,1:T(8,128)(2,1)S(1)}, bf16[2048,768]{0,1:T(8,128)(2,1)}, u32[]{:S(2)}) copy-start(bf16[2048,768]{0,1:T(8,128)(2,1)} %get-tuple-element.214) | copy-start | bytes 9437188
  453.6 16.6 %copy-start.50 = (bf16[2048,768]{0,1:T(8,128)(2,1)S(1)}, bf16[2048,768]{0,1:T(8,128)(2,1)}, u32[]{:S(2)}) copy-start(bf16[2048,768]{0,1:T(8,128)(2,1)} %get-tuple-element.194) | copy-start | bytes 9437188
  453.6 16.6 %copy-start.52 = (bf16[2048,768]{0,1:T(8,128)(2,1)S(1)}, bf16[2048,768]{0,1:T(8,128)(2,1)}, u32[]{:S(2)}) copy-start(bf16[2048,768]{0,1:T(8,128)(2,1)} %copy-done.51) | copy-start | bytes 9437188
  487.5 1.4 copy-start.42
  487.5 3.3 copy-start.13
  487.5 182.2 %reduce-scatter.6.cloned.1.call-start = ((), (), s32[]{:S(2)}) async-start(), calls=%async_computation.7 | async-start | bytes 7864320 | tf_op jit(solution)/shard_map/reduce_scatter | solution.py:1472
  490.9 1.6 copy-start.8
  492.5 80.6 %copy-start.6 = (f32[2048,4]{1,0:T(8,128)S(1)}, f32[2048,4]{1,0:T(8,128)}, u32[]{:S(2)}) copy-start(f32[2048,4]{1,0:T(8,128)} %copy.125.refs_7_.refs_9_.refs_14_) | copy-start | bytes 98308
  492.5 80.6 %copy-start.12 = (bf16[2048,320]{1,0:T(8,128)(2,1)S(1)}, bf16[2048,320]{1,0:T(8,128)(2,1)}, u32[]{:S(2)}) copy-start(bf16[2048,320]{1,0:T(8,128)(2,1)} %copy-done.11) | copy-start | bytes 3932164
  492.5 80.6 %copy-start.24 = (bf16[2,160,2048]{2,1,0:T(8,128)(2,1)S(1)}, bf16[2,160,2048]{2,1,0:T(8,128)(2,1)}, u32[]{:S(2)}) copy-start(bf16[2,160,2048]{2,1,0:T(8,128)(2,1)} %copy-done.22) | copy-start | bytes 3932164
  492.5 80.6 %copy-start.30 = (f32[8,320]{1,0:T(8,128)S(1)}, f32[8,320]{1,0:T(8,128)}, u32[]{:S(2)}) copy-start(f32[8,320]{1,0:T(8,128)} %copy-done.29) | copy-start | bytes 30724
  568.3 3.3 copy-start.9
  573.0 13.8 %copy-start.31 = (f32[8,2048]{1,0:T(8,128)}, f32[8,2048]{1,0:T(8,128)S(1)}, u32[]{:S(2)}) copy-start(f32[8,2048]{1,0:T(8,128)S(1)} %get-tuple-element.118.refs_4_) | copy-start | bytes 196612
  573.0 31.5 %copy-start.18 = (bf16[2,1040,320]{2,1,0:T(8,128)(2,1)S(1)}, bf16[2,1040,320]{2,1,0:T(8,128)(2,1)}, u32[]{:S(2)}) copy-start(bf16[2,1040,320]{2,1,0:T(8,128)(2,1)} %copy-done.17) | copy-start | bytes 3993604
  586.8 1.6 copy-start.14
  604.5 22.3 %copy-start.48 = (bf16[320,1]{0,1:T(2,128)(2,1)S(1)}, bf16[320,1]{0,1:T(2,128)(2,1)}, u32[]{:S(2)}) copy-start(bf16[320,1]{0,1:T(2,128)(2,1)} %copy-done.47) | copy-start | bytes 1924
  625.3 1.5 copy-start.37
  626.9 17.2 %collective-permute-start = (f32[2,8,320]{2,1,0:T(8,128)S(1)}, f32[2,8,320]{2,1,0:T(8,128)S(1)}, u32[]{:S(2)}, u32[]{:S(2)}) collective-permute-start(f32[2,8,320]{2,1,0:T(8,128)S(1)} %get-tuple-element.116), channel_id=1, source_target_pairs={{4,0},{8,4},{12,8},{5,1},{9,5},{13,9},{6,2},{10,6},{14,10},{7,3},{... | collective-permute-start | bytes 61448 | tf_op jit(solution)/shard_map/ppermute | solution.py:1482
  628.8 3.4 copy-start.44
  648.0 11.4 %copy-start.38 = (bf16[2048,640]{1,0:T(8,128)(2,1)S(1)}, bf16[2048,640]{1,0:T(8,128)(2,1)}, u32[]{:S(2)}) copy-start(bf16[2048,640]{1,0:T(8,128)(2,1)} %dynamic_update_slice.15) | copy-start | bytes 7864324
  837.4 1.9 copy-start.15
  843.2 5.4 copy-start.43
  843.2 6.7 copy-start.1
  (14 other events, 15.7 us)
Sparse Core Ops, SparseCore 0:
  9.9 81.0 all-gather.5
  212.1 59.3 all-gather.11
  277.5 61.8 all-gather.7
  340.8 62.1 all-gather.9
  414.7 72.1 reduce-scatter.3
  489.1 59.9 reduce-scatter.7
  552.1 115.9 reduce-scatter.5

commit v4 on v3

--- a/solution.py
+++ b/solution.py
@@ -96,8 +96,26 @@
         step(pl.ds(pl.multiple_of(i * rows, rows), rows))
 
 
+def block_maker(lhs, rhs, length, transposed):
+    def make(slot, target):
+        rows = lhs[pl.ds(pl.multiple_of(slot * length, length), length)]
+        wide = target.shape[1] // 4
+        for part in range(4):
+            at = slice(part * wide, (part + 1) * wide)
+            if transposed:
+                block = lax.dot_general(
+                    rows, rhs[at], (((1,), (1,)), ((), ())), preferred_element_type=F32
+                )
+            else:
+                block = jnp.dot(rows, rhs[:, at], preferred_element_type=F32)
+            target[:, at] = block.astype(BF)
+
+    return make
+
+
 class PlaneSum:
-    def __init__(self, wires, partial, own, got, hop_a, hop_b, cuts):
+    def __init__(self, wires, make, away, own, got, hop_a, hop_b, cuts):
+        self.make, self.away = make, away
         self.own, self.got, self.hop_a, self.hop_b = own, got, hop_a, hop_b
         self.cuts, self.part = cuts, own.shape[1] // cuts
         me, core, side_a, side_b = sides()
@@ -105,31 +123,28 @@
         self.chips = [me, side_a, side_b, diag]
         self.theirs = {0: 0, 1: 2, 2: 1, 3: 3}
         self.order = [3, 1, 2, 0]
-        self.swaps, self.loads = {}, {}
+        self.swaps = {}
         self.far_a, self.near_a, self.far_b = {}, {}, {}
         for piece in range(cuts):
             rows = pl.ds(piece * self.part, self.part)
             for rel in self.order:
-                chip = self.chips[rel]
-                away = slot_of((chip[0], chip[1], chip[2], 1 - me[3]))
                 self.swaps[rel, piece] = wires.far(
-                    partial.at[away, rows], got.at[self.theirs[rel], rows], core
-                )
-                self.loads[rel, piece] = wires.near(
-                    partial.at[slot_of(chip), rows], own.at[rel, rows]
+                    away.at[rel, rows], got.at[self.theirs[rel], rows], core
                 )
             self.far_a[piece] = wires.far(own.at[3, rows], hop_a.at[0, rows], side_a)
             self.near_a[piece] = wires.far(own.at[1, rows], hop_a.at[1, rows], side_a)
             self.far_b[piece] = wires.far(own.at[2, rows], hop_b.at[rows], side_b)
 
-    def start(self):
-        for rel in self.order:
-            for piece in range(self.cuts):
-                self.swaps[rel, piece].start()
-                self.loads[rel, piece].start()
+    def make_away(self, rel):
+        chip = self.chips[rel]
+        self.make(slot_of((chip[0], chip[1], chip[2], 1 - chip[3])), self.away.at[rel])
+        for piece in range(self.cuts):
+            self.swaps[rel, piece].start()
+
+    def make_home(self, rel):
+        self.make(slot_of(self.chips[rel]), self.own.at[rel])
 
     def landed(self, rel, piece):
-        self.loads[rel, piece].wait()
         self.swaps[self.theirs[rel], piece].wait_recv()
 
     def join(self, rel, piece, hopped):
@@ -141,12 +156,23 @@
                 total = total + self.hop_a[0, rows].astype(F32)
             self.own[rel, rows] = total.astype(BF)
 
+    def pass_side(self, rel, copies):
+        for piece in range(self.cuts):
+            self.landed(rel, piece)
+            self.join(rel, piece, False)
+            copies[piece].start()
+
     def first_side(self):
-        for rel, copies in ((3, self.far_a), (1, self.near_a)):
-            for piece in range(self.cuts):
-                self.landed(rel, piece)
-                self.join(rel, piece, False)
-                copies[piece].start()
+        self.make_away(3)
+        self.make_home(3)
+        self.make_away(2)
+        self.pass_side(3, self.far_a)
+        self.make_home(1)
+        self.make_away(1)
+        self.pass_side(1, self.near_a)
+        self.make_home(2)
+        self.make_away(0)
+        self.make_home(0)
 
     def second_side(self):
         for piece in range(self.cuts):
@@ -303,17 +329,34 @@
 
 def plane_kernel(mode, cuts, *refs):
     refs = list(refs)
-    partial, base_ref = refs.pop(0), refs.pop(0)
-    up_ref = refs.pop(0) if mode == "back" else None
-    gain_ref, out_ref = refs.pop(0), refs.pop(0)
+    lhs_far, rhs_far, base_far = refs.pop(0), refs.pop(0), refs.pop(0)
+    up_far = refs.pop(0) if mode == "back" else None
+    gain_ref, out_far = refs.pop(0), refs.pop(0)
     gain_out = refs.pop(0) if mode == "back" else None
-    all_ref, own, got, hop_a, hop_b, mine, send_sems, recv_sems = refs
+    all_ref, lhs, rhs, away, own, got, hop_a, hop_b, base_ref, out_ref = refs[:10]
+    up_ref = refs[10] if mode == "back" else None
+    mine, send_sems, recv_sems = refs[-3:]
     _, core, side_a, side_b = sides()
     wires = Wires(send_sems, recv_sems)
+    operands = [wires.near(lhs_far, lhs), wires.near(rhs_far, rhs)]
+    for copy in operands:
+        copy.start()
     greet([core, side_a, side_b])
-    total = PlaneSum(wires, partial, own, got, hop_a, hop_b, cuts)
+    make = block_maker(lhs, rhs, out_ref.shape[0], mode == "back")
+    total = PlaneSum(wires, make, away, own, got, hop_a, hop_b, cuts)
     spread = PlaneGather(wires, mine, all_ref, cuts)
-    total.start()
+    loads = [wires.near(base_far, base_ref)]
+    if mode == "back":
+        loads.append(wires.near(up_far, up_ref))
+    part = out_ref.shape[0] // cuts
+    stores = []
+    for piece in range(cuts):
+        rows = pl.ds(piece * part, part)
+        stores.append(wires.near(out_ref.at[rows], out_far.at[rows]))
+    for copy in operands:
+        copy.wait()
+    for copy in loads:
+        copy.start()
     total.first_side()
     total.second_side()
     if mode == "back":
@@ -321,18 +364,27 @@
         use = back_rows(base_ref, up_ref, gain_ref, out_ref, gain_out, mine)
     else:
         use = forward_rows(base_ref, gain_ref, out_ref, mine)
+    for copy in loads:
+        copy.wait()
     for piece in range(cuts):
         total.finish(piece, use)
         spread.start(piece)
+    for copy in stores:
+        copy.start()
     spread.forward("a", ("ab", "ac"))
     spread.forward("b", ("bc",))
     spread.forward("ab", ("dc",))
     spread.finish()
+    for copy in stores:
+        copy.wait()
     total.drain()
 
 
-def sum_scratch(length, width):
+def sum_scratch(lhs, rhs, length, width):
     return [
+        pltpu.VMEM(lhs.shape, BF),
+        pltpu.VMEM(rhs.shape, BF),
+        pltpu.VMEM((4, length, width), BF),
         pltpu.VMEM((4, length, width), BF),
         pltpu.VMEM((4, length, width), BF),
         pltpu.VMEM((2, length, width), BF),
@@ -340,40 +392,43 @@
     ]
 
 
-def plane_sum(partial, base, up, gain, number):
+def plane_sum(lhs, rhs, base, up, gain, number):
     mode = "forward" if up is None else "back"
     length, width = base.shape
     cuts = 2
     vmem, left = pl.BlockSpec(memory_space=pltpu.VMEM), pl.BlockSpec(memory_space=pl.ANY)
-    args, specs = [partial.reshape(8, length, width), base], [left, vmem]
-    outs, out_specs = [jax.ShapeDtypeStruct((length, width), F32)], [vmem]
+    args, specs = [lhs, rhs, base], [left, left, left]
+    outs, out_specs = [jax.ShapeDtypeStruct((length, width), F32)], [left]
+    scratch = [pltpu.VMEM((length, width), base.dtype), pltpu.VMEM((length, width), F32)]
     if mode == "back":
         args.append(up)
-        specs.append(vmem)
+        specs.append(left)
         outs.append(jax.ShapeDtypeStruct((8, width), F32))
         out_specs.append(vmem)
+        scratch.append(pltpu.VMEM((length, width), up.dtype))
     args.append(gain.reshape(1, width))
     specs.append(vmem)
     outs.append(jax.ShapeDtypeStruct((8, length, width), BF))
     out_specs.append(left)
-    sems = cuts * (8 + 3 + 8)
+    sems = cuts * (4 + 3 + 8 + 1) + 4
     got = list(
         pl.pallas_call(
             functools.partial(plane_kernel, mode, cuts),
             out_shape=outs,
             in_specs=specs,
             out_specs=out_specs,
-            scratch_shapes=sum_scratch(length, width)
+            scratch_shapes=sum_scratch(lhs, rhs, length, width)
+            + scratch
             + [
                 pltpu.VMEM((length, width), BF),
                 pltpu.SemaphoreType.DMA((sems,)),
                 pltpu.SemaphoreType.DMA((sems,)),
             ],
             compiler_params=pltpu.CompilerParams(
-                collective_id=number, has_side_effects=True, vmem_limit_bytes=40 << 20
+                collective_id=number, has_side_effects=True, vmem_limit_bytes=56 << 20
             ),
             cost_estimate=pl.CostEstimate(
-                flops=20 * base.size, bytes_accessed=400 * base.size, transcendentals=0
+                flops=2 * lhs.size * width, bytes_accessed=400 * base.size, transcendentals=0
             ),
             name=f"plane_{mode}_{number}",
         )(*args)
@@ -382,11 +437,14 @@
     return got
 
 
-def tail_kernel(lines, cuts, *refs):
-    (partial, base_ref, up_ref, gain_ref, other_gain, in_ref, chan_ref, upz, downz) = refs[:9]
-    (out_ref, in_all, chan_out, up_all, down_all, gains) = refs[9:15]
-    (own, got, hop_a, hop_b, gain_out, in_own, in_left, in_right) = refs[15:23]
-    (chan_own, chan_left, chan_right, chan_got, tiny, tiny_line, send_sems, recv_sems) = refs[23:]
+def tail_kernel(lines, cuts, straight, *refs):
+    (lhs_far, rhs_far, base_far, up_far, gain_ref, other_gain, in_ref, chan_ref, upz, downz) = refs[:10]
+    (out_far, in_all, chan_out, up_all, down_all, gains) = refs[10:16]
+    base_ref, up_ref, out_ref = refs[-3:]
+    refs = refs[:-3]
+    (lhs, rhs, away, own, got, hop_a, hop_b) = refs[16:23]
+    (gain_out, in_own, in_left, in_right) = refs[23:27]
+    (chan_own, chan_left, chan_right, chan_got, tiny, tiny_line, send_sems, recv_sems) = refs[27:]
     me, core, side_a, side_b = sides()
     x, l, y, c = me
     k = 2 * y + c
@@ -397,16 +455,17 @@
     others = [(x, lax.rem(l + d, lines), y, c) for d in range(1, lines)]
     greet(mates + [twin] + twins + others)
 
-    total = PlaneSum(wires, partial, own, got, hop_a, hop_b, cuts)
+    make = block_maker(lhs, rhs, out_ref.shape[0], True)
+    total = PlaneSum(wires, make, away, own, got, hop_a, hop_b, cuts)
+    operands = [wires.near(lhs_far, lhs), wires.near(rhs_far, rhs)]
     per = chan_ref.shape[0]
-    owner = (4 * x + k) * per
     load_in = wires.near(in_ref, in_own)
     load_chan = wires.near(chan_ref, chan_own)
     in_sums = [
         LineSum(wires, lines, in_own.at[q], in_left.at[q], in_right.at[q], q)
         for q in range(lines)
     ]
-    chan_roots = [(owner + i) // 4 for i in range(per)]
+    chan_roots = [owner_of(x, k, i, per, straight) // 4 for i in range(per)]
     chan_sums = [
         LineSum(wires, lines, chan_own.at[i], chan_left.at[i], chan_right.at[i], chan_roots[i])
         for i in range(per)
@@ -418,13 +477,24 @@
             copies.append(wires.far(block(2 * at[2] + at[3]), target.at[x, k], at))
         return copies
 
-    total.start()
+    loads = [wires.near(base_far, base_ref), wires.near(up_far, up_ref)]
+    part = out_ref.shape[0] // cuts
+    stores = []
+    for piece in range(cuts):
+        at = pl.ds(piece * part, part)
+        stores.append(wires.near(out_ref.at[at], out_far.at[at]))
     load_in.start()
+    for copy in operands:
+        copy.start()
     load_chan.start()
+    for copy in loads:
+        copy.start()
     up_copies = deliver(lambda to: upz.at[to], up_all)
     down_copies = [wires.near(downz, down_all.at[x]), wires.far(downz, down_all.at[x], twin)]
     load_in.wait()
     load_chan.wait()
+    for copy in operands:
+        copy.wait()
 
     def pass_right(q):
         one = in_sums[q]
@@ -471,8 +541,11 @@
         one.begin()
     gain_out[...] = jnp.zeros_like(gain_out)
     use = back_rows(base_ref, up_ref, gain_ref, out_ref, gain_out, None)
+    for copy in loads:
+        copy.wait()
     for piece in range(cuts):
         total.finish(piece, use)
+        stores[piece].start()
     for one in chan_sums:
         one.through()
     for q in range(lines):
@@ -500,10 +573,11 @@
     for one in chan_sums:
         one.end()
     goal = 4 * l + k
-    holds = goal // (4 * per) == x
+    for_x, holder, piece = holder_of(goal, per, straight)
+    holds = for_x == x
     chan_far, chan_near = [], []
     for i in range(per):
-        s = owner + i
+        s = owner_of(x, k, i, per, straight)
         mate = (x, l, lax.rem(s, 4) // 2, lax.rem(s, 2))
         far = wires.far(chan_own.at[i], chan_got, mate)
         near = wires.near(chan_own.at[i], chan_got)
@@ -522,9 +596,8 @@
             near.start()
             near.wait()
 
-    holder = lax.rem(goal // per, 4)
     for i in range(per):
-        mine_here = jnp.logical_and(holds, lax.rem(goal, per) == i)
+        mine_here = jnp.logical_and(holds, piece == i)
 
         @pl.when(jnp.logical_and(mine_here, holder != k))
         def _():
@@ -548,7 +621,7 @@
     gains[...] = tiny_line[0]
     for q in range(1, lines):
         gains[...] += tiny_line[q]
-    for copies in (in_copies, up_copies, down_copies):
+    for copies in (in_copies, up_copies, down_copies, stores):
         for copy in copies:
             copy.wait()
 
@@ -567,16 +640,16 @@
     total.drain()
 
 
-def tail(partial, base, up, gain, other_gain, in_grad, chan, upz, downz, lines):
+def tail(lhs, rhs, base, up, gain, other_gain, in_grad, chan, upz, downz, lines, straight):
     length, width = base.shape
     cuts = 2
     vmem, left = pl.BlockSpec(memory_space=pltpu.VMEM), pl.BlockSpec(memory_space=pl.ANY)
     rows = in_grad.shape[0] // (4 * lines)
     pieces = in_grad.reshape(lines, 4 * rows, in_grad.shape[1])
     per = chan.shape[0]
-    sems = cuts * 11 + 2 + 2 * (lines + per) + 16 + 2 + 8 + 3 + lines + 2 * per + 4
+    sems = cuts * 8 + 6 + 2 * (lines + per) + 16 + 2 + 8 + 3 + lines + 2 * per + 4
     return pl.pallas_call(
-        functools.partial(tail_kernel, lines, cuts),
+        functools.partial(tail_kernel, lines, cuts, straight),
         out_shape=[
             jax.ShapeDtypeStruct((length, width), F32),
             jax.ShapeDtypeStruct((2, 4, rows, in_grad.shape[1]), BF),
@@ -585,9 +658,9 @@
             jax.ShapeDtypeStruct((2,) + downz.shape, BF),
             jax.ShapeDtypeStruct((8, width), F32),
         ],
-        in_specs=[left, vmem, vmem, vmem, vmem, left, left, left, left],
-        out_specs=[vmem, left, left, left, left, vmem],
-        scratch_shapes=sum_scratch(length, width)
+        in_specs=[left, left, left, left, vmem, vmem, left, left, left, left],
+        out_specs=[left, left, left, left, left, vmem],
+        scratch_shapes=sum_scratch(lhs, rhs, length, width)
         + [pltpu.VMEM((8, width), F32)]
         + [pltpu.VMEM(pieces.shape, BF)] * 3
         + [pltpu.VMEM(chan.shape, BF)] * 3
@@ -597,6 +670,9 @@
             pltpu.VMEM((lines, 8, width), F32),
             pltpu.SemaphoreType.DMA((sems,)),
             pltpu.SemaphoreType.DMA((sems,)),
+            pltpu.VMEM((length, width), base.dtype),
+            pltpu.VMEM((length, width), F32),
+            pltpu.VMEM((length, width), F32),
         ],
         compiler_params=pltpu.CompilerParams(
             collective_id=3, has_side_effects=True, vmem_limit_bytes=56 << 20
@@ -605,7 +681,17 @@
             flops=20 * base.size, bytes_accessed=400 * base.size, transcendentals=0
         ),
         name="tail",
-    )(partial.reshape(8, length, width), base, up, gain.reshape(1, width), other_gain, pieces, chan, upz, downz)
+    )(lhs, rhs, base, up, gain.reshape(1, width), other_gain, pieces, chan, upz, downz)
+
+
+def owner_of(x, k, i, per, straight):
+    return 4 * (x * per + i) + k if straight else (4 * x + k) * per + i
+
+
+def holder_of(s, per, straight):
+    if straight:
+        return s // 4 // per, lax.rem(s, 4), lax.rem(s // 4, per)
+    return s // (4 * per), lax.rem(s // per, 4), lax.rem(s, per)
 
 
 class LineGather:
@@ -656,15 +742,14 @@
 
 
 class FromRoot:
-    def __init__(self, wires, lines, source, target, i, per):
+    def __init__(self, wires, lines, source, target, i, per, straight):
         x, l, y, c = (lax.axis_index(name) for name in EVERY)
         k = 2 * y + c
-        s = 4 * l + k
         self.l, self.lines = l, lines
-        wanted = (4 * x + k) * per + i
+        wanted = owner_of(x, k, i, per, straight)
         self.root = wanted // 4
-        mine = jnp.logical_and(s // (4 * per) == x, lax.rem(s, per) == i)
-        goal = lax.rem(s // per, 4)
+        for_x, goal, piece = holder_of(4 * l + k, per, straight)
+        mine = jnp.logical_and(for_x == x, piece == i)
         self.leaves = jnp.logical_and(mine, goal != k)
         self.stays = jnp.logical_and(mine, goal == k)
         self.comes = jnp.logical_and(self.root == l, lax.rem(wanted, 4) != k)
@@ -733,10 +818,10 @@
             self.left.wait_send()
 
 
-def start_kernel(lines, cuts, *refs):
-    (tok, mix, up, small, out, tiny) = refs[:6]
-    (tok_all, halo, mix_all, up_all, small_all, out_all, tiny_all) = refs[6:13]
-    send_sems, recv_sems = refs[13:]
+def start_kernel(lines, cuts, straight, *refs):
+    (tok, mix, up, small, tiny) = refs[:5]
+    (tok_all, halo, mix_all, up_all, small_all, tiny_all) = refs[5:11]
+    send_sems, recv_sems = refs[11:]
     me, core, side_a, side_b = sides()
     x, l, y, c = me
     k = 2 * y + c
@@ -757,10 +842,7 @@
     up_swap = exchange(up, up_all)
     spread = PlaneGather(wires, tok, tok_all, cuts)
     walk = LineGather(wires, lines, mix_all)
-    roots = []
-    for i in range(per):
-        roots.append(FromRoot(wires, lines, small, small_all, i, per))
-        roots.append(FromRoot(wires, lines, out, out_all, i, per))
+    roots = [FromRoot(wires, lines, small, small_all, i, per, straight) for i in range(per)]
     tiny_own = wires.near(tiny, tiny_all.at[x, c, y, l])
     tiny_line = [wires.far(tiny, tiny_all.at[x, c, y, l], at) for at in others]
     tiny_steps = [
@@ -778,37 +860,34 @@
 
     for copy in mix_swap + [tiny_own] + tiny_line:
         copy.start()
-    for piece in range(cuts):
-        spread.start(piece)
     for one in roots:
         one.start()
-    for copy in up_swap:
-        copy.start()
+    for piece in range(cuts):
+        spread.copies["a", piece].start()
+    for piece in range(cuts):
+        spread.copies["b", piece].start()
     for copy in mix_swap:
         copy.wait()
     walk.step(0)
-    for one in roots[:2]:
+    for one in roots:
         one.from_owner()
+    for piece in range(cuts):
+        spread.copies["c", piece].start()
+        spread.copies["own", piece].start()
     for copy in [tiny_own] + tiny_line:
         copy.wait()
-    for copy in tiny_steps[:2]:
+    for copy in tiny_steps:
         copy.start()
         copy.wait()
     walk.step(1)
-    for one in roots[2:]:
-        one.from_owner()
-    tiny_steps[2].start()
-    tiny_steps[2].wait()
-    for d in range(2, lines - 1):
+    spread.forward("a", ("ab", "ac"))
+    for one in roots:
+        one.from_line()
+    spread.forward("b", ("bc",))
+    for copy in up_swap:
+        copy.start()
+    for d in range(2, lines):
         walk.step(d)
-    spread.forward("a", ("ab", "ac"))
-    for one in roots[:2]:
-        one.from_line()
-    if lines > 2:
-        walk.step(lines - 1)
-    spread.forward("b", ("bc",))
-    for one in roots[2:]:
-        one.from_line()
     spread.forward("ab", ("dc",))
     spread.finish()
 
@@ -841,36 +920,85 @@
         one.drain()
 
 
-def spread_inputs(tok, mix, up, small, out, tiny, lines, per):
+def spread_inputs(tok, mix, up, small, tiny, lines, per, straight):
     length, width = tok.shape
     cuts = 2
     vmem, left = pl.BlockSpec(memory_space=pltpu.VMEM), pl.BlockSpec(memory_space=pl.ANY)
-    sems = 8 + cuts * 8 + 2 * lines + 2 * per * 4 + lines + 1 + 3 + 4
+    sems = 12 + cuts * 8 + 2 * lines + per * 4 + lines + 1 + 3 + 4
     return pl.pallas_call(
-        functools.partial(start_kernel, lines, cuts),
+        functools.partial(start_kernel, lines, cuts, straight),
         out_shape=[
             jax.ShapeDtypeStruct((8, length, width), BF),
             jax.ShapeDtypeStruct((2, 8, width), BF),
             jax.ShapeDtypeStruct((lines,) + mix.shape, BF),
             jax.ShapeDtypeStruct(up.shape, BF),
             jax.ShapeDtypeStruct((per,) + small.shape, BF),
-            jax.ShapeDtypeStruct((per,) + out.shape, BF),
             jax.ShapeDtypeStruct((2, 2, 2, lines) + tiny.shape, F32),
         ],
-        in_specs=[left] * 5 + [vmem],
-        out_specs=[left] * 6 + [vmem],
+        in_specs=[left] * 4 + [vmem],
+        out_specs=[left] * 5 + [vmem],
         scratch_shapes=[
             pltpu.SemaphoreType.DMA((sems,)),
             pltpu.SemaphoreType.DMA((sems,)),
         ],
         compiler_params=pltpu.CompilerParams(
-            collective_id=4, has_side_effects=True, vmem_limit_bytes=16 << 20
+            collective_id=4, has_side_effects=True, vmem_limit_bytes=56 << 20
         ),
         cost_estimate=pl.CostEstimate(
             flops=20 * tok.size, bytes_accessed=400 * tok.size, transcendentals=0
         ),
         name="spread",
-    )(tok, mix, up, small, out, tiny)
+    )(tok, mix, up, small, tiny)
+
+
+def pick_kernel(lines, straight, mlp, mix, up, mix_out):
+    x = lax.axis_index("x")
+    share = up.shape[-1] // (2 * lines)
+    own = mix_out.shape[-1] // 2
+    for k in range(4):
+        parts = []
+        for g in range(2 * lines):
+            at = (4 * g + k) * 2 * share
+            first, second = mlp[:, at : at + share], mlp[:, at + share : at + 2 * share]
+            parts.append(jnp.where(x == 0, first, second))
+        up[k] = jnp.concatenate(parts, axis=1)
+    for k in range(4):
+        parts = []
+        for side in range(2):
+            halves = []
+            for half in range(2):
+                base = side * 8 * own + half * 4 * own
+                if straight:
+                    owned = own * 8 // (4 * lines)
+                    per = own // owned
+                    starts = [(base + (4 * i + k) * owned, owned) for i in range(per)]
+                else:
+                    starts = [(base + k * own, own)]
+                halves.append(
+                    jnp.concatenate([mix[:, at : at + wide] for at, wide in starts], axis=1)
+                )
+            parts.append(jnp.where(x == 0, halves[0], halves[1]))
+        mix_out[k] = jnp.concatenate(parts, axis=1)
+
+
+def pick(mlp_in, mix_in, lines, straight):
+    rows, wide = mlp_in.shape
+    narrow = mix_in.shape[1]
+    steps = 4 if rows % 64 == 0 else 1
+    r = rows // steps
+    shapes = [wide // 8, narrow // 8]
+    return pl.pallas_call(
+        functools.partial(pick_kernel, lines, straight),
+        grid=(steps,),
+        in_specs=[
+            pl.BlockSpec((r, wide), lambda i: (i, 0)),
+            pl.BlockSpec((r, narrow), lambda i: (i, 0)),
+        ],
+        out_specs=[pl.BlockSpec((4, r, w), lambda i: (0, i, 0)) for w in shapes],
+        out_shape=[jax.ShapeDtypeStruct((4, rows, w), BF) for w in shapes],
+        compiler_params=pltpu.CompilerParams(vmem_limit_bytes=40 << 20),
+        name="pick",
+    )(mlp_in, mix_in)
 
 
 def gelu_parts(value):
@@ -930,12 +1058,27 @@
 
 
 def mix_forward_kernel(*refs):
-    (tok, halo, weight, gain, chan_ref, gate_r, gate_i, fac) = refs[:8]
-    (normed, branch, conv_in, conv_out, pa, pb, ends) = refs[8:15]
-    (rows_in, coef, drive, carry) = refs[15:]
+    (tok, halo, weight, gain, chan_ref, gate_r, gate_i, fac, cot) = refs[:9]
+    (normed, branch, conv_in, conv_out, pa, pb, ends, cot_all) = refs[9:17]
+    (rows_in, coef, drive, carry, send_sems, recv_sems) = refs[17:]
     length, own = branch.shape
     chunk = pl.program_id(1)
     chan = chan_ref[...]
+    turn = pl.program_id(0) * pl.num_programs(1) + chunk
+    last = 2 * pl.num_programs(1) - 1
+    _, core, side_a, side_b = sides()
+    spread = PlaneGather(Wires(send_sems, recv_sems), cot, cot_all, 2)
+
+    @pl.when(turn == 0)
+    def _():
+        greet([core, side_a, side_b])
+        for piece in range(2):
+            spread.start(piece)
+
+    @pl.when(turn == last - 2)
+    def _():
+        spread.forward("a", ("ab", "ac"))
+        spread.forward("b", ("bc",))
 
     def norm_of(values):
         values = values.astype(F32)
@@ -982,6 +1125,11 @@
     scan_tiles(length, False, coef, drive, pa, pb, carry)
     ends[0, 0:8] = carry[0]
     ends[0, 8:16] = carry[1]
+
+    @pl.when(turn == last)
+    def _():
+        spread.forward("ab", ("dc",))
+        spread.finish()
 
 
 def mix_state_kernel(*refs):
@@ -1162,7 +1310,7 @@
     return steps, rows, slots, whole, held
 
 
-def mix_forward(tok_all, halo, weight, gain, chan, gate_r, gate_i, fac):
+def mix_forward(tok_all, halo, weight, gain, chan, gate_r, gate_i, fac, cot):
     slots_in, length, width = tok_all.shape
     own, run = chan.shape[1], 4 * length
     steps, rows, slots, whole, held = mix_specs(run, length, own, False)
@@ -1179,6 +1327,7 @@
             whole(own, own),
             whole(own, own),
             rows(fac.shape[1]),
+            pl.BlockSpec(memory_space=pl.ANY),
         ],
         out_specs=[
             slots(width),
@@ -1188,6 +1337,7 @@
             rows(own),
             rows(own),
             held(16, own),
+            pl.BlockSpec(memory_space=pl.ANY),
         ],
         out_shape=[
             jax.ShapeDtypeStruct(tok_all.shape, BF),
@@ -1197,19 +1347,24 @@
             flat,
             flat,
             jax.ShapeDtypeStruct((2, 16, own), F32),
+            jax.ShapeDtypeStruct((8,) + cot.shape, BF),
         ],
         scratch_shapes=[
             pltpu.VMEM((16 + length, own), F32),
             pltpu.VMEM((length, own), F32),
             pltpu.VMEM((length, own), F32),
             pltpu.VMEM((2, 8, own), F32),
-        ],
-        compiler_params=pltpu.CompilerParams(vmem_limit_bytes=40 << 20),
+            pltpu.SemaphoreType.DMA((16,)),
+            pltpu.SemaphoreType.DMA((16,)),
+        ],
+        compiler_params=pltpu.CompilerParams(
+            collective_id=7, has_side_effects=True, vmem_limit_bytes=40 << 20
+        ),
         cost_estimate=pl.CostEstimate(
             flops=4 * run * width * 2 * own, bytes_accessed=60 << 20, transcendentals=0
         ),
         name="mix_forward",
-    )(tok_all, halo, weight, gain.reshape(1, width), chan, gate_r, gate_i, fac)
+    )(tok_all, halo, weight, gain.reshape(1, width), chan, gate_r, gate_i, fac, cot)
 
 
 def mix_state(res, weight, branch, pa, pb, state_in, conv_out, chan, gate_r, fac, length):
@@ -1306,7 +1461,7 @@
     )(ta, tb, from_right, pa, pb, pa, pb, state_in, conv_in, conv_out, branch_grad, chan, gate_r, gate_i, fac)
 
 
-def settle_kernel(lines, up_all, in_all, down_all, chan, up_out, in_out, down_out, out_out):
+def settle_kernel(lines, straight, up_all, in_all, down_all, chan, up_out, in_out, down_out, out_out):
     share = up_all.shape[-1] // (2 * lines)
     own = in_all.shape[-1] // 2
     ups = [[up_all[x, k].astype(F32) for k in range(4)] for x in range(2)]
@@ -1315,21 +1470,30 @@
         row = [ups[x][k][:, at] for k in range(4) for x in range(2)]
         up_out[:, part * 8 * share : (part + 1) * 8 * share] = jnp.concatenate(row, axis=1)
     for part in range(2):
-        at = slice(part * own, (part + 1) * own)
-        row = [in_all[x, k].astype(F32)[:, at] for x in range(2) for k in range(4)]
+        if straight:
+            owned = own * 8 // (4 * lines)
+            row = [
+                in_all[x, k].astype(F32)[:, part * own + i * owned : part * own + (i + 1) * owned]
+                for x in range(2)
+                for i in range(own // owned)
+                for k in range(4)
+            ]
+        else:
+            at = slice(part * own, (part + 1) * own)
+            row = [in_all[x, k].astype(F32)[:, at] for x in range(2) for k in range(4)]
         in_out[:, part * 8 * own : (part + 1) * 8 * own] = jnp.concatenate(row, axis=1)
     down_out[...] = down_all[...].astype(F32)
     out_out[...] = chan[:, : out_out.shape[1]].astype(F32)
 
 
-def settle(up_all, in_all, down_all, chan, owned, width, lines):
+def settle(up_all, in_all, down_all, chan, owned, width, lines, straight):
     rows, share2 = up_all.shape[2], down_all.shape[0]
     steps = 4 if not (rows % 64 or share2 % 64 or owned % 32) else 1
     r, d, o = rows // steps, share2 // steps, owned // steps
     wide, narrow = up_all.shape[-1], in_all.shape[-1]
     shapes = [(rows, 8 * wide), (rows, 8 * narrow), (share2, width), (owned, width)]
     return pl.pallas_call(
-        functools.partial(settle_kernel, lines),
+        functools.partial(settle_kernel, lines, straight),
         grid=(steps,),
         in_specs=[
             pl.BlockSpec((2, 4, r, wide), lambda i: (0, 0, i, 0)),
@@ -1347,6 +1511,73 @@
         ),
         name="settle",
     )(up_all, in_all, down_all, chan[:owned])
+
+
+def act_back_kernel(cot, down, hidden, out):
+    part = down.shape[0]
+    grad = lax.dot_general(
+        cot[...], down[...], (((1,), (1,)), ((), ())), preferred_element_type=F32
+    )
+    gelu, slope = gelu_parts(hidden[:, :part])
+    out[:, :part] = (grad * hidden[:, part:] * slope).astype(BF)
+    out[:, part:] = (grad * gelu).astype(BF)
+
+
+def act_back(cot, down, hidden):
+    tokens, width = cot.shape
+    part = down.shape[0]
+    rows = 256
+    return pl.pallas_call(
+        act_back_kernel,
+        grid=(tokens // rows,),
+        in_specs=[
+            pl.BlockSpec((rows, width), lambda i: (i, 0)),
+            pl.BlockSpec((part, width), lambda i: (0, 0), pipeline_mode=pl.Buffered(1)),
+            pl.BlockSpec((rows, 2 * part), lambda i: (i, 0)),
+        ],
+        out_specs=pl.BlockSpec((rows, 2 * part), lambda i: (i, 0)),
+        out_shape=jax.ShapeDtypeStruct((tokens, 2 * part), BF),
+        compiler_params=pltpu.CompilerParams(vmem_limit_bytes=40 << 20),
+        cost_estimate=pl.CostEstimate(
+            flops=2 * tokens * width * part, bytes_accessed=30 << 20, transcendentals=0
+        ),
+        name="act_back",
+    )(cot, down, hidden)
+
+
+def act_kernel(two, up, hidden, out):
+    part = out.shape[1]
+    value = jnp.dot(two[...], up[...], preferred_element_type=F32)
+    hidden[...] = value
+    gelu, _ = gelu_parts(value[:, :part])
+    out[...] = (gelu * value[:, part:]).astype(BF)
+
+
+def act(two, up):
+    tokens, width = two.shape
+    wide = up.shape[1]
+    rows = 256
+    return pl.pallas_call(
+        act_kernel,
+        grid=(tokens // rows,),
+        in_specs=[
+            pl.BlockSpec((rows, width), lambda i: (i, 0)),
+            pl.BlockSpec((width, wide), lambda i: (0, 0), pipeline_mode=pl.Buffered(1)),
+        ],
+        out_specs=[
+            pl.BlockSpec((rows, wide), lambda i: (i, 0)),
+            pl.BlockSpec((rows, wide // 2), lambda i: (i, 0)),
+        ],
+        out_shape=[
+            jax.ShapeDtypeStruct((tokens, wide), F32),
+            jax.ShapeDtypeStruct((tokens, wide // 2), BF),
+        ],
+        compiler_params=pltpu.CompilerParams(vmem_limit_bytes=40 << 20),
+        cost_estimate=pl.CostEstimate(
+            flops=2 * tokens * width * wide, bytes_accessed=30 << 20, transcendentals=0
+        ),
+        name="act",
+    )(two, up)
 
 
 def on_device(
@@ -1382,24 +1613,25 @@
     rows = mix_in.shape[0]
 
     per = owners // 8
-    by_half = mix_in.reshape(rows, 2, 2, 4, own)
-    by_half = lax.dynamic_index_in_dim(by_half, half, 2, keepdims=False)
-    mix_sent = jnp.moveaxis(by_half, 2, 0).reshape(4, rows, 2 * own)
-    by_half = mlp_in.reshape(rows, 2 * lines, 4, 2, share)
-    by_half = lax.dynamic_index_in_dim(by_half, half, 3, keepdims=False)
-    up_sent = jnp.moveaxis(by_half, 2, 0).reshape(4, rows, 2 * lines * share)
+    owned = channels // owners
+    straight = owned == block_size
+    up_sent, mix_sent = pick(mlp_in, mix_in, lines, straight)
     small = jnp.concatenate([conv_par.T, gate_bias.T, decay[:, None], gate_w], axis=1)
     used = small.shape[1]
     small = jnp.pad(small, ((0, 0), (0, -used % 128)))
     tiny = jnp.concatenate([mix_gain.astype(F32), mlp_gain.astype(F32), seg_ids.astype(F32)])
     tiny = jnp.pad(tiny, (0, -tiny.shape[0] % 1024)).reshape(-1, 128)
-    tok_all, halo, in_matrix, up_rows, packed, out_matrix, tiny = spread_inputs(
-        tokens, mix_sent, up_sent, small, out_proj, tiny, lines, per
-    )
-    all_cot = plane_gather(cotangent)
-    tok_all, all_cot = lax.optimization_barrier((tok_all, all_cot))
+    tok_all, halo, in_matrix, up_rows, packed, tiny = spread_inputs(
+        tokens, mix_sent, up_sent, small, tiny, lines, per, straight
+    )
+    up_matrix = lax.all_gather(up_rows.reshape(4 * rows, -1), "l", axis=0, tiled=True)
+    if straight:
+        out_matrix = lax.all_gather(out_proj, "l", axis=0, tiled=True)
+        out_matrix = lax.dynamic_slice_in_dim(out_matrix, half * own, own, 0)
+    else:
+        out_matrix = lax.all_gather(out_proj, SHARD, axis=0, tiled=True)
+        out_matrix = lax.dynamic_slice_in_dim(out_matrix, mine * own, own, 0)
     in_matrix = in_matrix.reshape(-1, 2 * own)
-    out_matrix = out_matrix.reshape(own, width)
     packed = packed.reshape(own, -1)
     tiny = tiny.transpose(0, 3, 2, 1, 4, 5).reshape(2, owners, -1)
     gain_one = tiny[0, :, :rows].reshape(-1)
@@ -1408,14 +1640,11 @@
     decay_own = packed[:, 7].astype(F32)
     chan = packed[:, :8].T.astype(F32)
     chan = chan.at[7].set(-DECAY_RATE * jax.nn.softplus(-decay_own))
-    gates = packed[:, 8:used].reshape(blocks, block_size, 2, block_size)
+    place = lax.broadcasted_iota(jnp.int32, (own, own), 0) // block_size
+    place = place == lax.broadcasted_iota(jnp.int32, (own, own), 1) // block_size
     gate_r, gate_i = (
-        lax.dynamic_update_slice(
-            jnp.pad(gates[0, :, side], ((0, own - block_size), (0, own - block_size))),
-            gates[1, :, side],
-            (block_size, block_size),
-        )
-        for side in range(2)
+        jnp.where(place, jnp.concatenate([packed[:, at : at + block_size]] * blocks, axis=1), 0)
+        for at in (8, 8 + block_size)
     )
 
     ids = lax.dynamic_index_in_dim(ids_all, line, 1, keepdims=False)
@@ -1433,44 +1662,35 @@
     for offset in range(2, 4):
         fac.append(fac[-1] * same[:, 3 - offset : 3 - offset + run])
     fac = jnp.stack(fac + [keep], axis=-1).reshape(plane, 4)
-    all_one, branch, conv_in, conv_out, pa, pb, ends = mix_forward(
-        tok_all, halo, in_matrix, gain_one, chan, gate_r, gate_i, fac
+    all_one, branch, conv_in, conv_out, pa, pb, ends, all_cot = mix_forward(
+        tok_all, halo, in_matrix, gain_one, chan, gate_r, gate_i, fac, cotangent
     )
     all_one = all_one.reshape(plane, width)
+    all_cot = all_cot.reshape(plane, width)
+    ends, out_matrix = lax.optimization_barrier((ends, out_matrix))
     state_in = line_start(ends, lines, False, 5)
-    up_rows = up_rows.reshape(4 * rows, 2, -1)
-    first_up = lax.all_gather(up_rows[:, 0], "l", axis=0, tiled=True)
-    later, down_rows, state_in = lax.optimization_barrier((up_rows[:, 1], mlp_out, state_in))
-    second_up = lax.all_gather(later, "l", axis=0, tiled=True)
+    down_rows, state_in = lax.optimization_barrier((mlp_out, state_in))
     down_matrix = lax.all_gather(
         lax.dynamic_slice_in_dim(down_rows, half * share, share, 0), "l", axis=0, tiled=True
     )
     state = pb.reshape(2, run, own) + pa.reshape(2, run, own) * state_in[:, :1]
     mixed = (state * jax.nn.gelu(branch.reshape(2, run, own))).astype(BF).reshape(plane, own)
-    partial = jnp.dot(mixed, out_matrix, preferred_element_type=F32).astype(BF)
-    residual, all_two = plane_sum(partial, tokens, None, gain_two, 1)
-    gate_part = jnp.dot(all_two, first_up, preferred_element_type=F32)
-    up_part = jnp.dot(all_two, second_up, preferred_element_type=F32)
-    activated = gated_product(gate_part, up_part).astype(BF)
+    residual, all_two = plane_sum(mixed, out_matrix, tokens, None, gain_two, 1)
+    hidden, activated = act(all_two, up_matrix)
+    down_grad = contract_rows(activated, all_cot).astype(BF)
+    down_grad, cot = lax.optimization_barrier((down_grad, all_cot))
+    down_line = lax.psum_scatter(down_grad, "l", scatter_dimension=0, tiled=True)
+    hidden_grad = act_back(cot, down_matrix, hidden)
+    up_grad = contract_rows(all_two, hidden_grad).astype(BF)
+    up_grad, hidden_grad = lax.optimization_barrier((up_grad, hidden_grad))
+    up_line = lax.psum_scatter(up_grad, "l", scatter_dimension=0, tiled=True)
+    residual_grad, gain_two_grad, all_res = plane_sum(
+        hidden_grad, up_matrix, residual, cotangent, gain_two, 2
+    )
+    activated, all_res = lax.optimization_barrier((activated, all_res))
     out_partial = jnp.dot(activated, down_matrix, preferred_element_type=F32).astype(BF)
-    out_partial, all_cot = lax.optimization_barrier((out_partial, all_cot))
-    out_sum = plane_scatter(out_partial)
-
-    act_grad = times_transposed(all_cot, down_matrix)
-    _, act_pull = jax.vjp(gated_product, gate_part, up_part)
-    gate_back, up_back = (one.astype(BF) for one in act_pull(act_grad))
-    partial = times_transposed(gate_back, first_up) + times_transposed(up_back, second_up)
-    partial = partial.astype(BF)
-    down_grad = contract_rows(activated, all_cot).astype(BF)
-    hidden_grad = jnp.concatenate([gate_back, up_back], axis=1)
-    up_grad = contract_rows(all_two, hidden_grad).astype(BF)
-    partial, down_grad, up_grad, out_sum = lax.optimization_barrier(
-        (partial, down_grad, up_grad, out_sum)
-    )
-    output = (residual + out_sum.astype(F32)).astype(BF)
-    down_line = lax.psum_scatter(down_grad, "l", scatter_dimension=0, tiled=True)
-    up_line = lax.psum_scatter(up_grad, "l", scatter_dimension=0, tiled=True)
-    residual_grad, gain_two_grad, all_res = plane_sum(partial, residual, cotangent, gain_two, 2)
+    out_partial, all_res = lax.optimization_barrier((out_partial, all_res))
+    output = (residual + plane_scatter(out_partial).astype(F32)).astype(BF)
     out_grad = contract_rows(mixed, all_res)
     branch_grad, ta, tb, ends = mix_state(
         all_res, out_matrix, branch, pa, pb, state_in, conv_out, chan, gate_r, fac, length
@@ -1494,9 +1714,7 @@
         ]
     )
     gate_grad = gate_grad.transpose(0, 2, 1, 3).reshape(own, 2 * block_size)
-    partial = times_transposed(proj_grad, in_matrix).astype(BF)
     in_grad = contract_rows(all_one, proj_grad).astype(BF)
-    owned = channels // owners
     chan = jnp.concatenate(
         [out_grad, sums.T, gate_grad], axis=1
     ).astype(BF)
@@ -1505,7 +1723,8 @@
         chan.reshape(own // owned, owned, used), ((0, 0), (0, -owned % 16), (0, -used % 128))
     )
     input_grad, in_all, chan, up_all, down_all, gain_grads = tail(
-        partial,
+        proj_grad,
+        in_matrix,
         tokens,
         residual_grad,
         gain_one,
@@ -1515,9 +1734,10 @@
         up_line.reshape(4, rows, -1),
         down_line,
         lines,
+        straight,
     )
     up_grad, in_grad, down_grad, out_grad = settle(
-        up_all, in_all, down_all.reshape(2 * share, width), chan, owned, width, lines
+        up_all, in_all, down_all.reshape(2 * share, width), chan, owned, width, lines, straight
     )
     small = chan[:owned, width:used].astype(F32)
     gain_grads = lax.dynamic_slice_in_dim(gain_grads[:2], me * rows, rows, 1)

time: 866 us -> 718 us (0.83)
  matrix products: 148 us -> 56.7 us
  local copies, waits for them, and re-layouts: 96.1 us -> 55.9 us
  Pallas kernels: 579 us -> 562 us
    dot_general x7 -> x0, matrix products: 90.9 us -> none  [the longest x4 56.6 us: times_transposed(): lax.dot_general(left_in, matrix, (((1,), (1,)), ((), ())), preferred_elem...]
    pallas_call x3 -> x6, Pallas kernels: 333 us -> 292 us  [the longest x1 149 us: tail(): pl.pallas_call(functools.partial(tail_kernel, lines, cuts, straight), out...]
    unnamed x124 -> x72, local copies, waits for them, and re-layouts: 54.4 us -> 39.1 us
    pallas_call x2, Pallas kernels: 153 us -> 164 us  [plane_sum(): pl.pallas_call(functools.partial(plane_kernel, mode, cuts), out_shape=out...]
  transfers between devices with their start and end apart: 8 -> 7, of which waited for: 1 -> 0; matrix products, arithmetic and copies ran while one was open for 23% -> 13% of each run, Pallas kernels for 48% -> 79%
where the time goes in v4:
time: 718 us; the launch traced here: 710 us
  Pallas kernels  562 us (78%)
  matrix products  56.7 us (8%)
  local copies, waits for them, and re-layouts  55.9 us (8%)
  other arithmetic  16.8 us (2%)
  between operations  15.1 us (2%)
    pallas_call x2, Pallas kernels, plane_sum(): pl.pallas_call(functools.partial(plane_kernel, mode, cuts), out_shape=out...  164 us
    pallas_call x1, Pallas kernels, tail(): pl.pallas_call(functools.partial(tail_kernel, lines, cuts, straight), out...  149 us
    pallas_call x1, Pallas kernels, spread_inputs(): pl.pallas_call(functools.partial(start_kernel, lines, cuts, straight), ou...  103 us
    dot_general x4, matrix products, contract_rows(): lax.dot_general(left_in, right_in, (((0,), (0,)), ((), ())), preferred_el...  45.8 us
    pallas_call x1, Pallas kernels, mix_forward(): pl.pallas_call(mix_forward_kernel, grid=(2, steps), in_specs=[slots(width...  44.6 us
    unnamed x72, local copies, waits for them, and re-layouts  39.1 us
    pallas_call x2, Pallas kernels, line_start(): pl.pallas_call(functools.partial(line_kernel, lines, backward), out_shape...  26.7 us
    pallas_call x1, Pallas kernels, mix_gates(): pl.pallas_call(mix_gates_kernel, grid=(2, steps), in_specs=[rows(own), ro...  21.2 us
  transfers between devices with their start and end apart: 7, of which 0 were waited for; matrix products, arithmetic and copies ran while one was open for 13% of the time, Pallas kernels for 79%

profile of v4, /device:TPU:11, one launch (start us, length us, event | category | flops | bytes accessed | tf_op | source)
XLA Modules:
  0.0 710.3 jit_solution(418840649341292320)
XLA Ops:
  12.4 1.9 copy-done.11
  14.3 1.3 copy-done.19
  15.6 3.1 pick.1
  18.7 1.1 copy-done.17
  22.1 102.6 %spread.1 = (bf16[8,256,2048]{2,1,0:T(8,128)(2,1)}, bf16[2,8,2048]{2,1,0:T(8,128)(2,1)}, bf16[4,4,128,640]{3,2,1,0:T(8,128)(2,1)}, bf16[4,128,1536]{2,1,0:T(8,12...) custom-call(bf16[256,2048]{1,0:T(8,128)(2,1)} %refs_2_.3, bf16[4,128,640]{2,1,0:T(8,128)(2,1)} %copy-done.22, ...), custom_call_target="tpu_custom_call" | custom-call | flops 10485760 | bytes 209715200 | tf_op jit(solution)/shard_map/spread/pallas_call | solution.py:928
  126.3 1.1 fusion.26
  130.7 2.0 copy-done.13
  132.7 1.4 copy-done.25
  134.1 44.6 %mix_forward.1 = (bf16[8,256,2048]{2,1,0:T(8,128)(2,1)}, f32[2048,320]{1,0:T(8,128)S(1)}, bf16[2,1040,320]{2,1,0:T(8,128)(2,1)S(1)}, bf16[2048,320]{1,0:T(8,128)...) custom-call(bf16[8,256,2048]{2,1,0:T(8,128)(2,1)} %get-tuple-element, ...), custom_call_target="tpu_custom_call" | custom-call | flops 5368709120 | bytes 62914560 | tf_op jit(solution)/shard_map/mix_forward/pallas_call | solution.py:1318
  178.7 1.7 copy-done.2
  180.3 1.1 copy-done.4
  181.5 1.1 copy-done.15
  182.6 2.5 constant_dynamic-slice_fusion.2.refs_1_
  185.2 13.3 %line_5.1.refs_5_.refs_7_ = f32[2,8,320]{2,1,0:T(8,128)S(1)} custom-call(f32[2,16,320]{2,1,0:T(8,128)S(1)} %get-tuple-element.100.ends), custom_call_target="tpu_custom_call" | custom-call | tf_op jit(solution)/shard_map/line_5/pallas_call | solution.py:1275
  198.5 1.0 constant_dynamic-slice_fusion.1
  199.7 6.2 fusion.8.refs_0_
  205.9 79.0 %plane_forward_1.1 = (f32[256,2048]{1,0:T(8,128)}, bf16[8,256,2048]{2,1,0:T(8,128)(2,1)}) custom-call(bf16[2048,320]{1,0:T(8,128)(2,1)} %fusion.8.refs_0_, bf16[320,2048]{1,0:T(8,128)(2,1)} %constant_dynamic-slice_fusion.2.refs_1_, bf16[256,2048]{1,0:T(8,128)(2,1)} %refs_2_.3, f32[1,2048]{1,0:T(1,128)} %bitcast.128), custom_call_target="tpu_custom_call" | custom-call | flops 2684354560 | bytes 209715200 | tf_op jit(solution)/shard_map/plane_forward_1/pallas_call | solution.py:415
  285.0 2.8 copy-done.24
  287.8 17.0 %act.1 = (f32[2048,1536]{1,0:T(8,128)}, bf16[2048,768]{1,0:T(8,128)(2,1)S(1)}) custom-call(bf16[2048,2048]{1,0:T(8,128)(2,1)} %bitcast.131, bf16[2048,1536]{1,0:T(8,128)(2,1)S(1)} %copy-done.24), custom_call_target="tpu_custom_call" | custom-call | flops 12884901888 | bytes 31457280 | tf_op jit(solution)/shard_map/act/pallas_call | solution.py:1560
  304.7 1.7 copy-done.27
  306.4 10.4 %convolution_convert_fusion.2 = bf16[768,2048]{1,0:T(8,128)(2,1)} fusion(bf16[2048,768]{1,0:T(8,128)(2,1)S(1)} %get-tuple-element.114, bf16[2048,2048]{1,0:T(8,128)(2,1)} %bitcast.109), kind=kOutput, calls=%fused_computation.3 | convolution fusion | flops 6444023808 | bytes 14680064 | tf_op jit(solution)/shard_map/dot_general | solution.py:27
  317.3 1.9 copy-done.8
  319.2 14.7 %act_back.1.refs_0_ = bf16[2048,1536]{1,0:T(8,128)(2,1)S(1)} custom-call(bf16[2048,2048]{1,0:T(8,128)(2,1)} %bitcast.110, bf16[768,2048]{1,0:T(8,128)(2,1)S(1)} %copy-done.8, f32[2048,1536]{1,0:T(8,128)} %get-tuple-element.111.hidden), custom_call_target="tpu_custom_call" | custom-call | flops 6442450944 | bytes 31457280 | tf_op jit(solution)/shard_map/act_back/pallas_call | solution.py:1530
  333.9 2.7 copy-done.3
  336.6 15.1 %convolution_convert_fusion.1 = bf16[2048,1536]{1,0:T(8,128)(2,1)} fusion(bf16[2048,2048]{1,0:T(8,128)(2,1)S(1)} %bitcast.132, bf16[2048,1536]{1,0:T(8,128)(2,1)S(1)} %act_back.1.refs_0_), kind=kOutput, calls=%fused_computation.1 | convolution fusion | flops 12888047616 | bytes 20971520 | tf_op jit(solution)/shard_map/dot_general | solution.py:27
  351.8 85.0 %plane_back_2.1 = (f32[256,2048]{1,0:T(8,128)}, f32[8,2048]{1,0:T(8,128)}, bf16[8,256,2048]{2,1,0:T(8,128)(2,1)}) custom-call(bf16[2048,1536]{1,0:T(8,128)(2,1)} %copy-done.3, bf16[2048,1536]{1,0:T(8,128)(2,1)} %all-gather.6.cloned.1.call-done.up.refs_1_, f32[256,2048]{1,0:T(8,128)} %get-tuple-element.104.refs_2_, bf16[256,2048]{1,0:T(8,128)(2,1)} %refs_3_.1, ...), custom_call_target="tpu_custom_call" | custom-call | flops 12884901888 | bytes 209715200 | tf_op jit(solution)/shard_map/plane_back_2/pallas_call | solution.py:415
  436.7 10.9 %convolution_convert_fusion = bf16[2048,2048]{1,0:T(8,128)(2,1)} fusion(bf16[2048,768]{1,0:T(8,128)(2,1)} %copy-done.27, bf16[768,2048]{1,0:T(8,128)(2,1)S(1)} %copy-done.9), kind=kOutput, calls=%fused_computation | convolution fusion | flops 6446645248 | bytes 14680064 | tf_op jit(solution)/shard_map/dot_general | solution.py:1691
  447.9 1.1 copy-done.5
  449.1 1.3 copy-done.7
  450.4 13.9 %mix_state.1 = (bf16[2048,320]{1,0:T(8,128)(2,1)S(1)}, f32[2048,320]{1,0:T(8,128)S(1)}, f32[2048,320]{1,0:T(8,128)S(1)}, f32[2,16,320]{2,1,0:T(8,128)S(1)}) custom-call(bf16[2048,2048]{1,0:T(8,128)(2,1)} %bitcast.107, bf16[320,2048]{1,0:T(8,128)(2,1)S(1)} %copy-done.7, f32[2048,320]{1,0:T(8,128)} %copy-done.2, ...), custom_call_target="tpu_custom_call" | custom-call | flops 2684354560 | bytes 41943040 | tf_op jit(solution)/shard_map/mix_state/pallas_call | solution.py:1375
  464.3 1.7 copy-done.10
  466.0 13.4 %line_6.1.refs_2_ = f32[2,8,320]{2,1,0:T(8,128)S(1)} custom-call(f32[2,16,320]{2,1,0:T(8,128)S(1)} %get-tuple-element.121.ends), custom_call_target="tpu_custom_call" | custom-call | tf_op jit(solution)/shard_map/line_6/pallas_call | solution.py:1275
  479.4 21.2 %mix_gates.1 = (bf16[2048,640]{1,0:T(8,128)(2,1)S(1)}, f32[2,8,320]{2,1,0:T(8,128)S(1)}, f32[2,8,320]{2,1,0:T(8,128)S(1)}, f32[8,8,320]{2,1,0:T(8,128)S(1)}, f32[2,320,320]{2,1,0:T(8,128)S(1)}) custom-call(f32[2048,320]{1,0:T(8,128)S(1)} %get-tuple-element.119.refs_0_, f32[2048,320]{1,0:T(8,128)} %copy-done.10, f32[2,8,320]{2,1,0:T(8,128)S(1)} %line_6.1.refs_2_, ...), custom_call_target="tpu_custom_call" | custom-call | flops 1677721600 | bytes 41943040 | tf_op jit(solution)/shard_map/mix_gates/pallas_call | solution.py:1421
  500.6 1.5 copy-done.14
  502.2 1.9 collective-permute-start
  504.3 8.6 %convolution_convert_fusion.4 = bf16[320,2048]{1,0:T(8,128)(2,1)S(1)} fusion(bf16[2048,320]{1,0:T(8,128)(2,1)} %fusion.8.refs_0_, bf16[2048,2048]{1,0:T(8,128)(2,1)} %bitcast.108), kind=kOutput, calls=%fused_computation.16 | convolution fusion | flops 2685009920 | bytes 11010048 | tf_op jit(solution)/shard_map/dot_general | solution.py:27
  514.3 1.3 pad.23.refs_7_
  515.5 2.2 dynamic_update_slice.6
  517.7 1.6 dynamic_update_slice.7.refs_0_
  519.4 11.8 %convolution_convert_fusion.3 = bf16[2048,640]{1,0:T(8,128)(2,1)} fusion(bf16[2048,2048]{1,0:T(8,128)(2,1)} %bitcast.130, bf16[2048,640]{1,0:T(8,128)(2,1)} %dynamic_update_slice.7.refs_0_), kind=kOutput, calls=%fused_computation.4 | convolution fusion | flops 5370019840 | bytes 13631488 | tf_op jit(solution)/shard_map/dot_general | solution.py:27
  531.1 149.2 %tail.1 = (f32[256,2048]{1,0:T(8,128)}, bf16[2,4,128,640]{3,2,1,0:T(8,128)(2,1)}, bf16[160,2432]{1,0:T(8,128)(2,1)}, bf16[2,4,128,1536]{3,2,1,0:T(8,128)(2,1)}, ...) custom-call(bf16[2048,640]{1,0:T(8,128)(2,1)} %dynamic_update_slice.7.refs_0_, bf16[2048,640]{1,0:T(8,128)(2,1)} %bitcast.102, ...), custom_call_target="tpu_custom_call" | custom-call | flops 10485760 | bytes 209715200 | tf_op jit(solution)/shard_map/tail/pallas_call | solution.py:651
  684.4 1.9 copy-done.12
  686.3 1.4 copy-done.18
  687.7 1.3 copy-done.20
  689.0 1.1 copy-done.21
  690.2 5.2 settle.1
  696.7 3.2 add_convert_fusion
  699.9 3.1 copy.104
  (121 shorter events, 20.2 us)
Async XLA Ops:
  7.2 191.3 %copy-start = (bf16[384,2048]{1,0:T(8,128)(2,1)S(1)}, bf16[384,2048]{1,0:T(8,128)(2,1)}, u32[]{:S(2)}) copy-start(bf16[384,2048]{1,0:T(8,128)(2,1)} %param.28) | copy-start | bytes 4718596
  7.2 14.1 %copy-start.29 = (bf16[160,320]{1,0:T(8,128)(2,1)S(1)}, bf16[160,320]{1,0:T(8,128)(2,1)}, u32[]{:S(2)}) copy-start(bf16[160,320]{1,0:T(8,128)(2,1)} %param.22) | copy-start | bytes 307204
  7.2 175.4 %all-gather.4.cloned.1.call-start = ((), (), s32[]{:S(2)}) async-start(), calls=%async_computation.3 | async-start | bytes 3276800 | tf_op jit(solution)/shard_map/all_gather | solution.py:1629
  7.9 277.0 %all-gather.6.cloned.1.call-start = ((), (), s32[]{:S(2)}) async-start(), calls=%async_computation.4 | async-start | bytes 7864320 | tf_op jit(solution)/shard_map/all_gather | solution.py:1627
  12.4 1.9 copy-start.11
  14.3 1.3 copy-start.19
  18.7 1.1 copy-start.17
  19.9 0.8 copy-start.22
  124.7 5.5 copy-start.28
  124.7 6.0 copy-start.26
  124.7 192.6 %all-gather.8.cloned.1.call-start = ((), (), s32[]{:S(2)}) async-start(), calls=%async_computation.5 | async-start | bytes 3932160 | tf_op jit(solution)/shard_map/all_gather | solution.py:1673
  130.1 48.5 %copy-start.23 = (f32[1,16,128]{2,1,0:T(8,128)}, f32[1,16,128]{2,1,0:T(8,128)S(1)}, u32[]{:S(2)}) copy-start(f32[1,16,128]{2,1,0:T(8,128)S(1)} %get-tuple-element.209) | copy-start | bytes 24580
  130.7 2.0 copy-start.13
  132.7 1.4 copy-start.25
  178.7 1.7 copy-start.2
  180.3 1.1 copy-start.4
  181.5 1.1 copy-start.15
  199.5 331.7 %reduce-scatter.8.cloned.1.call-start = ((), (), s32[]{:S(2)}) async-start(), calls=%async_computation.8 | async-start | bytes 3932160 | tf_op jit(solution)/shard_map/reduce_scatter | solution.py:1682
  285.0 2.8 copy-start.24
  304.7 1.7 copy-start.27
  316.8 214.3 %reduce-scatter.6.cloned.1.call-start = ((), (), s32[]{:S(2)}) async-start(), calls=%async_computation.7 | async-start | bytes 7864320 | tf_op jit(solution)/shard_map/reduce_scatter | solution.py:1686
  317.3 1.9 copy-start.8
  319.2 17.4 %copy-start.30 = (bf16[8,256,2048]{2,1,0:T(8,128)(2,1)S(1)}, bf16[8,256,2048]{2,1,0:T(8,128)(2,1)}, u32[]{:S(2)}) copy-start(bf16[8,256,2048]{2,1,0:T(8,128)(2,1)} %get-tuple-element.105) | copy-start | bytes 25165828
  333.9 2.7 copy-start.3
  351.7 345.0 %reduce-scatter.4.cloned.1.call-start = ((), (), s32[]{:S(2)}) async-start(), calls=%async_computation.6 | async-start | bytes 9437184 | tf_op jit(solution)/shard_map/reduce_scatter | solution.py:47
  351.7 85.0 %copy-start.9 = (bf16[768,2048]{1,0:T(8,128)(2,1)S(1)}, bf16[768,2048]{1,0:T(8,128)(2,1)}, u32[]{:S(2)}) copy-start(bf16[768,2048]{1,0:T(8,128)(2,1)} %all-gather.8.cloned.1.call-done.down) | copy-start | bytes 9437188
  447.6 1.4 copy-start.5
  449.1 1.3 copy-start.7
  450.4 29.0 %copy-start.6 = (bf16[2048,320]{1,0:T(8,128)(2,1)S(1)}, bf16[2048,320]{1,0:T(8,128)(2,1)}, u32[]{:S(2)}) copy-start(bf16[2048,320]{1,0:T(8,128)(2,1)} %copy-done.4) | copy-start | bytes 3932164
  450.4 29.0 %copy-start.16 = (bf16[2,1040,320]{2,1,0:T(8,128)(2,1)S(1)}, bf16[2,1040,320]{2,1,0:T(8,128)(2,1)}, u32[]{:S(2)}) copy-start(bf16[2,1040,320]{2,1,0:T(8,128)(2,1)} %copy-done.15) | copy-start | bytes 3993604
  464.3 1.7 copy-start.10
  500.6 1.5 copy-start.14
  502.2 13.3 %collective-permute-start = (f32[2,8,320]{2,1,0:T(8,128)S(1)}, f32[2,8,320]{2,1,0:T(8,128)S(1)}, u32[]{:S(2)}, u32[]{:S(2)}) collective-permute-start(f32[2,8,320]{2,1,0:T(8,128)S(1)} %get-tuple-element.126), channel_id=1, source_target_pairs={{4,0},{8,4},{12,8},{5,1},{9,5},{13,9},{6,2},{10,6},{14,10},{7,3},{... | collective-permute-start | bytes 61448 | tf_op jit(solution)/shard_map/ppermute | solution.py:1702
  684.4 1.9 copy-start.12
  686.3 1.4 copy-start.18
  687.7 1.3 copy-start.20
  689.0 1.1 copy-start.21
  696.7 6.4 copy-start.1
Sparse Core Ops, SparseCore 0:
  9.6 70.5 all-gather.3
  124.8 115.0 all-gather.5
  242.1 63.0 all-gather.7
  316.9 57.5 reduce-scatter.7
  376.7 115.4 reduce-scatter.5
  495.5 78.3 reduce-scatter.3

commit v5 on v4

--- a/solution.py
+++ b/solution.py
@@ -331,10 +331,12 @@
     refs = list(refs)
     lhs_far, rhs_far, base_far = refs.pop(0), refs.pop(0), refs.pop(0)
     up_far = refs.pop(0) if mode == "back" else None
+    side_far = [refs.pop(0), refs.pop(0)] if mode == "back" else []
     gain_ref, out_far = refs.pop(0), refs.pop(0)
     gain_out = refs.pop(0) if mode == "back" else None
+    side_out = refs.pop(0) if mode == "back" else None
     all_ref, lhs, rhs, away, own, got, hop_a, hop_b, base_ref, out_ref = refs[:10]
-    up_ref = refs[10] if mode == "back" else None
+    up_ref, side_lhs, side_rhs, stage = refs[10:14] if mode == "back" else (None,) * 4
     mine, send_sems, recv_sems = refs[-3:]
     _, core, side_a, side_b = sides()
     wires = Wires(send_sems, recv_sems)
@@ -348,7 +350,23 @@
     loads = [wires.near(base_far, base_ref)]
     if mode == "back":
         loads.append(wires.near(up_far, up_ref))
-    part = out_ref.shape[0] // cuts
+    length = out_ref.shape[0]
+    part = length // cuts
+    beside = []
+    if mode == "back":
+        loads += [wires.near(side_far[0], side_lhs), wires.near(side_far[1], side_rhs)]
+        make_side = block_maker(side_lhs, side_rhs, length, False)
+        for block in range(8):
+            rows = pl.ds(block * length, length)
+            beside.append(wires.near(stage.at[block % 2], side_out.at[rows]))
+
+    def work(blocks):
+        for block in blocks if mode == "back" else ():
+            if block > 1:
+                beside[block - 2].wait()
+            make_side(block, stage.at[block % 2])
+            beside[block].start()
+
     stores = []
     for piece in range(cuts):
         rows = pl.ds(piece * part, part)
@@ -358,24 +376,27 @@
     for copy in loads:
         copy.start()
     total.first_side()
+    for copy in loads:
+        copy.wait()
+    work(range(3))
     total.second_side()
+    work(range(3, 5))
     if mode == "back":
         gain_out[...] = jnp.zeros_like(gain_out)
         use = back_rows(base_ref, up_ref, gain_ref, out_ref, gain_out, mine)
     else:
         use = forward_rows(base_ref, gain_ref, out_ref, mine)
-    for copy in loads:
-        copy.wait()
     for piece in range(cuts):
         total.finish(piece, use)
         spread.start(piece)
     for copy in stores:
         copy.start()
+    work(range(5, 8))
     spread.forward("a", ("ab", "ac"))
     spread.forward("b", ("bc",))
     spread.forward("ab", ("dc",))
     spread.finish()
-    for copy in stores:
+    for copy in stores + beside[6:]:
         copy.wait()
     total.drain()
 
@@ -392,7 +413,7 @@
     ]
 
 
-def plane_sum(lhs, rhs, base, up, gain, number):
+def plane_sum(lhs, rhs, base, up, gain, number, side=()):
     mode = "forward" if up is None else "back"
     length, width = base.shape
     cuts = 2
@@ -401,16 +422,19 @@
     outs, out_specs = [jax.ShapeDtypeStruct((length, width), F32)], [left]
     scratch = [pltpu.VMEM((length, width), base.dtype), pltpu.VMEM((length, width), F32)]
     if mode == "back":
-        args.append(up)
-        specs.append(left)
+        args += [up, *side]
+        specs += [left, left, left]
         outs.append(jax.ShapeDtypeStruct((8, width), F32))
-        out_specs.append(vmem)
+        outs.append(jax.ShapeDtypeStruct((8 * length, width), BF))
+        out_specs += [vmem, left]
         scratch.append(pltpu.VMEM((length, width), up.dtype))
+        scratch += [pltpu.VMEM(one.shape, BF) for one in side]
+        scratch.append(pltpu.VMEM((2, length, width), BF))
     args.append(gain.reshape(1, width))
     specs.append(vmem)
     outs.append(jax.ShapeDtypeStruct((8, length, width), BF))
     out_specs.append(left)
-    sems = cuts * (4 + 3 + 8 + 1) + 4
+    sems = cuts * (4 + 3 + 8 + 1) + 14
     got = list(
         pl.pallas_call(
             functools.partial(plane_kernel, mode, cuts),
@@ -438,13 +462,13 @@
 
 
 def tail_kernel(lines, cuts, straight, *refs):
-    (lhs_far, rhs_far, base_far, up_far, gain_ref, other_gain, in_ref, chan_ref, upz, downz) = refs[:10]
-    (out_far, in_all, chan_out, up_all, down_all, gains) = refs[10:16]
+    (lhs_far, rhs_far, base_far, up_far, gain_ref, other_gain, in_ref, chan_ref, upz) = refs[:9]
+    (out_far, in_all, chan_out, up_all, gains) = refs[9:14]
     base_ref, up_ref, out_ref = refs[-3:]
     refs = refs[:-3]
-    (lhs, rhs, away, own, got, hop_a, hop_b) = refs[16:23]
-    (gain_out, in_own, in_left, in_right) = refs[23:27]
-    (chan_own, chan_left, chan_right, chan_got, tiny, tiny_line, send_sems, recv_sems) = refs[27:]
+    (lhs, rhs, away, own, got, hop_a, hop_b) = refs[14:21]
+    (gain_out, in_own, in_left, in_right) = refs[21:25]
+    (chan_own, chan_left, chan_right, chan_got, tiny, tiny_line, send_sems, recv_sems) = refs[25:]
     me, core, side_a, side_b = sides()
     x, l, y, c = me
     k = 2 * y + c
@@ -490,7 +514,8 @@
     for copy in loads:
         copy.start()
     up_copies = deliver(lambda to: upz.at[to], up_all)
-    down_copies = [wires.near(downz, down_all.at[x]), wires.far(downz, down_all.at[x], twin)]
+    for copy in up_copies[:5]:
+        copy.start()
     load_in.wait()
     load_chan.wait()
     for copy in operands:
@@ -532,7 +557,7 @@
     total.second_side()
     for q in reversed(range(1, lines - 2)):
         send_ends(q)
-    for copy in down_copies + up_copies:
+    for copy in up_copies[5:]:
         copy.start()
     for q in reversed(range(1, lines - 1)):
         pass_right(q)
@@ -621,7 +646,7 @@
     gains[...] = tiny_line[0]
     for q in range(1, lines):
         gains[...] += tiny_line[q]
-    for copies in (in_copies, up_copies, down_copies, stores):
+    for copies in (in_copies, up_copies, stores):
         for copy in copies:
             copy.wait()
 
@@ -640,7 +665,7 @@
     total.drain()
 
 
-def tail(lhs, rhs, base, up, gain, other_gain, in_grad, chan, upz, downz, lines, straight):
+def tail(lhs, rhs, base, up, gain, other_gain, in_grad, chan, upz, lines, straight):
     length, width = base.shape
     cuts = 2
     vmem, left = pl.BlockSpec(memory_space=pltpu.VMEM), pl.BlockSpec(memory_space=pl.ANY)
@@ -655,11 +680,10 @@
             jax.ShapeDtypeStruct((2, 4, rows, in_grad.shape[1]), BF),
             jax.ShapeDtypeStruct(chan.shape[1:], BF),
             jax.ShapeDtypeStruct((2,) + upz.shape, BF),
-            jax.ShapeDtypeStruct((2,) + downz.shape, BF),
             jax.ShapeDtypeStruct((8, width), F32),
         ],
-        in_specs=[left, left, left, left, vmem, vmem, left, left, left, left],
-        out_specs=[left, left, left, left, left, vmem],
+        in_specs=[left, left, left, left, vmem, vmem, left, left, left],
+        out_specs=[left, left, left, left, vmem],
         scratch_shapes=sum_scratch(lhs, rhs, length, width)
         + [pltpu.VMEM((8, width), F32)]
         + [pltpu.VMEM(pieces.shape, BF)] * 3
@@ -681,7 +705,7 @@
             flops=20 * base.size, bytes_accessed=400 * base.size, transcendentals=0
         ),
         name="tail",
-    )(lhs, rhs, base, up, gain.reshape(1, width), other_gain, pieces, chan, upz, downz)
+    )(lhs, rhs, base, up, gain.reshape(1, width), other_gain, pieces, chan, upz)
 
 
 def owner_of(x, k, i, per, straight):
@@ -1133,12 +1157,23 @@
 
 
 def mix_state_kernel(*refs):
-    (res, weight, branch, pa, pb, state_in, conv_out, chan_ref, gate_r, fac) = refs[:10]
-    (branch_grad, ta, tb, ends) = refs[10:14]
-    (coef, grad, carry, first_coef) = refs[14:]
+    (res, weight, branch, pa, pb, state_in, conv_out, chan_ref, gate_r, fac, down) = refs[:11]
+    (branch_grad, ta, tb, ends, down_all) = refs[11:16]
+    (coef, grad, carry, first_coef, send_sems, recv_sems) = refs[16:]
     length, own = branch.shape
     chan = chan_ref[...]
     turn = pl.program_id(1)
+    x, l, y, c = (lax.axis_index(name) for name in EVERY)
+    twin = (1 - x, l, y, c)
+    wires = Wires(send_sems, recv_sems)
+    copies = [wires.near(down, down_all.at[x]), wires.far(down, down_all.at[x], twin)]
+    step = pl.program_id(0) * pl.num_programs(1) + turn
+
+    @pl.when(step == 0)
+    def _():
+        greet([twin])
+        for copy in copies:
+            copy.start()
 
     @pl.when(turn == 0)
     def _():
@@ -1162,6 +1197,11 @@
     scan_tiles(length, True, coef, grad, ta, tb, carry)
     ends[0, 0:8] = first * carry[0]
     ends[0, 8:16] = first * carry[1]
+
+    @pl.when(step == 2 * pl.num_programs(1) - 1)
+    def _():
+        for copy in copies:
+            copy.wait()
 
 
 def mix_gates_kernel(*refs):
@@ -1367,7 +1407,7 @@
     )(tok_all, halo, weight, gain.reshape(1, width), chan, gate_r, gate_i, fac, cot)
 
 
-def mix_state(res, weight, branch, pa, pb, state_in, conv_out, chan, gate_r, fac, length):
+def mix_state(res, weight, branch, pa, pb, state_in, conv_out, chan, gate_r, fac, down, length):
     own, width = weight.shape
     run = res.shape[0] // 2
     steps, rows, slots, whole, held = mix_specs(run, length, own, True)
@@ -1386,26 +1426,38 @@
             whole(8, own),
             whole(own, own),
             rows(fac.shape[1]),
-        ],
-        out_specs=[rows(own), rows(own), rows(own), held(16, own)],
+            pl.BlockSpec(memory_space=pl.ANY),
+        ],
+        out_specs=[
+            rows(own),
+            rows(own),
+            rows(own),
+            held(16, own),
+            pl.BlockSpec(memory_space=pl.ANY),
+        ],
         out_shape=[
             jax.ShapeDtypeStruct((2 * run, own), BF),
             flat,
             flat,
             jax.ShapeDtypeStruct((2, 16, own), F32),
+            jax.ShapeDtypeStruct((2,) + down.shape, BF),
         ],
         scratch_shapes=[
             pltpu.VMEM((length, own), F32),
             pltpu.VMEM((length, own), F32),
             pltpu.VMEM((2, 8, own), F32),
             pltpu.VMEM((8, own), F32),
-        ],
-        compiler_params=pltpu.CompilerParams(vmem_limit_bytes=40 << 20),
+            pltpu.SemaphoreType.DMA((2,)),
+            pltpu.SemaphoreType.DMA((2,)),
+        ],
+        compiler_params=pltpu.CompilerParams(
+            collective_id=8, has_side_effects=True, vmem_limit_bytes=40 << 20
+        ),
         cost_estimate=pl.CostEstimate(
             flops=4 * run * width * own, bytes_accessed=40 << 20, transcendentals=0
         ),
         name="mix_state",
-    )(res, weight, branch, pa, pb, state_in, conv_out, chan, gate_r, fac)
+    )(res, weight, branch, pa, pb, state_in, conv_out, chan, gate_r, fac, down)
 
 
 def mix_gates(
@@ -1684,16 +1736,13 @@
     up_grad = contract_rows(all_two, hidden_grad).astype(BF)
     up_grad, hidden_grad = lax.optimization_barrier((up_grad, hidden_grad))
     up_line = lax.psum_scatter(up_grad, "l", scatter_dimension=0, tiled=True)
-    residual_grad, gain_two_grad, all_res = plane_sum(
-        hidden_grad, up_matrix, residual, cotangent, gain_two, 2
-    )
-    activated, all_res = lax.optimization_barrier((activated, all_res))
-    out_partial = jnp.dot(activated, down_matrix, preferred_element_type=F32).astype(BF)
-    out_partial, all_res = lax.optimization_barrier((out_partial, all_res))
+    residual_grad, gain_two_grad, out_partial, all_res = plane_sum(
+        hidden_grad, up_matrix, residual, cotangent, gain_two, 2, (activated, down_matrix)
+    )
     output = (residual + plane_scatter(out_partial).astype(F32)).astype(BF)
     out_grad = contract_rows(mixed, all_res)
-    branch_grad, ta, tb, ends = mix_state(
-        all_res, out_matrix, branch, pa, pb, state_in, conv_out, chan, gate_r, fac, length
+    branch_grad, ta, tb, ends, down_all = mix_state(
+        all_res, out_matrix, branch, pa, pb, state_in, conv_out, chan, gate_r, fac, down_line, length
     )
     from_right = line_start(ends, lines, True, 6)
     proj_grad, last_rows, edges, sums, gate_grad = mix_gates(
@@ -1722,7 +1771,7 @@
     chan = jnp.pad(
         chan.reshape(own // owned, owned, used), ((0, 0), (0, -owned % 16), (0, -used % 128))
     )
-    input_grad, in_all, chan, up_all, down_all, gain_grads = tail(
+    input_grad, in_all, chan, up_all, gain_grads = tail(
         proj_grad,
         in_matrix,
         tokens,
@@ -1732,7 +1781,6 @@
         in_grad,
         chan,
         up_line.reshape(4, rows, -1),
-        down_line,
         lines,
         straight,
     )

time: 718 us -> 720 us (level)
  the two profiles are of different devices: /device:TPU:11 before, /device:TPU:24 now
where the time goes in v5:
time: 720 us; the launch traced here: 714 us
  Pallas kernels  576 us (80%)
  local copies, waits for them, and re-layouts  59 us (8%)
  matrix products  44.4 us (6%)
  other arithmetic  16.8 us (2%)
  between operations  14.9 us (2%)
    pallas_call x2, Pallas kernels, plane_sum(): pl.pallas_call(functools.partial(plane_kernel, mode, cuts), out_shape=out...  164 us
    pallas_call x1, Pallas kernels, tail(): pl.pallas_call(functools.partial(tail_kernel, lines, cuts, straight), out...  158 us
    pallas_call x1, Pallas kernels, spread_inputs(): pl.pallas_call(functools.partial(start_kernel, lines, cuts, straight), ou...  100 us
    pallas_call x1, Pallas kernels, mix_forward(): pl.pallas_call(mix_forward_kernel, grid=(2, steps), in_specs=[slots(width...  44.6 us
    dot_general x4, matrix products, contract_rows(): lax.dot_general(left_in, right_in, (((0,), (0,)), ((), ())), preferred_el...  44.4 us
    unnamed x76, local copies, waits for them, and re-layouts  38.6 us
    pallas_call x2, Pallas kernels, line_start(): pl.pallas_call(functools.partial(line_kernel, lines, backward), out_shape...  25.9 us
    pallas_call x1, Pallas kernels, mix_state(): pl.pallas_call(mix_state_kernel, grid=(2, steps), in_specs=[rows(width),...  21.3 us
  transfers between devices with their start and end apart: 7, of which 0 were waited for; matrix products, arithmetic and copies ran while one was open for 11% of the time, Pallas kernels for 81%

profile of v5, /device:TPU:24, one launch (start us, length us, event | category | flops | bytes accessed | tf_op | source)
XLA Modules:
  0.0 713.6 jit_solution(12022230739430942444)
XLA Ops:
  12.4 1.9 copy-done.10
  14.3 1.3 copy-done.19
  15.6 3.1 pick.1
  18.7 1.1 copy-done.16
  22.1 100.3 %spread.1 = (bf16[8,256,2048]{2,1,0:T(8,128)(2,1)}, bf16[2,8,2048]{2,1,0:T(8,128)(2,1)}, bf16[4,4,128,640]{3,2,1,0:T(8,128)(2,1)}, bf16[4,128,1536]{2,1,0:T(8,12...) custom-call(bf16[256,2048]{1,0:T(8,128)(2,1)} %refs_2_.3, bf16[4,128,640]{2,1,0:T(8,128)(2,1)} %copy-done.23, ...), custom_call_target="tpu_custom_call" | custom-call | flops 10485760 | bytes 209715200 | tf_op jit(solution)/shard_map/spread/pallas_call | solution.py:952
  124.0 1.1 fusion.26
  128.4 1.7 copy-done.12
  130.2 1.3 copy-done.26
  131.5 44.6 %mix_forward.1 = (bf16[8,256,2048]{2,1,0:T(8,128)(2,1)}, f32[2048,320]{1,0:T(8,128)S(1)}, bf16[2,1040,320]{2,1,0:T(8,128)(2,1)S(1)}, bf16[2048,320]{1,0:T(8,128)...) custom-call(bf16[8,256,2048]{2,1,0:T(8,128)(2,1)} %get-tuple-element, ...), custom_call_target="tpu_custom_call" | custom-call | flops 5368709120 | bytes 62914560 | tf_op jit(solution)/shard_map/mix_forward/pallas_call | solution.py:1358
  176.1 1.7 copy-done.2
  177.8 1.2 copy-done.4
  179.0 1.1 copy-done.14
  180.1 2.5 constant_dynamic-slice_fusion.2.refs_1_
  182.6 13.5 %line_5.1.refs_5_.refs_7_ = f32[2,8,320]{2,1,0:T(8,128)S(1)} custom-call(f32[2,16,320]{2,1,0:T(8,128)S(1)} %get-tuple-element.97.ends), custom_call_target="tpu_custom_call" | custom-call | tf_op jit(solution)/shard_map/line_5/pallas_call | solution.py:1315
  197.4 6.2 fusion.8.refs_0_
  203.6 79.8 %plane_forward_1.1 = (f32[256,2048]{1,0:T(8,128)}, bf16[8,256,2048]{2,1,0:T(8,128)(2,1)}) custom-call(bf16[2048,320]{1,0:T(8,128)(2,1)} %fusion.8.refs_0_, bf16[320,2048]{1,0:T(8,128)(2,1)} %constant_dynamic-slice_fusion.2.refs_1_, bf16[256,2048]{1,0:T(8,128)(2,1)} %refs_2_.3, f32[1,2048]{1,0:T(1,128)} %bitcast.130), custom_call_target="tpu_custom_call" | custom-call | flops 2684354560 | bytes 209715200 | tf_op jit(solution)/shard_map/plane_forward_1/pallas_call | solution.py:439
  283.5 2.8 copy-done.25
  286.3 17.0 %act.1 = (f32[2048,1536]{1,0:T(8,128)}, bf16[2048,768]{1,0:T(8,128)(2,1)S(1)}) custom-call(bf16[2048,2048]{1,0:T(8,128)(2,1)} %bitcast.133, bf16[2048,1536]{1,0:T(8,128)(2,1)S(1)} %copy-done.25), custom_call_target="tpu_custom_call" | custom-call | flops 12884901888 | bytes 31457280 | tf_op jit(solution)/shard_map/act/pallas_call | solution.py:1612
  303.3 1.7 copy-done.28
  304.9 10.3 %convolution_convert_fusion.1 = bf16[768,2048]{1,0:T(8,128)(2,1)} fusion(bf16[2048,768]{1,0:T(8,128)(2,1)S(1)} %get-tuple-element.104.refs_4_, bf16[2048,2048]{1,0:T(8,128)(2,1)} %bitcast.110), kind=kOutput, calls=%fused_computation.2 | convolution fusion | flops 6444023808 | bytes 14680064 | tf_op jit(solution)/shard_map/dot_general | solution.py:27
  315.6 1.9 copy-done.8
  317.5 15.2 %act_back.1.refs_0_ = bf16[2048,1536]{1,0:T(8,128)(2,1)S(1)} custom-call(bf16[2048,2048]{1,0:T(8,128)(2,1)} %bitcast.111, bf16[768,2048]{1,0:T(8,128)(2,1)S(1)} %copy-done.8, f32[2048,1536]{1,0:T(8,128)} %get-tuple-element.108.hidden), custom_call_target="tpu_custom_call" | custom-call | flops 6442450944 | bytes 31457280 | tf_op jit(solution)/shard_map/act_back/pallas_call | solution.py:1582
  332.7 2.7 copy-done.3
  335.4 15.1 %convolution_convert_fusion = bf16[2048,1536]{1,0:T(8,128)(2,1)} fusion(bf16[2048,2048]{1,0:T(8,128)(2,1)S(1)} %bitcast.134, bf16[2048,1536]{1,0:T(8,128)(2,1)S(1)} %act_back.1.refs_0_), kind=kOutput, calls=%fused_computation | convolution fusion | flops 12888047616 | bytes 20971520 | tf_op jit(solution)/shard_map/dot_general | solution.py:27
  350.6 84.3 %plane_back_2.1 = (f32[256,2048]{1,0:T(8,128)}, f32[8,2048]{1,0:T(8,128)}, bf16[2048,2048]{1,0:T(8,128)(2,1)}, bf16[8,256,2048]{2,1,0:T(8,128)(2,1)}) custom-call(bf16[2048,1536]{1,0:T(8,128)(2,1)} %copy-done.3, bf16[2048,1536]{1,0:T(8,128)(2,1)} %all-gather.6.cloned.1.call-done.up.refs_1_, f32[256,2048]{1,0:T(8,128)} %get-tuple-element.101.refs_2_, ...), custom_call_target="tpu_custom_call" | custom-call | flops 12884901888 | bytes 209715200 | tf_op jit(solution)/shard_map/plane_back_2/pallas_call | solution.py:439
  435.2 1.2 copy-done.29
  436.3 1.5 copy.89
  437.9 7.9 %convolution_convert_fusion.3 = bf16[2,160,2048]{2,1,0:T(8,128)(2,1)} fusion(bf16[2,160,2048]{2,1,0:T(8,128)(2,1)} %bitcast.120, bf16[2048,2048,1]{1,0,2:T(8,128)(2,1)} %bitcast.108), kind=kOutput, calls=%fused_computation.15 | convolution fusion | flops 2685009920 | bytes 11010048 | tf_op jit(solution)/shard_map/dot_general | solution.py:27
  445.7 1.3 copy-done.7
  447.1 1.1 copy-done.22
  448.2 21.3 %mix_state.1 = (bf16[2048,320]{1,0:T(8,128)(2,1)S(1)}, f32[2048,320]{1,0:T(8,128)S(1)}, f32[2048,320]{1,0:T(8,128)S(1)}, f32[2,16,320]{2,1,0:T(8,128)S(1)}, bf16[2,192,2048]{2,1,0:T(8,128)(2,1)S(1)}) custom-call(bf16[2048,2048]{1,0:T(8,128)(2,1)} %bitcast.109, bf16[320,2048]{1,0:T(8,128)(2,1)S(1)} %copy-done.7, f32[2048,320]{1,0:T(8,128)} %copy-done.2, ...), custom_call_target="tpu_custom_call" | custom-call | flops 2684354560 | bytes 41943040 | tf_op jit(solution)/shard_map/mix_state/pallas_call | solution.py:1415
  469.5 1.7 copy-done.9
  471.2 12.4 %line_6.1.refs_2_ = f32[2,8,320]{2,1,0:T(8,128)S(1)} custom-call(f32[2,16,320]{2,1,0:T(8,128)S(1)} %get-tuple-element.116.ends), custom_call_target="tpu_custom_call" | custom-call | tf_op jit(solution)/shard_map/line_6/pallas_call | solution.py:1315
  483.7 21.0 %mix_gates.1 = (bf16[2048,640]{1,0:T(8,128)(2,1)S(1)}, f32[2,8,320]{2,1,0:T(8,128)S(1)}, f32[2,8,320]{2,1,0:T(8,128)S(1)}, f32[8,8,320]{2,1,0:T(8,128)S(1)}, f32[2,320,320]{2,1,0:T(8,128)S(1)}) custom-call(f32[2048,320]{1,0:T(8,128)S(1)} %get-tuple-element.114.refs_0_, f32[2048,320]{1,0:T(8,128)} %copy-done.9, f32[2,8,320]{2,1,0:T(8,128)S(1)} %line_6.1.refs_2_, ...), custom_call_target="tpu_custom_call" | custom-call | flops 1677721600 | bytes 41943040 | tf_op jit(solution)/shard_map/mix_gates/pallas_call | solution.py:1473
  504.6 1.5 copy-done.13
  506.2 1.3 collective-permute-start
  508.5 2.7 concatenate.40
  511.1 1.3 pad.23.refs_7_
  512.4 2.2 dynamic_update_slice.6
  514.6 1.6 dynamic_update_slice.7.refs_0_
  516.3 11.1 %convolution_convert_fusion.2 = bf16[2048,640]{1,0:T(8,128)(2,1)} fusion(bf16[2048,2048]{1,0:T(8,128)(2,1)} %bitcast.132, bf16[2048,640]{1,0:T(8,128)(2,1)} %dynamic_update_slice.7.refs_0_), kind=kOutput, calls=%fused_computation.3 | convolution fusion | flops 5370019840 | bytes 13631488 | tf_op jit(solution)/shard_map/dot_general | solution.py:27
  527.3 157.9 %tail.1 = (f32[256,2048]{1,0:T(8,128)}, bf16[2,4,128,640]{3,2,1,0:T(8,128)(2,1)}, bf16[160,2432]{1,0:T(8,128)(2,1)}, bf16[2,4,128,1536]{3,2,1,0:T(8,128)(2,1)}, f32[8,2048]{1,0:T(8,128)}) custom-call(bf16[2048,640]{1,0:T(8,128)(2,1)} %dynamic_update_slice.7.refs_0_, bf16[2048,640]{1,0:T(8,128)(2,1)} %bitcast.103, bf16[256,2048]{1,0:T(8,128)(2,1)} %refs_2_.3, ...), custom_call_target="tpu_custom_call" | custom-call | flops 10485760 | bytes 209715200 | tf_op jit(solution)/shard_map/tail/pallas_call | solution.py:676
  689.3 1.9 copy-done.11
  691.2 1.3 copy-done.20
  692.5 1.1 copy-done.21
  693.7 5.2 settle.1
  700.2 3.2 add_convert_fusion
  703.4 3.1 copy.109
  (125 shorter events, 20.3 us)
Async XLA Ops:
  7.2 189.0 %copy-start = (bf16[384,2048]{1,0:T(8,128)(2,1)S(1)}, bf16[384,2048]{1,0:T(8,128)(2,1)}, u32[]{:S(2)}) copy-start(bf16[384,2048]{1,0:T(8,128)(2,1)} %param.28) | copy-start | bytes 4718596
  7.2 14.1 %copy-start.31 = (bf16[160,320]{1,0:T(8,128)(2,1)S(1)}, bf16[160,320]{1,0:T(8,128)(2,1)}, u32[]{:S(2)}) copy-start(bf16[160,320]{1,0:T(8,128)(2,1)} %param.22) | copy-start | bytes 307204
  7.2 172.9 %all-gather.4.cloned.1.call-start = ((), (), s32[]{:S(2)}) async-start(), calls=%async_computation.3 | async-start | bytes 3276800 | tf_op jit(solution)/shard_map/all_gather | solution.py:1681
  7.9 275.5 %all-gather.6.cloned.1.call-start = ((), (), s32[]{:S(2)}) async-start(), calls=%async_computation.4 | async-start | bytes 7864320 | tf_op jit(solution)/shard_map/all_gather | solution.py:1679
  12.4 1.9 copy-start.10
  14.3 1.3 copy-start.19
  18.7 1.1 copy-start.16
  19.9 0.8 copy-start.23
  122.4 5.5 copy-start.30
  122.4 6.0 copy-start.27
  122.5 193.1 %all-gather.8.cloned.1.call-start = ((), (), s32[]{:S(2)}) async-start(), calls=%async_computation.5 | async-start | bytes 3932160 | tf_op jit(solution)/shard_map/all_gather | solution.py:1725
  127.9 48.2 %copy-start.24 = (f32[1,16,128]{2,1,0:T(8,128)}, f32[1,16,128]{2,1,0:T(8,128)S(1)}, u32[]{:S(2)}) copy-start(f32[1,16,128]{2,1,0:T(8,128)S(1)} %get-tuple-element.203) | copy-start | bytes 24580
  128.4 1.7 copy-start.12
  130.2 1.3 copy-start.26
  176.1 1.7 copy-start.2
  177.8 1.2 copy-start.4
  179.0 1.1 copy-start.14
  197.1 248.6 %reduce-scatter.6.cloned.1.call-start = ((), (), s32[]{:S(2)}) async-start(), calls=%async_computation.7 | async-start | bytes 3932160 | tf_op jit(solution)/shard_map/reduce_scatter | solution.py:1734
  283.5 2.9 copy-start.25
  303.3 1.7 copy-start.28
  315.3 212.0 %reduce-scatter.8.cloned.1.call-start = ((), (), s32[]{:S(2)}) async-start(), calls=%async_computation.8 | async-start | bytes 7864320 | tf_op jit(solution)/shard_map/reduce_scatter | solution.py:1738
  315.6 1.9 copy-start.8
  317.5 17.9 %copy-start.32 = (bf16[8,256,2048]{2,1,0:T(8,128)(2,1)S(1)}, bf16[8,256,2048]{2,1,0:T(8,128)(2,1)}, u32[]{:S(2)}) copy-start(bf16[8,256,2048]{2,1,0:T(8,128)(2,1)} %get-tuple-element.102) | copy-start | bytes 25165828
  332.7 2.7 copy-start.3
  350.5 349.6 %reduce-scatter.4.cloned.1.call-start = ((), (), s32[]{:S(2)}) async-start(), calls=%async_computation.6 | async-start | bytes 9437184 | tf_op jit(solution)/shard_map/reduce_scatter | solution.py:47
  434.9 1.5 copy-start.29
  437.9 7.9 %copy-start.5 = (bf16[2048,320]{1,0:T(8,128)(2,1)S(1)}, bf16[2048,320]{1,0:T(8,128)(2,1)}, u32[]{:S(2)}) copy-start(bf16[2048,320]{1,0:T(8,128)(2,1)} %copy-done.4) | copy-start | bytes 3932164
  445.7 1.3 copy-start.7
  447.1 1.1 copy-start.22
  448.2 35.4 %copy-start.6 = (bf16[2048,320]{1,0:T(8,128)(2,1)S(1)}, bf16[2048,320]{1,0:T(8,128)(2,1)}, u32[]{:S(2)}) copy-start(bf16[2048,320]{1,0:T(8,128)(2,1)} %copy-done.4) | copy-start | bytes 3932164
  448.2 35.5 %copy-start.15 = (bf16[2,1040,320]{2,1,0:T(8,128)(2,1)S(1)}, bf16[2,1040,320]{2,1,0:T(8,128)(2,1)}, u32[]{:S(2)}) copy-start(bf16[2,1040,320]{2,1,0:T(8,128)(2,1)} %copy-done.14) | copy-start | bytes 3993604
  469.5 1.7 copy-start.9
  471.2 33.4 %copy-start.17 = (bf16[2,192,2048]{2,1,0:T(8,128)(2,1)}, bf16[2,192,2048]{2,1,0:T(8,128)(2,1)S(1)}, u32[]{:S(2)}) copy-start(bf16[2,192,2048]{2,1,0:T(8,128)(2,1)S(1)} %get-tuple-element.132) | copy-start | bytes 4718596
  504.6 1.5 copy-start.13
  506.2 6.2 collective-permute-start
  527.3 162.0 %copy-start.18 = (bf16[2,192,2048]{2,1,0:T(8,128)(2,1)S(1)}, bf16[2,192,2048]{2,1,0:T(8,128)(2,1)}, u32[]{:S(2)}) copy-start(bf16[2,192,2048]{2,1,0:T(8,128)(2,1)} %copy-done.17) | copy-start | bytes 4718596
  689.3 1.9 copy-start.11
  691.2 1.3 copy-start.20
  692.5 1.1 copy-start.21
  700.1 6.4 copy-start.1
Sparse Core Ops, SparseCore 0:
  9.6 66.8 all-gather.3
  122.6 117.8 all-gather.5
  242.7 62.0 all-gather.7
  315.4 58.1 reduce-scatter.5
  375.8 114.5 reduce-scatter.7
  493.7 96.2 reduce-scatter.3
